TPU v7x, 512 devices: a whole 4x4x16 slice. The times are simulated.
512 devices in a mesh: dom: 128 (over z, y, core), src: 4 (over x).
Axes of the slice: x: 4, y: 4, z: 16, core: 2. Of those that a mesh axis runs over, the one named last changes fastest.
Arguments:
- features: bfloat16 [524288, 256], P(('dom', 'src')), may hold values from -6 to 6
- cotangent: bfloat16 [524288, 256], P(('dom', 'src')), may hold values from -6 to 6
- w_self: bfloat16 [256, 256], replicated, may hold values from -0.375 to 0.375
- w_neigh: bfloat16 [256, 256], replicated, may hold values from -0.375 to 0.375
- bias: bfloat16 [256], replicated, may hold values from -3 to 3
- send_rows: int32 [128, 4, 128, 8], P('dom', 'src'), may hold values from -1 to 1023, as said below
- edge_src: int32 [128, 4, 8192], P('dom', 'src'), may hold values from 0 to 2047, as said below
- edge_dst: int32 [128, 4, 8192], P('dom', 'src'), may hold values from 0 to 4095
- tile_count: int32 [128, 4], P('dom', 'src'), may hold values from 16 to 64, as said below
Outputs:
- activations: bfloat16 [524288, 256], P(('dom', 'src'))
- feature_grad: float32 [524288, 256], P(('dom', 'src'))
Inputs may be any that keep to these rules, and one draw needn't show every extreme that they name: `send_rows`: slots of a list are filled from the first one; some list of every owner is full; an account's own part sends it nothing. `edge_src`: every edge refers to a local row or to a filled slot. Edge slots after the first tile_count * 128 are ignored.
All inputs are finite; a program needn't handle non-finite values.
Results may differ from a plain program's by a relative error of at most 0.009.
Values may be sent and summed in bfloat16 or wider, within the bound.
No kernel may reach another device: no remote copies, remote signals or barrier semaphores. Data moves between devices by JAX's collectives and lax.ppermute only.
A program may use at most 64 MiB of HBM per device.

v0:
```python
import jax
import jax.numpy as jnp
from jax import lax
from jax.sharding import PartitionSpec as P


def local(features, cotangent, w_self, w_neigh, bias, send_rows, edge_src, edge_dst, tile_count):
    node_rows = features.shape[0]
    feature_width = features.shape[1]
    peer_total = lax.axis_size("dom")
    senders = send_rows[0, 0]
    capacity = senders.shape[1]
    halo_total = peer_total * capacity
    sources = edge_src[0, 0]
    targets = edge_dst[0, 0]
    edge_total = sources.shape[0]
    part_total = node_rows * lax.axis_size("src")
    active = jnp.arange(edge_total) // 128 < tile_count[0, 0]
    filled = senders >= 0
    zero_half = jnp.zeros((), jnp.bfloat16)
    picked = jnp.where(filled[:, :, None], features[jnp.maximum(senders, 0)], zero_half)
    counts = jnp.zeros((part_total,), jnp.float32).at[targets].add(active.astype(jnp.float32))
    degree_all = lax.psum(counts, "src")
    inverse_all = 1.0 / jnp.maximum(degree_all, 1.0)
    inverse = lax.dynamic_slice_in_dim(inverse_all, lax.axis_index("src") * node_rows, node_rows)
    remote = lax.all_to_all(picked, "dom", split_axis=0, concat_axis=0, tiled=True).reshape(
        halo_total, feature_width
    )
    table = jnp.concatenate([features, remote], axis=0)
    taken = jnp.where(active[:, None], table[sources], zero_half)
    partial_value = (
        jnp.zeros((part_total, feature_width), jnp.float32)
        .at[targets]
        .add(taken.astype(jnp.float32))
    )
    totals = lax.psum_scatter(
        partial_value.astype(jnp.bfloat16), "src", scatter_dimension=0, tiled=True
    ).astype(jnp.float32)
    neighbour_mean = (totals * inverse[:, None]).astype(jnp.bfloat16)
    preact = (
        jnp.dot(features, w_self, preferred_element_type=jnp.float32)
        + jnp.dot(neighbour_mean, w_neigh, preferred_element_type=jnp.float32)
        + bias.astype(jnp.float32)
    )
    sigma = jax.nn.sigmoid(preact)
    outputs = (preact * sigma).astype(jnp.bfloat16)
    slope = sigma * (1.0 + preact * (1.0 - sigma))
    upstream = (cotangent.astype(jnp.float32) * slope).astype(jnp.bfloat16)
    grad_own = jnp.dot(upstream, w_self.T, preferred_element_type=jnp.float32)
    scaled = (
        jnp.dot(upstream, w_neigh.T, preferred_element_type=jnp.float32) * inverse[:, None]
    ).astype(jnp.bfloat16)
    spread = lax.all_gather(scaled, "src", axis=0, tiled=True)
    contrib = jnp.where(active[:, None], spread[targets], zero_half).astype(jnp.float32)
    grad_table = (
        jnp.zeros((node_rows + halo_total, feature_width), jnp.float32).at[sources].add(contrib)
    )
    remote_grad = grad_table[node_rows:]
    local_grad = grad_table[:node_rows]
    returned = lax.all_to_all(
        remote_grad.reshape(peer_total, capacity, feature_width).astype(jnp.bfloat16),
        "dom",
        split_axis=0,
        concat_axis=0,
        tiled=True,
    ).astype(jnp.float32)
    back_rows = jnp.where(filled, senders, node_rows)
    incoming = (
        jnp.zeros((node_rows, feature_width), jnp.float32).at[back_rows].add(returned, mode="drop")
    )
    return (outputs, grad_own + local_grad + incoming)


def solution(mesh):
    placed = (
        P(("dom", "src"), None),
        P(("dom", "src"), None),
        P(),
        P(),
        P(),
        P("dom", "src", None, None),
        P("dom", "src", None),
        P("dom", "src", None),
        P("dom", "src"),
    )
    return jax.shard_map(
        local,
        mesh=mesh,
        in_specs=placed,
        out_specs=(P(("dom", "src"), None), P(("dom", "src"), None)),
        check_vma=False,
    )
```

profile of v0, /device:TPU:33, one launch (start us, length us, event | category | flops | bytes accessed | tf_op | source)
XLA Modules:
  0.0 406.8 jit_solution(14900899894254317384)
XLA Ops:
  7.2 0.0 copy-start
  7.2 0.0 copy-start.1
  7.2 0.0 copy-start.3
  7.2 0.0 copy-start.4
  7.2 0.8 compare_select_fusion.2
  8.0 0.7 compare_bitcast_fusion
  8.7 0.1 copy.13
  8.8 0.1 reshape.127
  8.9 0.1 copy.12
  9.0 4.6 %gather_fusion = bf16[1024,256]{1,0:T(8,128)(2,1)S(1)} fusion(bf16[1024,256]{1,0:T(8,128)(2,1)} %param.9, s32[1024]{0:T(1024)S(1)} %broadcast_clamp_fusion.2), kind=kCustom, calls=%fused_computation | custom fusion | bytes 1052672 | tf_op jit(solution)/shard_map/gather | solution.py:21
  13.6 1.0 bitcast_select_fusion
  14.6 19.5 %all-to-all-start = ((bf16[128,8,256]{2,1,0:T(8,128)(2,1)}), bf16[128,8,256]{2,1,0:T(8,128)(2,1)S(1)}, u32[]{:S(2)}, u32[]{:S(2)}) async-start(bf16[128,8,256]{2,1,0:T(8,128)(2,1)} %bitcast_select_fusion), calls=%async_computation | async-start | bytes 1048576 | tf_op jit(solution)/shard_map/all_to_all | solution.py:26
  34.1 0.0 reduce-scatter.2.cloned.1.call-start
  34.8 0.0 copy-done.3
  34.8 0.0 copy-done.4
  34.9 32.7 %all-to-all-done = bf16[128,8,256]{2,1,0:T(8,128)(2,1)S(1)} async-done(((bf16[128,8,256]{2,1,0:T(8,128)(2,1)}), bf16[128,8,256]{2,1,0:T(8,128)(2,1)S(1)}, u32[]{:S(2)}, u32[]{:S(2)}) %all-to-all-start) | async-done | bytes 524320 | tf_op jit(solution)/shard_map/all_to_all | solution.py:26
  67.6 0.0 copy-done.1
  67.6 0.1 pad_maximum_fusion
  67.7 76.8 %scatter_custom_fusion = f32[4096,256]{1,0:T(8,128)} fusion(s32[8192]{0:T(1024)S(1)} %bitcast.39, pred[8192]{0:T(1024)(128)(4,1)S(1)} %fusion.19, bf16[]{:T(256)} %constant.41.clone.1, f32[]{:T(128)} %constant.14.clone.1, bf16[2048,256]{1,0:T(8,128)(2,1)S(1)} %pad_maximum_fusion, s32[8192]{0:T(1024)S(1)} %broadcast_clamp_fusion.1), kind=kCustom, calls=%fused_computation.9 | custom fusion | flops 6291456 | bytes 5283846 | tf_op jit(solution)/shard_map/scatter-add | solution.py:34
  144.6 0.0 copy-start.6
  144.6 0.0 copy-start.2
  144.6 0.0 copy-start.5
  144.6 3.8 convert_element_type.41
  148.3 0.0 reduce-scatter.2.cloned.1.call-update
  148.4 0.0 all-gather.2.cloned.1.call-start
  148.4 43.2 %scatter_custom_fusion.1 = f32[4096]{0:T(1024)S(1)} fusion(s32[8192]{0:T(1024)S(1)} %bitcast.40, f32[8192]{0:T(1024)S(1)} %fusion.25, f32[]{:T(128)} %constant.14.clone.1), kind=kCustom, calls=%fused_computation.50 | custom fusion | flops 8192 | bytes 16388 | tf_op jit(solution)/shard_map/scatter-add | solution.py:22
  191.7 0.0 copy-done.6
  191.7 13.2 %psum.7 = f32[4096]{0:T(1024)S(1)} all-reduce(f32[4096]{0:T(1024)S(1)} %scatter_custom_fusion.1), channel_id=1, replica_groups=mesh['dom'=128,'src'=4] {'src'}, use_global_device_ids=true, to_apply=%region_3.4 | all-reduce | flops 4096 | bytes 32768 | tf_op jit(solution)/shard_map/psum | solution.py:23
  204.8 0.0 copy-done.2
  204.8 0.3 fusion.29
  205.1 0.0 reduce-scatter.2.cloned.1.call-done
  205.2 0.0 copy-done
  205.2 0.0 copy-done.5
  205.2 2.6 multiply_convert_fusion
  207.8 1.1 fusion.12
  208.9 0.0 all-gather.2.cloned.1.call-update
  208.9 31.2 %all-gather.2.cloned.1.call-done = bf16[4096,256]{1,0:T(8,128)(2,1)} async-done(((bf16[1024,256]{1,0:T(8,128)(2,1)}), bf16[4096,256]{1,0:T(8,128)(2,1)}) %all-gather.2.cloned.1.call-update) | async-done | bytes 2097168 | tf_op jit(solution)/shard_map/all_gather | solution.py:53
  240.1 100.4 %scatter_custom_fusion.2 = f32[2048,256]{1,0:T(8,128)S(1)} fusion(s32[8192]{0:T(1024)S(1)} %bitcast.38, pred[8192]{0:T(1024)(128)(4,1)S(1)} %fusion.19, bf16[]{:T(256)} %constant.41.clone.1, f32[]{:T(128)} %constant.14.clone.1, bf16[4096,256]{1,0:T(8,128)(2,1)} %all-gather.2.cloned.1.call-done, s32[8192]{0:T(1024)S(1)} %broadcast_clamp_fusion), kind=kCustom, calls=%fused_computation.7 | custom fusion | flops 6291456 | bytes 4235270 | tf_op jit(solution)/shard_map/scatter-add | solution.py:56
  340.5 0.8 fusion.16
  341.4 16.8 %all-to-all-start.1 = ((bf16[128,8,256]{2,1,0:T(8,128)(2,1)}), bf16[128,8,256]{2,1,0:T(8,128)(2,1)S(1)}, u32[]{:S(2)}, u32[]{:S(2)}) async-start(bf16[128,8,256]{2,1,0:T(8,128)(2,1)} %fusion.16), calls=%async_computation.2 | async-start | bytes 1048576 | tf_op jit(solution)/shard_map/all_to_all | solution.py:60
  358.1 0.1 copy.14
  358.2 0.1 reshape.175
  358.3 1.3 convolution_add_fusion
  359.6 32.1 %all-to-all-done.1 = bf16[128,8,256]{2,1,0:T(8,128)(2,1)S(1)} async-done(((bf16[128,8,256]{2,1,0:T(8,128)(2,1)}), bf16[128,8,256]{2,1,0:T(8,128)(2,1)S(1)}, u32[]{:S(2)}, u32[]{:S(2)}) %all-to-all-start.1) | async-done | bytes 524320 | tf_op jit(solution)/shard_map/all_to_all | solution.py:60
  391.7 8.3 %scatter_custom_fusion.3 = f32[1024,256]{1,0:T(8,128)} fusion(f32[1024,256]{1,0:T(8,128)} %convolution_add_fusion, s32[1024]{0:T(1024)S(1)} %reshape.175, bf16[128,8,256]{2,1,0:T(8,128)(2,1)S(1)} %all-to-all-done.1), kind=kCustom, calls=%fused_computation.25 | custom fusion | flops 524288 | bytes 1572864 | tf_op jit(solution)/shard_map/scatter-add | solution.py:69
  (9 shorter events, 0.1 us)
Async XLA Ops:
  7.2 198.0 %copy-start = (bf16[256,256]{1,0:T(8,128)(2,1)S(1)}, bf16[256,256]{1,0:T(8,128)(2,1)}, u32[]{:S(2)}) copy-start(bf16[256,256]{1,0:T(8,128)(2,1)} %param.12) | copy-start | bytes 393220
  7.2 60.5 %copy-start.1 = (bf16[1024,256]{1,0:T(8,128)(2,1)S(1)}, bf16[1024,256]{1,0:T(8,128)(2,1)}, u32[]{:S(2)}) copy-start(bf16[1024,256]{1,0:T(8,128)(2,1)} %param.9) | copy-start | bytes 1572868
  7.2 27.6 %copy-start.3 = (s32[1,1,8192]{2,1,0:T(1,128)S(1)}, s32[1,1,8192]{2,1,0:T(1,128)}, u32[]{:S(2)}) copy-start(s32[1,1,8192]{2,1,0:T(1,128)} %param.15) | copy-start | bytes 98308
  7.2 27.6 %copy-start.4 = (s32[1,1,8192]{2,1,0:T(1,128)S(1)}, s32[1,1,8192]{2,1,0:T(1,128)}, u32[]{:S(2)}) copy-start(s32[1,1,8192]{2,1,0:T(1,128)} %param.16) | copy-start | bytes 98308
  14.6 53.1 %all-to-all-start = ((bf16[128,8,256]{2,1,0:T(8,128)(2,1)}), bf16[128,8,256]{2,1,0:T(8,128)(2,1)S(1)}, u32[]{:S(2)}, u32[]{:S(2)}) async-start(bf16[128,8,256]{2,1,0:T(8,128)(2,1)} %bitcast_select_fusion), calls=%async_computation | async-start | bytes 1048576 | tf_op jit(solution)/shard_map/all_to_all | solution.py:26
  34.1 171.1 %reduce-scatter.2.cloned.1.call-start = ((), (), s32[]{:S(2)}) async-start(), calls=%async_computation.3 | async-start | bytes 2621440 | tf_op jit(solution)/shard_map/reduce_scatter | solution.py:36
  144.6 47.1 %copy-start.6 = (bf16[256]{0:T(256)(128)(2,1)S(1)}, bf16[256]{0:T(256)(128)(2,1)}, u32[]{:S(2)}) copy-start(bf16[256]{0:T(256)(128)(2,1)} %param.13) | copy-start | bytes 1540
  144.6 60.3 %copy-start.2 = (bf16[256,256]{1,0:T(8,128)(2,1)S(1)}, bf16[256,256]{1,0:T(8,128)(2,1)}, u32[]{:S(2)}) copy-start(bf16[256,256]{1,0:T(8,128)(2,1)} %param.11) | copy-start | bytes 393220
  144.6 60.6 %copy-start.5 = (bf16[1024,256]{1,0:T(8,128)(2,1)S(1)}, bf16[1024,256]{1,0:T(8,128)(2,1)}, u32[]{:S(2)}) copy-start(bf16[1024,256]{1,0:T(8,128)(2,1)} %param.10) | copy-start | bytes 1572868
  148.4 91.7 %all-gather.2.cloned.1.call-start = ((), (), s32[]{:S(2)}) async-start(), calls=%async_computation.4 | async-start | bytes 2621440 | tf_op jit(solution)/shard_map/all_gather | solution.py:53
  341.4 50.4 %all-to-all-start.1 = ((bf16[128,8,256]{2,1,0:T(8,128)(2,1)}), bf16[128,8,256]{2,1,0:T(8,128)(2,1)S(1)}, u32[]{:S(2)}, u32[]{:S(2)}) async-start(bf16[128,8,256]{2,1,0:T(8,128)(2,1)} %fusion.16), calls=%async_computation.2 | async-start | bytes 1048576 | tf_op jit(solution)/shard_map/all_to_all | solution.py:60
Sparse Core Ops, SparseCore 0:
  148.5 28.3 reduce-scatter.1
  209.0 31.0 all-gather.1
where the time goes:
time: 408 us; the launch traced here: 407 us
  other arithmetic  235 us (58%)
  waiting for transfers between devices  96.1 us (24%)
  starting transfers between devices  36.3 us (9%)
  between operations  14.9 us (4%)
  blocking collectives  13.2 us (3%)
  local copies, waits for them, and re-layouts  5.95 us (1%)
  matrix products  5.3 us (1%)
    scatter-add x1, other arithmetic, local(): jnp.zeros((node_rows + halo_total, feature_width), jnp.float32).at[sources]  100 us
    scatter-add x1, other arithmetic, local(): partial_value = jnp.zeros((part_total, feature_width), jnp.float32).at[ta...  76.8 us
    scatter-add x1, other arithmetic, local(): jnp.zeros((part_total,), jnp.float32).at[targets]  43.2 us
    all_to_all x1, waiting for transfers between devices, local(): lax.all_to_all(picked, 'dom', split_axis=0, concat_axis=0, tiled=True)  32.7 us
    all_to_all x1, waiting for transfers between devices, local(): lax.all_to_all(remote_grad.reshape(peer_total, capacity, feature_width).a...  32.1 us
    all_gather x1, waiting for transfers between devices, local(): spread = lax.all_gather(scaled, 'src', axis=0, tiled=True)  31.2 us
    all_to_all x1, starting transfers between devices, local(): lax.all_to_all(picked, 'dom', split_axis=0, concat_axis=0, tiled=True)  19.5 us
    all_to_all x1, starting transfers between devices, local(): lax.all_to_all(remote_grad.reshape(peer_total, capacity, feature_width).a...  16.8 us
  transfers between devices with their start and end apart: 4, of which 3 were waited for; matrix products, arithmetic and copies ran while one was open for 11% of the time, Pallas kernels for 0%

commit v1 on v0

v1 whole, which is shorter than its diff:
```python
import functools

import jax
import jax.numpy as jnp
from jax import lax
from jax.experimental import pallas as pl
from jax.experimental.pallas import tpu as pltpu
from jax.sharding import PartitionSpec as P

ROWS = 1024
WIDTH = 256
PART = 4096
EDGES = 8192
CHUNK = 512
SUB = 256
WIN = 384
PADDED = PART + WIN
CNT = 16
LOCAL_END = 1 << 22
ACTIVE_END = 1 << 23
F32 = jnp.float32
BF16 = jnp.bfloat16


def one_hot(mask):
    return jnp.where(mask, 1.0, 0.0).astype(BF16)


def iota(shape, dim):
    return lax.broadcasted_iota(jnp.int32, shape, dim)


def key_column(row):
    return jnp.transpose(jnp.broadcast_to(row, (128, 128)))


def source_of(keys, remote):
    return jnp.where((keys >> 22) == remote, keys & 1023, -1)


def target_of(keys):
    return (keys >> 10) & 4095


def local_edges(keys_s):
    def step(i, lo):
        probe = lo + (4096 >> i)
        return jnp.where(keys_s[probe - 1] < LOCAL_END, probe, lo)

    lo = lax.fori_loop(0, 13, step, 0)
    return jnp.where((lo == EDGES - 1) & (keys_s[EDGES - 1] < LOCAL_END), EDGES, lo)


def edge_range(keys_s, active_s, remote):
    boundary = local_edges(keys_s)
    if remote:
        return boundary, active_s[0] * 128
    return 0, boundary


def sub_range(keys_s, start, lo, hi):
    first = jnp.maximum(start, lo)
    last = jnp.minimum(start + SUB - 1, hi - 1)
    base = (target_of(keys_s[first]) // 16) * 16
    count = jnp.where(last >= first, (target_of(keys_s[last]) - base) // WIN + 1, 0)
    return base, count


def aggregate(keys_s, active_s, keys_v, table, acc, remote, ready):
    lo, hi = edge_range(keys_s, active_s, remote)
    ready()

    def tile(t, carry):
        rows = [keys_v[4 * t + j] for j in range(4)]
        parts = []
        for j in range(4):
            src = source_of(key_column(rows[j]), remote)
            parts.append(
                jnp.concatenate(
                    [one_hot(src == iota((128, 128), 1) + 128 * c) for c in range(ROWS // 128)], axis=1
                )
            )
        pick = jnp.concatenate(parts, axis=0)
        got = jnp.dot(pick, table[...], preferred_element_type=F32).astype(BF16)
        for sub in range(CHUNK // SUB):
            base, count = sub_range(keys_s, t * CHUNK + sub * SUB, lo, hi)
            piece = got[sub * SUB : (sub + 1) * SUB]
            targets = [target_of(rows[2 * sub + j]) for j in range(2)]

            def window(w, c):
                off = pl.multiple_of(base + w * WIN, 16)
                place = jnp.concatenate(
                    [one_hot(iota((WIN, 128), 0) + off == targets[j]) for j in range(2)], axis=1
                )
                acc[pl.ds(off, WIN), :] += jnp.dot(place, piece, preferred_element_type=F32)
                return c

            lax.fori_loop(0, count, window, 0)
        return carry

    lax.fori_loop(lo // CHUNK, (hi + CHUNK - 1) // CHUNK, tile, 0)


def forward_local_kernel(keys_s, active_s, keys_v, table, acc, counts):
    acc[...] = jnp.zeros_like(acc)
    aggregate(keys_s, active_s, keys_v, table, acc, 0, lambda: None)

    def tally(t, total):
        keys = [keys_v[4 * t + j] for j in range(4)]
        high = jnp.concatenate(
            [one_hot((iota((32, 128), 0) == (target_of(k) >> 7)) & (k < ACTIVE_END)) for k in keys], axis=1
        )
        low = jnp.concatenate([one_hot(iota((128, 128), 0) == (target_of(k) & 127)) for k in keys], axis=1)
        return total + lax.dot_general(high, low, (((1,), (1,)), ((), ())), preferred_element_type=F32)

    total = lax.fori_loop(0, EDGES // CHUNK, tally, jnp.zeros((32, 128), F32))
    upper = jnp.floor(total * (1.0 / 256.0))
    lower = total - upper * 256.0
    for s in range(4):
        both = jnp.concatenate([upper[8 * s : 8 * s + 8], lower[8 * s : 8 * s + 8]], axis=1)
        counts[s] = jnp.concatenate([both, jnp.zeros((8, WIDTH), F32)], axis=0).astype(BF16)


def forward_remote_kernel(keys_s, active_s, keys_v, table, counts, before, out, acc, sem):
    copy = pltpu.make_async_copy(before, acc, sem)
    copy.start()
    aggregate(keys_s, active_s, keys_v, table, acc, 1, copy.wait)
    for s in range(4):
        out[s, :ROWS, :] = acc[s * ROWS : (s + 1) * ROWS, :].astype(BF16)
        out[s, ROWS:, :] = counts[s]


def dense_kernel(feats, cots, w_self, w_neigh, bias, recv, counts, acts, scaled, own, inv_ref):
    i = pl.program_id(0)

    @pl.when(i == 0)
    def _():
        deg = jnp.zeros((8, 128), F32)
        for s in range(4):
            c = counts[s].astype(F32)
            deg = deg + c[:8, :128] * 256.0 + c[:8, 128:]
        inv = 1.0 / jnp.maximum(deg, 1.0)
        for r in range(8):
            inv_ref[r] = inv[r : r + 1]

    cols = [key_column(inv_ref[2 * i + r]) for r in range(2)]
    inverse = jnp.concatenate([jnp.concatenate([c, c], axis=1) for c in cols], axis=0)
    totals = recv[0].astype(F32)
    for s in range(1, 4):
        totals = totals + recv[s].astype(F32)
    mean = (totals * inverse).astype(BF16)
    pre = (
        jnp.dot(feats[...], w_self[...], preferred_element_type=F32)
        + jnp.dot(mean, w_neigh[...], preferred_element_type=F32)
        + bias[...].astype(F32)
    )
    sigma = jax.nn.sigmoid(pre)
    acts[...] = (pre * sigma).astype(BF16)
    slope = sigma * (1.0 + pre * (1.0 - sigma))
    up = (cots[...].astype(F32) * slope).astype(BF16)
    contract = (((1,), (1,)), ((), ()))
    back = lax.dot_general(up, w_neigh[...], contract, preferred_element_type=F32)
    value = (back * inverse).astype(BF16)
    for s in range(4):
        scaled[s] = value
    own[...] = lax.dot_general(up, w_self[...], contract, preferred_element_type=F32)


def scatter_back(keys_s, active_s, keys_v, spread, rows_ref, acc, remote):
    lo, hi = edge_range(keys_s, active_s, remote)

    def tile(t, carry):
        rows = [keys_v[4 * t + j] for j in range(4)]
        for sub in range(CHUNK // SUB):
            base, count = sub_range(keys_s, t * CHUNK + sub * SUB, lo, hi)
            cols = [target_of(key_column(rows[2 * sub + j])) for j in range(2)]

            def window(w):
                off = pl.multiple_of(base + w * WIN, 16)
                pick = jnp.concatenate(
                    [
                        jnp.concatenate(
                            [one_hot(c - off == iota((128, 128), 1) + 128 * k) for k in range(WIN // 128)], axis=1
                        )
                        for c in cols
                    ],
                    axis=0,
                )
                return jnp.dot(pick, spread[pl.ds(off, WIN), :], preferred_element_type=F32)

            rows_ref[sub * SUB : (sub + 1) * SUB, :] = window(0)

            def more(w, c):
                rows_ref[sub * SUB : (sub + 1) * SUB, :] += window(w)
                return c

            lax.fori_loop(1, count, more, 0)
        place = jnp.concatenate(
            [one_hot(iota((ROWS, 128), 0) == source_of(rows[j], remote)) for j in range(4)], axis=1
        )
        acc[...] += jnp.dot(place, rows_ref[...].astype(BF16), preferred_element_type=F32)
        return carry

    lax.fori_loop(lo // CHUNK, (hi + CHUNK - 1) // CHUNK, tile, 0)


def load_spread(spread_hbm, spread, sem):
    copy = pltpu.make_async_copy(spread_hbm, spread.at[pl.ds(0, PART), :], sem)
    copy.start()
    spread[PART:, :] = jnp.zeros((WIN, WIDTH), BF16)
    copy.wait()


def backward_remote_kernel(keys_s, active_s, keys_v, spread_hbm, out, spread, rows_ref, acc, sem):
    load_spread(spread_hbm, spread, sem)
    acc[...] = jnp.zeros_like(acc)
    scatter_back(keys_s, active_s, keys_v, spread, rows_ref, acc, 1)
    out[...] = acc[...].astype(BF16)


def backward_local_kernel(keys_s, active_s, keys_v, own, spread_hbm, out, spread, rows_ref, sem):
    load_spread(spread_hbm, spread, sem)
    out[...] = own[...]
    scatter_back(keys_s, active_s, keys_v, spread, rows_ref, out, 0)


VMEM = pl.BlockSpec(memory_space=pltpu.VMEM)
ANY = pl.BlockSpec(memory_space=pl.ANY)
PARAMS = pltpu.CompilerParams(vmem_limit_bytes=40 << 20)


def call(kernel, in_specs, out_shape, scratch, name):
    single = not isinstance(out_shape, tuple)
    return pl.pallas_call(
        kernel,
        grid_spec=pltpu.PrefetchScalarGridSpec(
            num_scalar_prefetch=2,
            grid=(),
            in_specs=in_specs,
            out_specs=VMEM if single else tuple(VMEM for _ in out_shape),
            scratch_shapes=scratch,
        ),
        out_shape=out_shape,
        compiler_params=PARAMS,
        name=name,
    )


def local(features, cotangent, w_self, w_neigh, bias, send_rows, edge_src, edge_dst, tile_count):
    peers, capacity = send_rows.shape[2], send_rows.shape[3]
    senders = send_rows.reshape(peers * capacity)
    nodes = jnp.arange(ROWS, dtype=jnp.int32)
    choose = (senders[:, None] == nodes[None, :]).astype(BF16)
    picked = jnp.dot(choose, features, preferred_element_type=F32).astype(BF16)
    remote = lax.all_to_all(
        picked.reshape(peers, capacity, WIDTH), "dom", split_axis=0, concat_axis=0, tiled=True
    ).reshape(peers * capacity, WIDTH)

    sources = edge_src.reshape(EDGES)
    targets = edge_dst.reshape(EDGES)
    active = tile_count.reshape(1)
    live = jnp.arange(EDGES, dtype=jnp.int32) < active[0] * 128
    keys = ((sources >> 10) << 22) + (targets << 10) + (sources & 1023)
    keys_s = lax.sort(jnp.where(live, keys, ACTIVE_END))
    keys_v = keys_s.reshape(EDGES // 128, 1, 128)

    shape = jax.ShapeDtypeStruct
    before, counts = call(
        forward_local_kernel,
        [VMEM, VMEM],
        (shape((PADDED, WIDTH), F32), shape((4, CNT, WIDTH), BF16)),
        [],
        "aggregate_local",
    )(keys_s, active, keys_v, features)
    partial = call(
        forward_remote_kernel,
        [VMEM, VMEM, VMEM, ANY],
        shape((4, ROWS + CNT, WIDTH), BF16),
        [pltpu.VMEM((PADDED, WIDTH), F32), pltpu.SemaphoreType.DMA],
        "aggregate_remote",
    )(keys_s, active, keys_v, remote, counts, before)
    recv = lax.all_to_all(partial, "src", split_axis=0, concat_axis=0, tiled=True)

    block = ROWS // 4
    tile = pl.BlockSpec((block, WIDTH), lambda i: (i, 0))
    whole = pl.BlockSpec((WIDTH, WIDTH), lambda i: (0, 0))
    four = pl.BlockSpec((4, block, WIDTH), lambda i: (0, i, 0))
    acts, scaled, own = pl.pallas_call(
        dense_kernel,
        grid=(4,),
        in_specs=[
            tile,
            tile,
            whole,
            whole,
            pl.BlockSpec((1, WIDTH), lambda i: (0, 0)),
            four,
            pl.BlockSpec((4, CNT, WIDTH), lambda i: (0, ROWS // CNT, 0)),
        ],
        out_specs=(tile, four, tile),
        out_shape=(shape((ROWS, WIDTH), BF16), shape((4, ROWS, WIDTH), BF16), shape((ROWS, WIDTH), F32)),
        scratch_shapes=[pltpu.VMEM((8, 1, 128), F32)],
        compiler_params=PARAMS,
        name="dense_layer",
    )(features, cotangent, w_self, w_neigh, bias.reshape(1, WIDTH), recv, recv)
    spread = lax.all_to_all(scaled, "src", split_axis=0, concat_axis=0, tiled=True).reshape(PART, WIDTH)

    held = [
        pltpu.VMEM((PADDED, WIDTH), BF16),
        pltpu.VMEM((CHUNK, WIDTH), F32),
    ]
    outgoing = call(
        backward_remote_kernel,
        [VMEM, ANY],
        shape((ROWS, WIDTH), BF16),
        held + [pltpu.VMEM((ROWS, WIDTH), F32), pltpu.SemaphoreType.DMA],
        "scatter_remote",
    )(keys_s, active, keys_v, spread)
    returned = lax.all_to_all(
        outgoing.reshape(peers, capacity, WIDTH), "dom", split_axis=0, concat_axis=0, tiled=True
    ).reshape(peers * capacity, WIDTH)
    kept = call(
        backward_local_kernel,
        [VMEM, VMEM, ANY],
        shape((ROWS, WIDTH), F32),
        held + [pltpu.SemaphoreType.DMA],
        "scatter_local",
    )(keys_s, active, keys_v, own, spread)
    place = (nodes[:, None] == senders[None, :]).astype(BF16)
    incoming = jnp.dot(place, returned, preferred_element_type=F32)
    return acts, kept + incoming


def solution(mesh):
    placed = (
        P(("dom", "src"), None),
        P(("dom", "src"), None),
        P(),
        P(),
        P(),
        P("dom", "src", None, None),
        P("dom", "src", None),
        P("dom", "src", None),
        P("dom", "src"),
    )
    return jax.shard_map(
        local,
        mesh=mesh,
        in_specs=placed,
        out_specs=(P(("dom", "src"), None), P(("dom", "src"), None)),
        check_vma=False,
    )
```

time: 408 us -> 187 us (0.46)
  other arithmetic: 235 us -> 6.85 us
  Pallas kernels: 0 us -> 40.5 us
  waiting for transfers between devices: 96.1 us -> 62.6 us
  blocking collectives: 13.2 us -> 26.9 us
  between operations: 14.9 us -> 1.46 us
    scatter-add x4 -> x0, other arithmetic: 229 us -> none  [the longest x1 100 us: local(): jnp.zeros((node_rows + halo_total, feature_width), jnp.float32).at[sources]]
    pallas_call x0 -> x5, Pallas kernels: none -> 40.5 us  [the longest x1 10.8 us: local(): call(forward_local_kernel, [VMEM, VMEM], (shape((PADDED, WIDTH), F32), sh...]
    all_gather x1 -> x0, waiting for transfers between devices: 31.2 us -> none  [local(): spread = lax.all_gather(scaled, 'src', axis=0, tiled=True)]
    all_to_all x0 -> x1, blocking collectives: none -> 26.9 us  [local(): lax.all_to_all(scaled, 'src', split_axis=0, concat_axis=0, tiled=True)]
    psum x1 -> x0, blocking collectives: 13.2 us -> none  [local(): degree_all = lax.psum(counts, 'src')]
    unnamed x14 -> x27, local copies, waits for them, and re-layouts: 0.04 us -> 7.56 us
    sort x0 -> x1, other arithmetic: none -> 6.77 us  [local(): keys_s = lax.sort(jnp.where(live, keys, ACTIVE_END))]
    gather x1 -> x0, local copies, waits for them, and re-layouts: 4.57 us -> none  [local(): features[jnp.maximum(senders, 0)]]
  transfers between devices with their start and end apart: 4 -> 3, of which waited for: 3 -> 3; matrix products, arithmetic and copies ran while one was open for 11% -> 4% of each run, Pallas kernels for 0% -> 10%
where the time goes in v1:
time: 187 us
  waiting for transfers between devices  62.6 us (33%)
  Pallas kernels  40.5 us (22%)
  starting transfers between devices  35 us (19%)
  blocking collectives  26.9 us (14%)
  local copies, waits for them, and re-layouts  7.67 us (4%)
  other arithmetic  6.85 us (4%)
  matrix products  5.84 us (3%)
    all_to_all x1, blocking collectives, local(): lax.all_to_all(scaled, 'src', split_axis=0, concat_axis=0, tiled=True)  26.9 us
    all_to_all x1, waiting for transfers between devices, local(): lax.all_to_all(partial, 'src', split_axis=0, concat_axis=0, tiled=True)  25.7 us
    all_to_all x1, waiting for transfers between devices, local(): lax.all_to_all(outgoing.reshape(peers, capacity, WIDTH), 'dom', split_axi...  23.7 us
    all_to_all x1, starting transfers between devices, local(): lax.all_to_all(picked.reshape(peers, capacity, WIDTH), 'dom', split_axis=...  19.5 us
    all_to_all x1, waiting for transfers between devices, local(): lax.all_to_all(picked.reshape(peers, capacity, WIDTH), 'dom', split_axis=...  13.2 us
    all_to_all x1, starting transfers between devices, local(): lax.all_to_all(outgoing.reshape(peers, capacity, WIDTH), 'dom', split_axi...  11.9 us
    pallas_call x1, Pallas kernels, local(): call(forward_local_kernel, [VMEM, VMEM], (shape((PADDED, WIDTH), F32), sh...  10.8 us
    pallas_call x1, Pallas kernels, local(): call(backward_remote_kernel, [VMEM, ANY], shape((ROWS, WIDTH), BF16), hel...  9.67 us
  transfers between devices with their start and end apart: 3, of which 3 were waited for; matrix products, arithmetic and copies ran while one was open for 4% of the time, Pallas kernels for 10%

profile of v1, /device:TPU:33, one launch (start us, length us, event | category | flops | bytes accessed | tf_op | source)
XLA Modules:
  0.0 186.7 jit_solution(10048657503353574629)
XLA Ops:
  0.6 0.0 copy-start.3
  0.6 0.0 copy-start.10
  0.7 0.0 copy-start.11
  0.7 0.8 copy.11
  1.5 0.1 eq.28
  1.6 2.7 %fusion.6 = bf16[128,8,256]{2,1,0:T(8,128)(2,1)} fusion(bf16[1024,256]{1,0:T(8,128)(2,1)} %feats.1, s32[1024]{0:T(1024)S(1)} %eq.28), kind=kOutput, calls=%fused_computation.8 | convolution fusion | flops 538181632 | bytes 1052672 | tf_op jit(solution)/shard_map/dot_general | solution.py:254
  4.3 19.5 %all-to-all-start = ((bf16[128,8,256]{2,1,0:T(8,128)(2,1)}), bf16[128,8,256]{2,1,0:T(8,128)(2,1)S(1)}, u32[]{:S(2)}, u32[]{:S(2)}) async-start(bf16[128,8,256]{2,1,0:T(8,128)(2,1)} %fusion.6), calls=%async_computation | async-start | bytes 1048576 | tf_op jit(solution)/shard_map/all_to_all | solution.py:255
  24.4 0.0 copy-done.10
  24.4 0.0 copy-done.11
  24.4 0.1 and_add_fusion
  24.5 6.8 %sort.10 = (s32[8192]{0:T(1024)S(1)}, s32[8192]{0:T(1024)}) sort(s32[8192]{0:T(1024)S(1)} %fusion.8, s32[8192]{0:T(1024)S(1)} %iota.14), dimensions={0}, to_apply=%region_0.1 | sort | flops 106496 | bytes 131072 | tf_op jit(solution)/shard_map/sort | solution.py:264
  31.3 0.0 copy-done.3
  31.3 10.8 %aggregate_local.1 = (f32[4480,256]{1,0:T(8,128)S(1)}, bf16[4,16,256]{2,1,0:T(8,128)(2,1)S(1)}) custom-call(s32[8192]{0:T(1024)S(1)} %get-tuple-element.9.keys_s, s32[1]{0:T(128)} %bitcast.15.active_s, s32[64,1,128]{2,1,0:T(1,128)S(1)} %bitcast.21, bf16[1024,256]{1,0:T(8,128)(2,1)S(1)} %copy-done.3), custom_call_target="tpu_custom_call" | custom-call | tf_op jit(solution)/shard_map/aggregate_local/pallas_call | solution.py:268
  42.1 0.0 copy-start.1
  42.1 2.1 %copy-done.1 = f32[4480,256]{1,0:T(8,128)} copy-done((f32[4480,256]{1,0:T(8,128)}, f32[4480,256]{1,0:T(8,128)S(1)}, u32[]{:S(2)}) %copy-start.1) | copy-done | bytes 4587544
  44.2 13.2 %all-to-all-done = bf16[128,8,256]{2,1,0:T(8,128)(2,1)S(1)} async-done(((bf16[128,8,256]{2,1,0:T(8,128)(2,1)}), bf16[128,8,256]{2,1,0:T(8,128)(2,1)S(1)}, u32[]{:S(2)}, u32[]{:S(2)}) %all-to-all-start) | async-done | bytes 524320 | tf_op jit(solution)/shard_map/all_to_all | solution.py:255
  57.3 0.0 copy-start.2
  57.3 2.3 %copy-done.2 = f32[4480,256]{1,0:T(8,128)S(1)} copy-done((f32[4480,256]{1,0:T(8,128)S(1)}, f32[4480,256]{1,0:T(8,128)}, u32[]{:S(2)}) %copy-start.2) | copy-done | bytes 4587544
  59.6 0.0 copy-start.12
  59.6 0.0 copy-start.7
  59.7 0.0 copy-start.8
  59.7 0.0 copy-start.9
  59.7 8.4 %aggregate_remote.1 = bf16[4,1040,256]{2,1,0:T(8,128)(2,1)S(1)} custom-call(s32[8192]{0:T(1024)S(1)} %get-tuple-element.9.keys_s, s32[1]{0:T(128)} %bitcast.16.active_s, s32[64,1,128]{2,1,0:T(1,128)S(1)} %bitcast.22, bf16[1024,256]{1,0:T(8,128)(2,1)S(1)} %bitcast.25, bf16[4,16,256]{2,1,0:T(8,128)(2,1)S(1)} %get-tuple-element.10.counts, f32[4480,256]{1,0:T(8,128)S(1)} %copy-done.2), custom_call_target="tpu_custom_call" | custom-call | tf_op jit(solution)/shard_map/aggregate_remote/pallas_call | solution.py:275
  68.1 0.0 copy-start
  68.1 1.3 copy-done
  69.4 3.6 %all-to-all-start.1 = ((bf16[4,1040,256]{2,1,0:T(8,128)(2,1)}), bf16[4,1040,256]{2,1,0:T(8,128)(2,1)S(1)}, u32[]{:S(2)}, u32[]{:S(2)}) async-start(bf16[4,1040,256]{2,1,0:T(8,128)(2,1)} %copy-done), calls=%async_computation.1 | async-start | bytes 4259840 | tf_op jit(solution)/shard_map/all_to_all | solution.py:282
  73.1 0.0 copy-done.12
  73.1 25.7 %all-to-all-done.1.recv.counts = bf16[4,1040,256]{2,1,0:T(8,128)(2,1)S(1)} async-done(((bf16[4,1040,256]{2,1,0:T(8,128)(2,1)}), bf16[4,1040,256]{2,1,0:T(8,128)(2,1)S(1)}, u32[]{:S(2)}, u32[]{:S(2)}) %all-to-all-start.1) | async-done | bytes 2129952 | tf_op jit(solution)/shard_map/all_to_all | solution.py:282
  98.7 0.0 copy-done.7
  98.7 0.0 copy-done.8
  98.7 0.0 copy-done.9
  98.8 3.1 %dense_layer.1 = (bf16[1024,256]{1,0:T(8,128)(2,1)}, bf16[4,1024,256]{2,1,0:T(8,128)(2,1)S(1)}, f32[1024,256]{1,0:T(8,128)S(1)}) custom-call(bf16[1024,256]{1,0:T(8,128)(2,1)S(1)} %copy-done.3, bf16[1024,256]{1,0:T(8,128)(2,1)S(1)} %copy-done.7, bf16[256,256]{1,0:T(8,128)(2,1)S(1)} %copy-done.8, bf16[256,256]{1,0:T(8,128)(2,1)S(1)} %copy-done.9, ...), custom_call_target="tpu_custom_call" | custom-call | tf_op jit(solution)/shard_map/dense_layer/pallas_call | solution.py:288
  101.9 0.0 copy-start.4
  101.9 26.9 %all_to_all.20 = bf16[4,1024,256]{2,1,0:T(8,128)(2,1)S(1)} all-to-all(bf16[4,1024,256]{2,1,0:T(8,128)(2,1)S(1)} %get-tuple-element.14), channel_id=1, replica_groups=mesh['dom'=128,'src'=4] {'src'}, dimensions={0} | all-to-all | bytes 4194304 | tf_op jit(solution)/shard_map/all_to_all | solution.py:306
  128.8 0.0 copy-done.4
  128.8 0.0 copy-start.5
  128.8 9.7 %scatter_remote.1 = bf16[1024,256]{1,0:T(8,128)(2,1)} custom-call(s32[8192]{0:T(1024)S(1)} %get-tuple-element.9.keys_s, s32[1]{0:T(128)} %bitcast.18.active_s, s32[64,1,128]{2,1,0:T(1,128)S(1)} %bitcast.23, bf16[4096,256]{1,0:T(8,128)(2,1)S(1)} %bitcast.19), custom_call_target="tpu_custom_call" | custom-call | tf_op jit(solution)/shard_map/scatter_remote/pallas_call | solution.py:312
  138.4 11.9 %all-to-all-start.3 = ((bf16[128,8,256]{2,1,0:T(8,128)(2,1)}), bf16[128,8,256]{2,1,0:T(8,128)(2,1)}, u32[]{:S(2)}, u32[]{:S(2)}) async-start(bf16[128,8,256]{2,1,0:T(8,128)(2,1)} %bitcast.7), calls=%async_computation.3 | async-start | bytes 1048576 | tf_op jit(solution)/shard_map/all_to_all | solution.py:319
  150.3 0.0 copy-done.5
  150.3 8.5 %scatter_local.1 = f32[1024,256]{1,0:T(8,128)S(1)} custom-call(s32[8192]{0:T(1024)S(1)} %get-tuple-element.9.keys_s, s32[1]{0:T(128)} %bitcast.17.active_s, s32[64,1,128]{2,1,0:T(1,128)S(1)} %bitcast.24, f32[1024,256]{1,0:T(8,128)S(1)} %copy-done.5, bf16[4096,256]{1,0:T(8,128)(2,1)S(1)} %bitcast.20), custom_call_target="tpu_custom_call" | custom-call | tf_op jit(solution)/shard_map/scatter_local/pallas_call | solution.py:322
  158.9 0.0 copy-start.6
  158.9 1.0 copy-done.6
  159.8 23.7 %all-to-all-done.3 = bf16[128,8,256]{2,1,0:T(8,128)(2,1)} async-done(((bf16[128,8,256]{2,1,0:T(8,128)(2,1)}), bf16[128,8,256]{2,1,0:T(8,128)(2,1)}, u32[]{:S(2)}, u32[]{:S(2)}) %all-to-all-start.3) | async-done | bytes 524320 | tf_op jit(solution)/shard_map/all_to_all | solution.py:319
  183.6 3.2 %fusion.4 = f32[1024,256]{1,0:T(8,128)} fusion(f32[1024,256]{1,0:T(8,128)} %copy-done.6, s32[1024]{0:T(1024)S(1)} %eq.28, bf16[128,8,256]{2,1,0:T(8,128)(2,1)} %all-to-all-done.3), kind=kOutput, calls=%fused_computation.6 | convolution fusion | flops 538181632 | bytes 2625536 | tf_op jit(solution)/shard_map/dot_general | solution.py:330
  (3 shorter events, 0.0 us)
Async XLA Ops:
  0.6 30.7 %copy-start.3 = (bf16[1024,256]{1,0:T(8,128)(2,1)S(1)}, bf16[1024,256]{1,0:T(8,128)(2,1)}, u32[]{:S(2)}) copy-start(bf16[1024,256]{1,0:T(8,128)(2,1)} %feats.1) | copy-start | bytes 1572868
  0.6 23.8 %copy-start.10 = (s32[1,1,8192]{2,1,0:T(1,128)S(1)}, s32[1,1,8192]{2,1,0:T(1,128)}, u32[]{:S(2)}) copy-start(s32[1,1,8192]{2,1,0:T(1,128)} %param.15) | copy-start | bytes 98308
  0.7 23.8 %copy-start.11 = (s32[1,1,8192]{2,1,0:T(1,128)S(1)}, s32[1,1,8192]{2,1,0:T(1,128)}, u32[]{:S(2)}) copy-start(s32[1,1,8192]{2,1,0:T(1,128)} %param.16) | copy-start | bytes 98308
  4.3 53.1 %all-to-all-start = ((bf16[128,8,256]{2,1,0:T(8,128)(2,1)}), bf16[128,8,256]{2,1,0:T(8,128)(2,1)S(1)}, u32[]{:S(2)}, u32[]{:S(2)}) async-start(bf16[128,8,256]{2,1,0:T(8,128)(2,1)} %fusion.6), calls=%async_computation | async-start | bytes 1048576 | tf_op jit(solution)/shard_map/all_to_all | solution.py:255
  42.1 2.1 %copy-start.1 = (f32[4480,256]{1,0:T(8,128)}, f32[4480,256]{1,0:T(8,128)S(1)}, u32[]{:S(2)}) copy-start(f32[4480,256]{1,0:T(8,128)S(1)} %get-tuple-element.11.before) | copy-start | bytes 13762564
  57.3 2.3 %copy-start.2 = (f32[4480,256]{1,0:T(8,128)S(1)}, f32[4480,256]{1,0:T(8,128)}, u32[]{:S(2)}) copy-start(f32[4480,256]{1,0:T(8,128)} %copy-done.1) | copy-start | bytes 13762564
  59.6 13.4 %copy-start.12 = (bf16[256]{0:T(256)(128)(2,1)S(1)}, bf16[256]{0:T(256)(128)(2,1)}, u32[]{:S(2)}) copy-start(bf16[256]{0:T(256)(128)(2,1)} %param.13) | copy-start | bytes 1540
  59.6 39.1 %copy-start.7 = (bf16[1024,256]{1,0:T(8,128)(2,1)S(1)}, bf16[1024,256]{1,0:T(8,128)(2,1)}, u32[]{:S(2)}) copy-start(bf16[1024,256]{1,0:T(8,128)(2,1)} %cots.1) | copy-start | bytes 1572868
  59.7 39.1 %copy-start.8 = (bf16[256,256]{1,0:T(8,128)(2,1)S(1)}, bf16[256,256]{1,0:T(8,128)(2,1)}, u32[]{:S(2)}) copy-start(bf16[256,256]{1,0:T(8,128)(2,1)} %w_self.1) | copy-start | bytes 393220
  59.7 39.1 %copy-start.9 = (bf16[256,256]{1,0:T(8,128)(2,1)S(1)}, bf16[256,256]{1,0:T(8,128)(2,1)}, u32[]{:S(2)}) copy-start(bf16[256,256]{1,0:T(8,128)(2,1)} %w_neigh.1) | copy-start | bytes 393220
  68.1 1.3 copy-start
  69.4 29.3 %all-to-all-start.1 = ((bf16[4,1040,256]{2,1,0:T(8,128)(2,1)}), bf16[4,1040,256]{2,1,0:T(8,128)(2,1)S(1)}, u32[]{:S(2)}, u32[]{:S(2)}) async-start(bf16[4,1040,256]{2,1,0:T(8,128)(2,1)} %copy-done), calls=%async_computation.1 | async-start | bytes 4259840 | tf_op jit(solution)/shard_map/all_to_all | solution.py:282
  101.9 26.9 %copy-start.4 = (f32[1024,256]{1,0:T(8,128)}, f32[1024,256]{1,0:T(8,128)S(1)}, u32[]{:S(2)}) copy-start(f32[1024,256]{1,0:T(8,128)S(1)} %get-tuple-element.13.own) | copy-start | bytes 3145732
  128.8 21.6 %copy-start.5 = (f32[1024,256]{1,0:T(8,128)S(1)}, f32[1024,256]{1,0:T(8,128)}, u32[]{:S(2)}) copy-start(f32[1024,256]{1,0:T(8,128)} %copy-done.4) | copy-start | bytes 3145732
  138.4 45.1 %all-to-all-start.3 = ((bf16[128,8,256]{2,1,0:T(8,128)(2,1)}), bf16[128,8,256]{2,1,0:T(8,128)(2,1)}, u32[]{:S(2)}, u32[]{:S(2)}) async-start(bf16[128,8,256]{2,1,0:T(8,128)(2,1)} %bitcast.7), calls=%async_computation.3 | async-start | bytes 1048576 | tf_op jit(solution)/shard_map/all_to_all | solution.py:319
  158.9 1.0 copy-start.6

commit v2 on v1

--- a/solution.py
+++ b/solution.py
@@ -1,5 +1,3 @@
-import functools
-
 import jax
 import jax.numpy as jnp
 from jax import lax
@@ -12,6 +10,7 @@
 PART = 4096
 EDGES = 8192
 CHUNK = 512
+UNROLL = 4
 SUB = 256
 WIN = 384
 PADDED = PART + WIN
@@ -22,6 +21,10 @@
 BF16 = jnp.bfloat16
 
 
+def in_hbm(x):
+    return pltpu.with_memory_space_constraint(x, pltpu.HBM)
+
+
 def one_hot(mask):
     return jnp.where(mask, 1.0, 0.0).astype(BF16)
 
@@ -66,68 +69,165 @@
     return base, count
 
 
-def aggregate(keys_s, active_s, keys_v, table, acc, remote, ready):
-    lo, hi = edge_range(keys_s, active_s, remote)
-    ready()
-
+def place_of(targets, off):
+    return jnp.concatenate([one_hot(iota((WIN, 128), 0) + off == x) for x in targets], axis=1)
+
+
+def pick_of(rows, remote):
+    parts = []
+    for row in rows:
+        src = source_of(key_column(row), remote)
+        parts.append(
+            jnp.concatenate([one_hot(src == iota((128, 128), 1) + 128 * c) for c in range(ROWS // 128)], axis=1)
+        )
+    return jnp.concatenate(parts, axis=0)
+
+
+def further_windows(todo, run):
+    most = todo[0][1]
+    for item in todo[1:]:
+        most = jnp.maximum(most, item[1])
+
+    @pl.when(most > 1)
+    def _():
+        for item in todo:
+
+            def window(w, c):
+                run(item, pl.multiple_of(item[0] + w * WIN, 16))
+                return c
+
+            lax.fori_loop(1, item[1], window, 0)
+
+
+def build_adjacency(keys_s, keys_v, adj, lo, hi):
     def tile(t, carry):
-        rows = [keys_v[4 * t + j] for j in range(4)]
-        parts = []
-        for j in range(4):
-            src = source_of(key_column(rows[j]), remote)
-            parts.append(
-                jnp.concatenate(
-                    [one_hot(src == iota((128, 128), 1) + 128 * c) for c in range(ROWS // 128)], axis=1
-                )
-            )
-        pick = jnp.concatenate(parts, axis=0)
-        got = jnp.dot(pick, table[...], preferred_element_type=F32).astype(BF16)
-        for sub in range(CHUNK // SUB):
-            base, count = sub_range(keys_s, t * CHUNK + sub * SUB, lo, hi)
-            piece = got[sub * SUB : (sub + 1) * SUB]
-            targets = [target_of(rows[2 * sub + j]) for j in range(2)]
-
-            def window(w, c):
-                off = pl.multiple_of(base + w * WIN, 16)
-                place = jnp.concatenate(
-                    [one_hot(iota((WIN, 128), 0) + off == targets[j]) for j in range(2)], axis=1
-                )
-                acc[pl.ds(off, WIN), :] += jnp.dot(place, piece, preferred_element_type=F32)
-                return c
-
-            lax.fori_loop(0, count, window, 0)
+        todo = []
+        for u in range(UNROLL):
+            rows = [keys_v[2 * UNROLL * t + 2 * u + j] for j in range(2)]
+            base, count = sub_range(keys_s, (t * UNROLL + u) * SUB, lo, hi)
+            base = pl.multiple_of(base, 16)
+            targets = [target_of(r) for r in rows]
+            first = jnp.dot(place_of(targets, base), pick_of(rows, 1), preferred_element_type=F32).astype(BF16)
+            todo.append((base, count, targets, rows, first))
+        for base, count, targets, rows, first in todo:
+            adj[pl.ds(base, WIN), :] += first
+
+        def run(item, off):
+            more = jnp.dot(place_of(item[2], off), pick_of(item[3], 1), preferred_element_type=F32)
+            adj[pl.ds(off, WIN), :] += more.astype(BF16)
+
+        further_windows(todo, run)
         return carry
 
-    lax.fori_loop(lo // CHUNK, (hi + CHUNK - 1) // CHUNK, tile, 0)
-
-
-def forward_local_kernel(keys_s, active_s, keys_v, table, acc, counts):
+    size = SUB * UNROLL
+    lax.fori_loop(lo // size, (hi + size - 1) // size, tile, 0)
+
+
+def aggregate_local(keys_s, keys_v, table, acc, lo, hi):
+    def tile(t, carry):
+        rows = [keys_v[2 * UNROLL * t + j] for j in range(2 * UNROLL)]
+        got = jnp.dot(pick_of(rows, 0), table[...], preferred_element_type=F32).astype(BF16)
+        todo = []
+        for u in range(UNROLL):
+            base, count = sub_range(keys_s, (t * UNROLL + u) * SUB, lo, hi)
+            base = pl.multiple_of(base, 16)
+            targets = [target_of(r) for r in rows[2 * u : 2 * u + 2]]
+            piece = got[SUB * u : SUB * u + SUB]
+            first = jnp.dot(place_of(targets, base), piece, preferred_element_type=F32)
+            todo.append((base, count, targets, piece, first))
+        for base, count, targets, piece, first in todo:
+            acc[pl.ds(base, WIN), :] += first
+
+        def run(item, off):
+            acc[pl.ds(off, WIN), :] += jnp.dot(place_of(item[2], off), item[3], preferred_element_type=F32)
+
+        further_windows(todo, run)
+        return carry
+
+    size = SUB * UNROLL
+    lax.fori_loop(lo // size, (hi + size - 1) // size, tile, 0)
+
+
+def prepare_kernel(keys_s, active_s, keys_v, table, adj_out, local_out, counts, adj, acc, sems):
+    boundary = local_edges(keys_s)
+    adj[...] = jnp.zeros_like(adj)
+    build_adjacency(keys_s, keys_v, adj, boundary, active_s[0] * 128)
+    save_adj = pltpu.make_async_copy(adj.at[pl.ds(0, PART), :], adj_out, sems.at[0])
+    save_adj.start()
     acc[...] = jnp.zeros_like(acc)
-    aggregate(keys_s, active_s, keys_v, table, acc, 0, lambda: None)
+    aggregate_local(keys_s, keys_v, table, acc, 0, boundary)
+    save_acc = pltpu.make_async_copy(acc.at[pl.ds(0, PART), :], local_out, sems.at[1])
+    save_acc.start()
 
     def tally(t, total):
-        keys = [keys_v[4 * t + j] for j in range(4)]
+        keys = [keys_v[8 * t + j] for j in range(8)]
         high = jnp.concatenate(
             [one_hot((iota((32, 128), 0) == (target_of(k) >> 7)) & (k < ACTIVE_END)) for k in keys], axis=1
         )
         low = jnp.concatenate([one_hot(iota((128, 128), 0) == (target_of(k) & 127)) for k in keys], axis=1)
         return total + lax.dot_general(high, low, (((1,), (1,)), ((), ())), preferred_element_type=F32)
 
-    total = lax.fori_loop(0, EDGES // CHUNK, tally, jnp.zeros((32, 128), F32))
+    total = lax.fori_loop(0, EDGES // 1024, tally, jnp.zeros((32, 128), F32))
     upper = jnp.floor(total * (1.0 / 256.0))
     lower = total - upper * 256.0
     for s in range(4):
         both = jnp.concatenate([upper[8 * s : 8 * s + 8], lower[8 * s : 8 * s + 8]], axis=1)
         counts[s] = jnp.concatenate([both, jnp.zeros((8, WIDTH), F32)], axis=0).astype(BF16)
-
-
-def forward_remote_kernel(keys_s, active_s, keys_v, table, counts, before, out, acc, sem):
-    copy = pltpu.make_async_copy(before, acc, sem)
-    copy.start()
-    aggregate(keys_s, active_s, keys_v, table, acc, 1, copy.wait)
+    save_adj.wait()
+    save_acc.wait()
+
+
+def transpose_kernel(adj, out):
+    out[0] = jnp.transpose(adj[...])
+
+
+def forward_remote_kernel(table, counts, adj_hbm, local_hbm, out_hbm, adj, local_part, out, sems):
+    loads = []
+    for i in range(PART // CHUNK):
+        rows = pl.ds(i * CHUNK, CHUNK)
+        loads.append(
+            (
+                pltpu.make_async_copy(adj_hbm.at[rows, :], adj.at[i], sems.at[0, i]),
+                pltpu.make_async_copy(local_hbm.at[rows, :], local_part.at[i], sems.at[1, i]),
+            )
+        )
+        for copy in loads[i]:
+            copy.start()
     for s in range(4):
-        out[s, :ROWS, :] = acc[s * ROWS : (s + 1) * ROWS, :].astype(BF16)
         out[s, ROWS:, :] = counts[s]
+    saves = []
+    for i in range(PART // CHUNK):
+        for copy in loads[i]:
+            copy.wait()
+        total = local_part[i] + jnp.dot(adj[i], table[...], preferred_element_type=F32)
+        s, h = i // 2, i % 2
+        out[s, h * CHUNK : h * CHUNK + CHUNK, :] = total.astype(BF16)
+        if h == 1:
+            saves.append(pltpu.make_async_copy(out.at[s], out_hbm.at[s], sems.at[2, s]))
+            saves[s].start()
+    for copy in saves:
+        copy.wait()
+
+
+def pick_kernel(senders, table, out, acc):
+    for c in range(8):
+        col = key_column(senders[c : c + 1, :])
+        pick = jnp.concatenate([one_hot(col == iota((128, 128), 1) + 128 * k) for k in range(ROWS // 128)], axis=1)
+        acc[:, c, :] = jnp.dot(pick, table[...], preferred_element_type=F32)
+    out[...] = acc[...].astype(BF16)
+
+
+def combine_kernel(senders, returned, kept, out_hbm, out, sems):
+    saves = []
+    for i in range(4):
+        rows = pl.ds(i * (ROWS // 4), ROWS // 4)
+        nodes = iota((ROWS // 4, 128), 0) + i * (ROWS // 4)
+        place = jnp.concatenate([one_hot(nodes == senders[j]) for j in range(ROWS // 128)], axis=1)
+        out[rows, :] = kept[rows, :] + jnp.dot(place, returned[...], preferred_element_type=F32)
+        saves.append(pltpu.make_async_copy(out.at[rows, :], out_hbm.at[rows, :], sems.at[i]))
+        saves[i].start()
+    for copy in saves:
+        copy.wait()
 
 
 def dense_kernel(feats, cots, w_self, w_neigh, bias, recv, counts, acts, scaled, own, inv_ref):
@@ -211,11 +311,15 @@
     copy.wait()
 
 
-def backward_remote_kernel(keys_s, active_s, keys_v, spread_hbm, out, spread, rows_ref, acc, sem):
-    load_spread(spread_hbm, spread, sem)
-    acc[...] = jnp.zeros_like(acc)
-    scatter_back(keys_s, active_s, keys_v, spread, rows_ref, acc, 1)
-    out[...] = acc[...].astype(BF16)
+def backward_remote_kernel(spread, adj_hbm, out, adj, sems):
+    loads = [pltpu.make_async_copy(adj_hbm.at[i], adj.at[i], sems.at[i]) for i in range(PART // CHUNK)]
+    for copy in loads:
+        copy.start()
+    total = jnp.zeros((ROWS, WIDTH), F32)
+    for i, copy in enumerate(loads):
+        copy.wait()
+        total = total + jnp.dot(adj[i], spread[i * CHUNK : i * CHUNK + CHUNK, :], preferred_element_type=F32)
+    out[...] = total.astype(BF16)
 
 
 def backward_local_kernel(keys_s, active_s, keys_v, own, spread_hbm, out, spread, rows_ref, sem):
@@ -226,7 +330,8 @@
 
 VMEM = pl.BlockSpec(memory_space=pltpu.VMEM)
 ANY = pl.BlockSpec(memory_space=pl.ANY)
-PARAMS = pltpu.CompilerParams(vmem_limit_bytes=40 << 20)
+HBM = pl.BlockSpec(memory_space=pltpu.HBM)
+PARAMS = pltpu.CompilerParams(vmem_limit_bytes=30 << 20)
 
 
 def call(kernel, in_specs, out_shape, scratch, name):
@@ -248,13 +353,21 @@
 
 def local(features, cotangent, w_self, w_neigh, bias, send_rows, edge_src, edge_dst, tile_count):
     peers, capacity = send_rows.shape[2], send_rows.shape[3]
-    senders = send_rows.reshape(peers * capacity)
-    nodes = jnp.arange(ROWS, dtype=jnp.int32)
-    choose = (senders[:, None] == nodes[None, :]).astype(BF16)
-    picked = jnp.dot(choose, features, preferred_element_type=F32).astype(BF16)
-    remote = lax.all_to_all(
-        picked.reshape(peers, capacity, WIDTH), "dom", split_axis=0, concat_axis=0, tiled=True
-    ).reshape(peers * capacity, WIDTH)
+    shape = jax.ShapeDtypeStruct
+    picked = pl.pallas_call(
+        pick_kernel,
+        grid=(1,),
+        in_specs=[
+            pl.BlockSpec((capacity, peers), lambda i: (0, 0)),
+            pl.BlockSpec((ROWS, WIDTH), lambda i: (0, 0)),
+        ],
+        out_specs=pl.BlockSpec((peers, capacity, WIDTH), lambda i: (0, 0, 0)),
+        out_shape=shape((peers, capacity, WIDTH), BF16),
+        scratch_shapes=[pltpu.VMEM((peers, capacity, WIDTH), F32)],
+        compiler_params=PARAMS,
+        name="pick_rows",
+    )(in_hbm(jnp.transpose(send_rows.reshape(peers, capacity))), in_hbm(features))
+    remote = lax.all_to_all(picked, "dom", split_axis=0, concat_axis=0, tiled=True).reshape(peers * capacity, WIDTH)
 
     sources = edge_src.reshape(EDGES)
     targets = edge_dst.reshape(EDGES)
@@ -264,22 +377,53 @@
     keys_s = lax.sort(jnp.where(live, keys, ACTIVE_END))
     keys_v = keys_s.reshape(EDGES // 128, 1, 128)
 
-    shape = jax.ShapeDtypeStruct
-    before, counts = call(
-        forward_local_kernel,
-        [VMEM, VMEM],
-        (shape((PADDED, WIDTH), F32), shape((4, CNT, WIDTH), BF16)),
-        [],
-        "aggregate_local",
+    adj, before, counts = pl.pallas_call(
+        prepare_kernel,
+        grid_spec=pltpu.PrefetchScalarGridSpec(
+            num_scalar_prefetch=2,
+            grid=(),
+            in_specs=[VMEM, VMEM],
+            out_specs=(HBM, HBM, VMEM),
+            scratch_shapes=[
+                pltpu.VMEM((PADDED, ROWS), BF16),
+                pltpu.VMEM((PADDED, WIDTH), F32),
+                pltpu.SemaphoreType.DMA((2,)),
+            ],
+        ),
+        out_shape=(
+            pltpu.HBM((PART, ROWS), BF16),
+            pltpu.HBM((PART, WIDTH), F32),
+            shape((4, CNT, WIDTH), BF16),
+        ),
+        compiler_params=PARAMS,
+        name="prepare",
     )(keys_s, active, keys_v, features)
-    partial = call(
+    chunks = PART // CHUNK
+    partial = pl.pallas_call(
         forward_remote_kernel,
-        [VMEM, VMEM, VMEM, ANY],
-        shape((4, ROWS + CNT, WIDTH), BF16),
-        [pltpu.VMEM((PADDED, WIDTH), F32), pltpu.SemaphoreType.DMA],
-        "aggregate_remote",
-    )(keys_s, active, keys_v, remote, counts, before)
+        in_specs=[VMEM, VMEM, HBM, HBM],
+        out_specs=HBM,
+        out_shape=pltpu.HBM((4, ROWS + CNT, WIDTH), BF16),
+        scratch_shapes=[
+            pltpu.VMEM((chunks, CHUNK, ROWS), BF16),
+            pltpu.VMEM((chunks, CHUNK, WIDTH), F32),
+            pltpu.VMEM((4, ROWS + CNT, WIDTH), BF16),
+            pltpu.SemaphoreType.DMA((3, chunks)),
+        ],
+        compiler_params=PARAMS,
+        name="aggregate_remote",
+    )(remote, counts, in_hbm(adj), in_hbm(before))
     recv = lax.all_to_all(partial, "src", split_axis=0, concat_axis=0, tiled=True)
+    adj, partial = lax.optimization_barrier((adj, partial))
+    adj_t = pl.pallas_call(
+        transpose_kernel,
+        grid=(chunks,),
+        in_specs=[pl.BlockSpec((CHUNK, ROWS), lambda i: (i, 0))],
+        out_specs=pl.BlockSpec((1, ROWS, CHUNK), lambda i: (i, 0, 0)),
+        out_shape=pltpu.HBM((chunks, ROWS, CHUNK), BF16),
+        compiler_params=PARAMS,
+        name="adjacency_transposed",
+    )(in_hbm(adj))
 
     block = ROWS // 4
     tile = pl.BlockSpec((block, WIDTH), lambda i: (i, 0))
@@ -298,24 +442,26 @@
             pl.BlockSpec((4, CNT, WIDTH), lambda i: (0, ROWS // CNT, 0)),
         ],
         out_specs=(tile, four, tile),
-        out_shape=(shape((ROWS, WIDTH), BF16), shape((4, ROWS, WIDTH), BF16), shape((ROWS, WIDTH), F32)),
+        out_shape=(shape((ROWS, WIDTH), BF16), pltpu.HBM((4, ROWS, WIDTH), BF16), pltpu.HBM((ROWS, WIDTH), F32)),
         scratch_shapes=[pltpu.VMEM((8, 1, 128), F32)],
         compiler_params=PARAMS,
         name="dense_layer",
-    )(features, cotangent, w_self, w_neigh, bias.reshape(1, WIDTH), recv, recv)
+    )(features, in_hbm(cotangent), w_self, w_neigh, bias.reshape(1, WIDTH), recv, recv)
     spread = lax.all_to_all(scaled, "src", split_axis=0, concat_axis=0, tiled=True).reshape(PART, WIDTH)
 
     held = [
         pltpu.VMEM((PADDED, WIDTH), BF16),
         pltpu.VMEM((CHUNK, WIDTH), F32),
     ]
-    outgoing = call(
+    outgoing = pl.pallas_call(
         backward_remote_kernel,
-        [VMEM, ANY],
-        shape((ROWS, WIDTH), BF16),
-        held + [pltpu.VMEM((ROWS, WIDTH), F32), pltpu.SemaphoreType.DMA],
-        "scatter_remote",
-    )(keys_s, active, keys_v, spread)
+        in_specs=[VMEM, HBM],
+        out_specs=VMEM,
+        out_shape=pltpu.HBM((ROWS, WIDTH), BF16),
+        scratch_shapes=[pltpu.VMEM((chunks, ROWS, CHUNK), BF16), pltpu.SemaphoreType.DMA((chunks,))],
+        compiler_params=PARAMS,
+        name="scatter_remote",
+    )(spread, in_hbm(adj_t))
     returned = lax.all_to_all(
         outgoing.reshape(peers, capacity, WIDTH), "dom", split_axis=0, concat_axis=0, tiled=True
     ).reshape(peers * capacity, WIDTH)
@@ -326,9 +472,16 @@
         held + [pltpu.SemaphoreType.DMA],
         "scatter_local",
     )(keys_s, active, keys_v, own, spread)
-    place = (nodes[:, None] == senders[None, :]).astype(BF16)
-    incoming = jnp.dot(place, returned, preferred_element_type=F32)
-    return acts, kept + incoming
+    total = pl.pallas_call(
+        combine_kernel,
+        in_specs=[VMEM] * 3,
+        out_specs=HBM,
+        out_shape=pltpu.HBM((ROWS, WIDTH), F32),
+        scratch_shapes=[pltpu.VMEM((ROWS, WIDTH), F32), pltpu.SemaphoreType.DMA((4,))],
+        compiler_params=PARAMS,
+        name="combine",
+    )(send_rows.reshape(peers * capacity // 128, 1, 128), returned, kept)
+    return acts, total
 
 
 def solution(mesh):

time: 187 us -> 184 us (0.984)
  blocking collectives: 26.9 us -> 0 us
  Pallas kernels: 40.5 us -> 57.6 us
  waiting for transfers between devices: 62.6 us -> 77.2 us
  local copies, waits for them, and re-layouts: 7.67 us -> 1.45 us
  matrix products: 5.84 us -> 0 us
  starting transfers between devices: 35 us -> 37.2 us
    all_to_all x1 -> x0, blocking collectives: 26.9 us -> none  [local(): lax.all_to_all(scaled, 'src', split_axis=0, concat_axis=0, tiled=True)]
    pallas_call x3 -> x6, Pallas kernels: 28.9 us -> 45.9 us  [the longest x1 15.2 us: local(): pl.pallas_call(prepare_kernel, grid_spec=pltpu.PrefetchScalarGridSpec(num...]
    all_to_all x1 -> x2, waiting for transfers between devices: 13.2 us -> 25.6 us  [the longest x1 15.6 us: local(): lax.all_to_all(scaled, 'src', split_axis=0, concat_axis=0, tiled=True)]
    unnamed x27 -> x13, local copies, waits for them, and re-layouts: 7.56 us -> 1.35 us
    dot_general x2 -> x0, matrix products: 5.84 us -> none  [the longest x1 3.17 us: local(): incoming = jnp.dot(place, returned, preferred_element_type=F32)]
    all_to_all x1 -> x2, starting transfers between devices: 19.5 us -> 23.1 us  [the longest x1 19.5 us: local(): lax.all_to_all(picked, 'dom', split_axis=0, concat_axis=0, tiled=True)]
    all_to_all x1, starting transfers between devices: 11.9 us -> 9.96 us  [local(): lax.all_to_all(outgoing.reshape(peers, capacity, WIDTH), 'dom', split_axi...]
  transfers between devices with their start and end apart: 3 -> 4, of which waited for: 3 -> 4; matrix products, arithmetic and copies ran while one was open for 4% -> 4% of each run, Pallas kernels for 10% -> 18%
where the time goes in v2:
time: 184 us; the launch traced here: 183 us
  waiting for transfers between devices  77.2 us (42%)
  Pallas kernels  57.6 us (31%)
  starting transfers between devices  37.2 us (20%)
  other arithmetic  7.62 us (4%)
    all_to_all x1, waiting for transfers between devices, local(): lax.all_to_all(partial, 'src', split_axis=0, concat_axis=0, tiled=True)  26.8 us
    all_to_all x1, waiting for transfers between devices, local(): lax.all_to_all(outgoing.reshape(peers, capacity, WIDTH), 'dom', split_axi...  24.8 us
    all_to_all x1, starting transfers between devices, local(): lax.all_to_all(picked, 'dom', split_axis=0, concat_axis=0, tiled=True)  19.5 us
    all_to_all x1, waiting for transfers between devices, local(): lax.all_to_all(scaled, 'src', split_axis=0, concat_axis=0, tiled=True)  15.6 us
    pallas_call x1, Pallas kernels, local(): pl.pallas_call(prepare_kernel, grid_spec=pltpu.PrefetchScalarGridSpec(num...  15.2 us
    all_to_all x1, waiting for transfers between devices, local(): lax.all_to_all(picked, 'dom', split_axis=0, concat_axis=0, tiled=True)  10 us
    all_to_all x1, starting transfers between devices, local(): lax.all_to_all(outgoing.reshape(peers, capacity, WIDTH), 'dom', split_axi...  9.96 us
    pallas_call x1, Pallas kernels, local(): pl.pallas_call(transpose_kernel, grid=(chunks,), in_specs=[pl.BlockSpec((...  9.87 us
  transfers between devices with their start and end apart: 4, of which 4 were waited for; matrix products, arithmetic and copies ran while one was open for 4% of the time, Pallas kernels for 18%

profile of v2, /device:TPU:33, one launch (start us, length us, event | category | flops | bytes accessed | tf_op | source)
XLA Modules:
  0.0 182.6 jit_solution(6767765650198811411)
XLA Ops:
  0.6 0.0 copy-start
  0.6 3.0 %pick_rows.1 = bf16[128,8,256]{2,1,0:T(8,128)(2,1)} custom-call(s32[8,128]{1,0:T(8,128)} %bitcast.24, bf16[1024,256]{1,0:T(8,128)(2,1)} %feats.1), custom_call_target="tpu_custom_call" | custom-call | tf_op jit(solution)/shard_map/pick_rows/pallas_call | solution.py:357
  3.6 19.5 %all-to-all-start = ((bf16[128,8,256]{2,1,0:T(8,128)(2,1)}), bf16[128,8,256]{2,1,0:T(8,128)(2,1)S(1)}, u32[]{:S(2)}, u32[]{:S(2)}) async-start(bf16[128,8,256]{2,1,0:T(8,128)(2,1)} %pick_rows.1), calls=%async_computation | async-start | bytes 1048576 | tf_op jit(solution)/shard_map/all_to_all | solution.py:370
  23.8 0.8 and_add_fusion
  24.6 6.8 %sort.10 = (s32[8192]{0:T(1024)S(1)}, s32[8192]{0:T(1024)}) sort(s32[8192]{0:T(1024)S(1)} %fusion, s32[8192]{0:T(1024)S(1)} %iota.7), dimensions={0}, to_apply=%region_0.1 | sort | flops 106496 | bytes 131072 | tf_op jit(solution)/shard_map/sort | solution.py:377
  31.4 0.0 copy-done
  31.4 15.2 %prepare.1 = (bf16[4096,1024]{1,0:T(8,128)(2,1)}, f32[4096,256]{1,0:T(8,128)}, bf16[4,16,256]{2,1,0:T(8,128)(2,1)S(1)}) custom-call(s32[8192]{0:T(1024)S(1)} %get-tuple-element.11.keys_s, s32[1]{0:T(128)} %bitcast.14.active_s, s32[64,1,128]{2,1,0:T(1,128)S(1)} %bitcast.19, bf16[1024,256]{1,0:T(8,128)(2,1)S(1)} %copy-done), custom_call_target="tpu_custom_call" | custom-call | tf_op jit(solution)/shard_map/prepare/pallas_call | solution.py:380
  46.7 10.0 %all-to-all-done = bf16[128,8,256]{2,1,0:T(8,128)(2,1)S(1)} async-done(((bf16[128,8,256]{2,1,0:T(8,128)(2,1)}), bf16[128,8,256]{2,1,0:T(8,128)(2,1)S(1)}, u32[]{:S(2)}, u32[]{:S(2)}) %all-to-all-start) | async-done | bytes 524320 | tf_op jit(solution)/shard_map/all_to_all | solution.py:370
  56.7 7.9 %aggregate_remote.1 = bf16[4,1040,256]{2,1,0:T(8,128)(2,1)} custom-call(bf16[1024,256]{1,0:T(8,128)(2,1)S(1)} %bitcast.18, bf16[4,16,256]{2,1,0:T(8,128)(2,1)S(1)} %get-tuple-element.12.counts, bf16[4096,1024]{1,0:T(8,128)(2,1)} %get-tuple-element.17.adj_hbm.adj, f32[4096,256]{1,0:T(8,128)} %get-tuple-element.14.local_hbm), custom_call_target="tpu_custom_call" | custom-call | tf_op jit(solution)/shard_map/aggregate_remote/pallas_call | solution.py:402
  64.6 0.0 copy-start.5
  64.6 0.0 copy-start.2
  64.7 0.0 copy-start.3
  64.7 4.2 %all-to-all-start.1 = ((bf16[4,1040,256]{2,1,0:T(8,128)(2,1)}), bf16[4,1040,256]{2,1,0:T(8,128)(2,1)S(1)}, u32[]{:S(2)}, u32[]{:S(2)}) async-start(bf16[4,1040,256]{2,1,0:T(8,128)(2,1)} %aggregate_remote.1), calls=%async_computation.1 | async-start | bytes 4259840 | tf_op jit(solution)/shard_map/all_to_all | solution.py:416
  68.8 0.0 copy-done.5
  68.8 26.8 %all-to-all-done.1.recv.counts = bf16[4,1040,256]{2,1,0:T(8,128)(2,1)S(1)} async-done(((bf16[4,1040,256]{2,1,0:T(8,128)(2,1)}), bf16[4,1040,256]{2,1,0:T(8,128)(2,1)S(1)}, u32[]{:S(2)}, u32[]{:S(2)}) %all-to-all-start.1) | async-done | bytes 2129952 | tf_op jit(solution)/shard_map/all_to_all | solution.py:416
  95.6 0.0 copy-done.2
  95.6 0.0 copy-done.3
  95.6 4.7 %dense_layer.1 = (bf16[1024,256]{1,0:T(8,128)(2,1)}, bf16[4,1024,256]{2,1,0:T(8,128)(2,1)}, f32[1024,256]{1,0:T(8,128)}) custom-call(bf16[1024,256]{1,0:T(8,128)(2,1)S(1)} %copy-done, bf16[1024,256]{1,0:T(8,128)(2,1)} %cots.1, bf16[256,256]{1,0:T(8,128)(2,1)S(1)} %copy-done.2, bf16[256,256]{1,0:T(8,128)(2,1)S(1)} %copy-done.3, ...), custom_call_target="tpu_custom_call" | custom-call | tf_op jit(solution)/shard_map/dense_layer/pallas_call | solution.py:432
  100.3 3.6 %all-to-all-start.2 = ((bf16[4,1024,256]{2,1,0:T(8,128)(2,1)}), bf16[4,1024,256]{2,1,0:T(8,128)(2,1)S(1)}, u32[]{:S(2)}, u32[]{:S(2)}) async-start(bf16[4,1024,256]{2,1,0:T(8,128)(2,1)} %get-tuple-element.16), calls=%async_computation.2 | async-start | bytes 4194304 | tf_op jit(solution)/shard_map/all_to_all | solution.py:450
  104.0 9.9 %adjacency_transposed.1.adj_hbm = bf16[8,1024,512]{2,1,0:T(8,128)(2,1)} custom-call(bf16[4096,1024]{1,0:T(8,128)(2,1)} %get-tuple-element.17.adj_hbm.adj), custom_call_target="tpu_custom_call" | custom-call | tf_op jit(solution)/shard_map/adjacency_transposed/pallas_call | solution.py:418
  113.8 15.6 %all-to-all-done.2 = bf16[4,1024,256]{2,1,0:T(8,128)(2,1)S(1)} async-done(((bf16[4,1024,256]{2,1,0:T(8,128)(2,1)}), bf16[4,1024,256]{2,1,0:T(8,128)(2,1)S(1)}, u32[]{:S(2)}, u32[]{:S(2)}) %all-to-all-start.2) | async-done | bytes 2097184 | tf_op jit(solution)/shard_map/all_to_all | solution.py:450
  129.4 0.0 copy-start.4
  129.4 7.2 %scatter_remote.1 = bf16[1024,256]{1,0:T(8,128)(2,1)} custom-call(bf16[4096,256]{1,0:T(8,128)(2,1)S(1)} %bitcast.16, bf16[8,1024,512]{2,1,0:T(8,128)(2,1)} %adjacency_transposed.1.adj_hbm), custom_call_target="tpu_custom_call" | custom-call | tf_op jit(solution)/shard_map/scatter_remote/pallas_call | solution.py:456
  136.7 10.0 %all-to-all-start.3 = ((bf16[128,8,256]{2,1,0:T(8,128)(2,1)}), bf16[128,8,256]{2,1,0:T(8,128)(2,1)}, u32[]{:S(2)}, u32[]{:S(2)}) async-start(bf16[128,8,256]{2,1,0:T(8,128)(2,1)} %bitcast.22), calls=%async_computation.3 | async-start | bytes 1048576 | tf_op jit(solution)/shard_map/all_to_all | solution.py:465
  146.6 0.0 copy-done.4
  146.6 0.1 copy.12
  146.7 0.1 reshape.50
  146.8 0.0 copy-start.1
  146.8 1.2 copy-done.1
  148.1 7.0 %scatter_local.1.kept = f32[1024,256]{1,0:T(8,128)S(1)} custom-call(s32[8192]{0:T(1024)S(1)} %get-tuple-element.11.keys_s, s32[1]{0:T(128)} %bitcast.15.active_s, s32[64,1,128]{2,1,0:T(1,128)S(1)} %bitcast.20, f32[1024,256]{1,0:T(8,128)S(1)} %copy-done.1, bf16[4096,256]{1,0:T(8,128)(2,1)S(1)} %bitcast.17), custom_call_target="tpu_custom_call" | custom-call | tf_op jit(solution)/shard_map/scatter_local/pallas_call | solution.py:468
  155.1 24.8 %all-to-all-done.3 = bf16[128,8,256]{2,1,0:T(8,128)(2,1)} async-done(((bf16[128,8,256]{2,1,0:T(8,128)(2,1)}), bf16[128,8,256]{2,1,0:T(8,128)(2,1)}, u32[]{:S(2)}, u32[]{:S(2)}) %all-to-all-start.3) | async-done | bytes 524320 | tf_op jit(solution)/shard_map/all_to_all | solution.py:465
  179.9 2.6 %combine.1 = f32[1024,256]{1,0:T(8,128)} custom-call(s32[8,1,128]{2,1,0:T(1,128)S(1)} %bitcast.21, bf16[1024,256]{1,0:T(8,128)(2,1)} %bitcast.10.returned, f32[1024,256]{1,0:T(8,128)S(1)} %scatter_local.1.kept), custom_call_target="tpu_custom_call" | custom-call | tf_op jit(solution)/shard_map/combine/pallas_call | solution.py:475
  (3 shorter events, 0.0 us)
Async XLA Ops:
  0.6 30.8 %copy-start = (bf16[1024,256]{1,0:T(8,128)(2,1)S(1)}, bf16[1024,256]{1,0:T(8,128)(2,1)}, u32[]{:S(2)}) copy-start(bf16[1024,256]{1,0:T(8,128)(2,1)} %feats.1) | copy-start | bytes 1572868
  3.6 53.1 %all-to-all-start = ((bf16[128,8,256]{2,1,0:T(8,128)(2,1)}), bf16[128,8,256]{2,1,0:T(8,128)(2,1)S(1)}, u32[]{:S(2)}, u32[]{:S(2)}) async-start(bf16[128,8,256]{2,1,0:T(8,128)(2,1)} %pick_rows.1), calls=%async_computation | async-start | bytes 1048576 | tf_op jit(solution)/shard_map/all_to_all | solution.py:370
  64.6 4.2 %copy-start.5 = (bf16[256]{0:T(256)(128)(2,1)S(1)}, bf16[256]{0:T(256)(128)(2,1)}, u32[]{:S(2)}) copy-start(bf16[256]{0:T(256)(128)(2,1)} %param.13) | copy-start | bytes 1540
  64.6 31.0 %copy-start.2 = (bf16[256,256]{1,0:T(8,128)(2,1)S(1)}, bf16[256,256]{1,0:T(8,128)(2,1)}, u32[]{:S(2)}) copy-start(bf16[256,256]{1,0:T(8,128)(2,1)} %w_self.1) | copy-start | bytes 393220
  64.7 31.0 %copy-start.3 = (bf16[256,256]{1,0:T(8,128)(2,1)S(1)}, bf16[256,256]{1,0:T(8,128)(2,1)}, u32[]{:S(2)}) copy-start(bf16[256,256]{1,0:T(8,128)(2,1)} %w_neigh.1) | copy-start | bytes 393220
  64.7 30.9 %all-to-all-start.1 = ((bf16[4,1040,256]{2,1,0:T(8,128)(2,1)}), bf16[4,1040,256]{2,1,0:T(8,128)(2,1)S(1)}, u32[]{:S(2)}, u32[]{:S(2)}) async-start(bf16[4,1040,256]{2,1,0:T(8,128)(2,1)} %aggregate_remote.1), calls=%async_computation.1 | async-start | bytes 4259840 | tf_op jit(solution)/shard_map/all_to_all | solution.py:416
  100.3 29.1 %all-to-all-start.2 = ((bf16[4,1024,256]{2,1,0:T(8,128)(2,1)}), bf16[4,1024,256]{2,1,0:T(8,128)(2,1)S(1)}, u32[]{:S(2)}, u32[]{:S(2)}) async-start(bf16[4,1024,256]{2,1,0:T(8,128)(2,1)} %get-tuple-element.16), calls=%async_computation.2 | async-start | bytes 4194304 | tf_op jit(solution)/shard_map/all_to_all | solution.py:450
  129.4 17.2 %copy-start.4 = (s32[1,1,128,8]{2,3,1,0:T(8,128)S(1)}, s32[1,1,128,8]{2,3,1,0:T(8,128)}, u32[]{:S(2)}) copy-start(s32[1,1,128,8]{2,3,1,0:T(8,128)} %param.14) | copy-start | bytes 12292
  136.7 43.2 %all-to-all-start.3 = ((bf16[128,8,256]{2,1,0:T(8,128)(2,1)}), bf16[128,8,256]{2,1,0:T(8,128)(2,1)}, u32[]{:S(2)}, u32[]{:S(2)}) async-start(bf16[128,8,256]{2,1,0:T(8,128)(2,1)} %bitcast.22), calls=%async_computation.3 | async-start | bytes 1048576 | tf_op jit(solution)/shard_map/all_to_all | solution.py:465
  146.8 1.2 copy-start.1

commit v3 on v2

--- a/solution.py
+++ b/solution.py
@@ -1,3 +1,5 @@
+import functools
+
 import jax
 import jax.numpy as jnp
 from jax import lax
@@ -181,32 +183,29 @@
     out[0] = jnp.transpose(adj[...])
 
 
-def forward_remote_kernel(table, counts, adj_hbm, local_hbm, out_hbm, adj, local_part, out, sems):
+def forward_remote_kernel(shifts, owner_s, table, counts, adj_hbm, local_hbm, *refs):
+    outs, (adj, local_part, sems) = refs[:-3], refs[-3:]
+    halves = ROWS // CHUNK
     loads = []
-    for i in range(PART // CHUNK):
-        rows = pl.ds(i * CHUNK, CHUNK)
-        loads.append(
-            (
+    for n in range(len(outs)):
+        for h in range(halves):
+            rows = pl.ds(pl.multiple_of(owner_s[shifts[n]] * ROWS + h * CHUNK, CHUNK), CHUNK)
+            i = n * halves + h
+            pair = (
                 pltpu.make_async_copy(adj_hbm.at[rows, :], adj.at[i], sems.at[0, i]),
                 pltpu.make_async_copy(local_hbm.at[rows, :], local_part.at[i], sems.at[1, i]),
             )
-        )
-        for copy in loads[i]:
-            copy.start()
-    for s in range(4):
-        out[s, ROWS:, :] = counts[s]
-    saves = []
-    for i in range(PART // CHUNK):
-        for copy in loads[i]:
-            copy.wait()
-        total = local_part[i] + jnp.dot(adj[i], table[...], preferred_element_type=F32)
-        s, h = i // 2, i % 2
-        out[s, h * CHUNK : h * CHUNK + CHUNK, :] = total.astype(BF16)
-        if h == 1:
-            saves.append(pltpu.make_async_copy(out.at[s], out_hbm.at[s], sems.at[2, s]))
-            saves[s].start()
-    for copy in saves:
-        copy.wait()
+            for copy in pair:
+                copy.start()
+            loads.append(pair)
+    for n, out in enumerate(outs):
+        out[ROWS:, :] = counts[owner_s[shifts[n]]]
+        for h in range(halves):
+            i = n * halves + h
+            for copy in loads[i]:
+                copy.wait()
+            total = local_part[i] + jnp.dot(adj[i], table[...], preferred_element_type=F32)
+            out[h * CHUNK : h * CHUNK + CHUNK, :] = total.astype(BF16)
 
 
 def pick_kernel(senders, table, out, acc):
@@ -230,14 +229,15 @@
         copy.wait()
 
 
-def dense_kernel(feats, cots, w_self, w_neigh, bias, recv, counts, acts, scaled, own, inv_ref):
+def dense_kernel(feats, cots, w_self, w_neigh, bias, *refs):
+    parts, counts, (acts, scaled, up_out, inv_ref) = refs[:4], refs[4:8], refs[8:]
     i = pl.program_id(0)
 
     @pl.when(i == 0)
     def _():
         deg = jnp.zeros((8, 128), F32)
         for s in range(4):
-            c = counts[s].astype(F32)
+            c = counts[s][...].astype(F32)
             deg = deg + c[:8, :128] * 256.0 + c[:8, 128:]
         inv = 1.0 / jnp.maximum(deg, 1.0)
         for r in range(8):
@@ -245,9 +245,9 @@
 
     cols = [key_column(inv_ref[2 * i + r]) for r in range(2)]
     inverse = jnp.concatenate([jnp.concatenate([c, c], axis=1) for c in cols], axis=0)
-    totals = recv[0].astype(F32)
+    totals = parts[0][...].astype(F32)
     for s in range(1, 4):
-        totals = totals + recv[s].astype(F32)
+        totals = totals + parts[s][...].astype(F32)
     mean = (totals * inverse).astype(BF16)
     pre = (
         jnp.dot(feats[...], w_self[...], preferred_element_type=F32)
@@ -258,12 +258,9 @@
     acts[...] = (pre * sigma).astype(BF16)
     slope = sigma * (1.0 + pre * (1.0 - sigma))
     up = (cots[...].astype(F32) * slope).astype(BF16)
-    contract = (((1,), (1,)), ((), ()))
-    back = lax.dot_general(up, w_neigh[...], contract, preferred_element_type=F32)
-    value = (back * inverse).astype(BF16)
-    for s in range(4):
-        scaled[s] = value
-    own[...] = lax.dot_general(up, w_self[...], contract, preferred_element_type=F32)
+    back = lax.dot_general(up, w_neigh[...], (((1,), (1,)), ((), ())), preferred_element_type=F32)
+    scaled[...] = (back * inverse).astype(BF16)
+    up_out[...] = up
 
 
 def scatter_back(keys_s, active_s, keys_v, spread, rows_ref, acc, remote):
@@ -304,51 +301,43 @@
     lax.fori_loop(lo // CHUNK, (hi + CHUNK - 1) // CHUNK, tile, 0)
 
 
-def load_spread(spread_hbm, spread, sem):
-    copy = pltpu.make_async_copy(spread_hbm, spread.at[pl.ds(0, PART), :], sem)
-    copy.start()
+def piece_sum(owner_s, pieces, adj, start):
+    halves = ROWS // CHUNK
+    total = start
+    for shift, piece in pieces:
+        for h in range(halves):
+            rows = piece[h * CHUNK : h * CHUNK + CHUNK, :]
+            part = jnp.dot(adj[owner_s[shift] * halves + h], rows, preferred_element_type=F32)
+            total = part if total is None else total + part
+    return total
+
+
+def backward_near_kernel(owner_s, own, left, right, adj, out):
+    out[...] = piece_sum(owner_s, ((0, own), (3, left), (1, right)), adj, None)
+
+
+def backward_far_kernel(owner_s, far, near, adj, out):
+    out[...] = piece_sum(owner_s, ((2, far),), adj, near[...]).astype(BF16)
+
+
+def backward_local_kernel(keys_s, active_s, owner_s, keys_v, up, w_self, p0, p1, p2, p3, out, spread, rows_ref, sems):
+    loads = []
+    for n, (shift, piece) in enumerate(((0, p0), (3, p1), (1, p2), (2, p3))):
+        rows = pl.ds(pl.multiple_of(owner_s[shift] * ROWS, ROWS), ROWS)
+        loads.append(pltpu.make_async_copy(piece, spread.at[rows, :], sems.at[n]))
+        loads[n].start()
     spread[PART:, :] = jnp.zeros((WIN, WIDTH), BF16)
-    copy.wait()
-
-
-def backward_remote_kernel(spread, adj_hbm, out, adj, sems):
-    loads = [pltpu.make_async_copy(adj_hbm.at[i], adj.at[i], sems.at[i]) for i in range(PART // CHUNK)]
+    out[...] = lax.dot_general(up[...], w_self[...], (((1,), (1,)), ((), ())), preferred_element_type=F32)
     for copy in loads:
-        copy.start()
-    total = jnp.zeros((ROWS, WIDTH), F32)
-    for i, copy in enumerate(loads):
         copy.wait()
-        total = total + jnp.dot(adj[i], spread[i * CHUNK : i * CHUNK + CHUNK, :], preferred_element_type=F32)
-    out[...] = total.astype(BF16)
-
-
-def backward_local_kernel(keys_s, active_s, keys_v, own, spread_hbm, out, spread, rows_ref, sem):
-    load_spread(spread_hbm, spread, sem)
-    out[...] = own[...]
     scatter_back(keys_s, active_s, keys_v, spread, rows_ref, out, 0)
 
 
 VMEM = pl.BlockSpec(memory_space=pltpu.VMEM)
 ANY = pl.BlockSpec(memory_space=pl.ANY)
 HBM = pl.BlockSpec(memory_space=pltpu.HBM)
-PARAMS = pltpu.CompilerParams(vmem_limit_bytes=30 << 20)
-
-
-def call(kernel, in_specs, out_shape, scratch, name):
-    single = not isinstance(out_shape, tuple)
-    return pl.pallas_call(
-        kernel,
-        grid_spec=pltpu.PrefetchScalarGridSpec(
-            num_scalar_prefetch=2,
-            grid=(),
-            in_specs=in_specs,
-            out_specs=VMEM if single else tuple(VMEM for _ in out_shape),
-            scratch_shapes=scratch,
-        ),
-        out_shape=out_shape,
-        compiler_params=PARAMS,
-        name=name,
-    )
+def params(mib):
+    return pltpu.CompilerParams(vmem_limit_bytes=mib << 20)
 
 
 def local(features, cotangent, w_self, w_neigh, bias, send_rows, edge_src, edge_dst, tile_count):
@@ -364,7 +353,7 @@
         out_specs=pl.BlockSpec((peers, capacity, WIDTH), lambda i: (0, 0, 0)),
         out_shape=shape((peers, capacity, WIDTH), BF16),
         scratch_shapes=[pltpu.VMEM((peers, capacity, WIDTH), F32)],
-        compiler_params=PARAMS,
+        compiler_params=params(8),
         name="pick_rows",
     )(in_hbm(jnp.transpose(send_rows.reshape(peers, capacity))), in_hbm(features))
     remote = lax.all_to_all(picked, "dom", split_axis=0, concat_axis=0, tiled=True).reshape(peers * capacity, WIDTH)
@@ -395,90 +384,118 @@
             pltpu.HBM((PART, WIDTH), F32),
             shape((4, CNT, WIDTH), BF16),
         ),
-        compiler_params=PARAMS,
+        compiler_params=params(30),
         name="prepare",
     )(keys_s, active, keys_v, features)
     chunks = PART // CHUNK
-    partial = pl.pallas_call(
-        forward_remote_kernel,
-        in_specs=[VMEM, VMEM, HBM, HBM],
-        out_specs=HBM,
-        out_shape=pltpu.HBM((4, ROWS + CNT, WIDTH), BF16),
-        scratch_shapes=[
-            pltpu.VMEM((chunks, CHUNK, ROWS), BF16),
-            pltpu.VMEM((chunks, CHUNK, WIDTH), F32),
-            pltpu.VMEM((4, ROWS + CNT, WIDTH), BF16),
-            pltpu.SemaphoreType.DMA((3, chunks)),
-        ],
-        compiler_params=PARAMS,
-        name="aggregate_remote",
-    )(remote, counts, in_hbm(adj), in_hbm(before))
-    recv = lax.all_to_all(partial, "src", split_axis=0, concat_axis=0, tiled=True)
+    rank = lax.axis_index("src")
+
+    order = lax.optimization_barrier((rank + jnp.arange(4, dtype=jnp.int32)) % 4)
+
+    def shifted(x, k):
+        return lax.ppermute(x, "src", [(j, (j + k) % 4) for j in range(4)])
+
+    def partials(table, *shifts):
+        count = len(shifts)
+        return pl.pallas_call(
+            functools.partial(forward_remote_kernel, shifts),
+            grid_spec=pltpu.PrefetchScalarGridSpec(
+                num_scalar_prefetch=1,
+                grid=(),
+                in_specs=[VMEM, VMEM, HBM, HBM],
+                out_specs=[VMEM] * count,
+                scratch_shapes=[
+                    pltpu.VMEM((2 * count, CHUNK, ROWS), BF16),
+                    pltpu.VMEM((2 * count, CHUNK, WIDTH), F32),
+                    pltpu.SemaphoreType.DMA((2, 2 * count)),
+                ],
+            ),
+            out_shape=[shape((ROWS + CNT, WIDTH), BF16)] * count,
+            compiler_params=params(12),
+            name="aggregate_remote_" + "_".join(str(k) for k in shifts),
+        )(order, table, counts, in_hbm(adj), in_hbm(before))
+
+    (partial_far,) = partials(remote, 2)
+    from_far = shifted(partial_far, 2)
+    remote, partial_far = lax.optimization_barrier((remote, partial_far))
+    partial_next, partial_prev = partials(remote, 1, 3)
+    from_prev = shifted(partial_next, 1)
+    from_next = shifted(partial_prev, 3)
+    remote, partial = lax.optimization_barrier((remote, partial_next))
+    (partial_own,) = partials(remote, 0)
     adj, partial = lax.optimization_barrier((adj, partial))
     adj_t = pl.pallas_call(
         transpose_kernel,
         grid=(chunks,),
         in_specs=[pl.BlockSpec((CHUNK, ROWS), lambda i: (i, 0))],
         out_specs=pl.BlockSpec((1, ROWS, CHUNK), lambda i: (i, 0, 0)),
-        out_shape=pltpu.HBM((chunks, ROWS, CHUNK), BF16),
-        compiler_params=PARAMS,
+        out_shape=shape((chunks, ROWS, CHUNK), BF16),
+        compiler_params=params(10),
         name="adjacency_transposed",
     )(in_hbm(adj))
+    adj_t, from_far = lax.optimization_barrier((adj_t, from_far))
 
     block = ROWS // 4
     tile = pl.BlockSpec((block, WIDTH), lambda i: (i, 0))
     whole = pl.BlockSpec((WIDTH, WIDTH), lambda i: (0, 0))
-    four = pl.BlockSpec((4, block, WIDTH), lambda i: (0, i, 0))
-    acts, scaled, own = pl.pallas_call(
+    count_rows = pl.BlockSpec((CNT, WIDTH), lambda i: (ROWS // CNT, 0))
+    received = (partial_own, from_prev, from_next, from_far)
+    acts, scaled, up = pl.pallas_call(
         dense_kernel,
         grid=(4,),
-        in_specs=[
-            tile,
-            tile,
-            whole,
-            whole,
-            pl.BlockSpec((1, WIDTH), lambda i: (0, 0)),
-            four,
-            pl.BlockSpec((4, CNT, WIDTH), lambda i: (0, ROWS // CNT, 0)),
-        ],
-        out_specs=(tile, four, tile),
-        out_shape=(shape((ROWS, WIDTH), BF16), pltpu.HBM((4, ROWS, WIDTH), BF16), pltpu.HBM((ROWS, WIDTH), F32)),
+        in_specs=[tile, tile, whole, whole, pl.BlockSpec((1, WIDTH), lambda i: (0, 0))]
+        + [tile] * 4
+        + [count_rows] * 4,
+        out_specs=(tile, tile, tile),
+        out_shape=(shape((ROWS, WIDTH), BF16), pltpu.HBM((ROWS, WIDTH), BF16), pltpu.HBM((ROWS, WIDTH), BF16)),
         scratch_shapes=[pltpu.VMEM((8, 1, 128), F32)],
-        compiler_params=PARAMS,
+        compiler_params=params(10),
         name="dense_layer",
-    )(features, in_hbm(cotangent), w_self, w_neigh, bias.reshape(1, WIDTH), recv, recv)
-    spread = lax.all_to_all(scaled, "src", split_axis=0, concat_axis=0, tiled=True).reshape(PART, WIDTH)
-
-    held = [
-        pltpu.VMEM((PADDED, WIDTH), BF16),
-        pltpu.VMEM((CHUNK, WIDTH), F32),
-    ]
-    outgoing = pl.pallas_call(
-        backward_remote_kernel,
-        in_specs=[VMEM, HBM],
-        out_specs=VMEM,
-        out_shape=pltpu.HBM((ROWS, WIDTH), BF16),
-        scratch_shapes=[pltpu.VMEM((chunks, ROWS, CHUNK), BF16), pltpu.SemaphoreType.DMA((chunks,))],
-        compiler_params=PARAMS,
-        name="scatter_remote",
-    )(spread, in_hbm(adj_t))
+    )(features, in_hbm(cotangent), w_self, w_neigh, bias.reshape(1, WIDTH), *received, *received)
+    far = shifted(scaled, 2)
+    prev = shifted(scaled, 1)
+    follow = shifted(scaled, 3)
+
+    def backward(kernel, pieces, dtype, name):
+        return pl.pallas_call(
+            kernel,
+            grid_spec=pltpu.PrefetchScalarGridSpec(
+                num_scalar_prefetch=1, grid=(), in_specs=[VMEM] * (len(pieces) + 1), out_specs=VMEM
+            ),
+            out_shape=shape((ROWS, WIDTH), dtype),
+            compiler_params=params(8),
+            name=name,
+        )(order, *pieces, adj_t)
+
+    near = backward(backward_near_kernel, (scaled, prev, follow), F32, "scatter_near")
+    outgoing = backward(backward_far_kernel, (far, near), BF16, "scatter_far")
     returned = lax.all_to_all(
         outgoing.reshape(peers, capacity, WIDTH), "dom", split_axis=0, concat_axis=0, tiled=True
     ).reshape(peers * capacity, WIDTH)
-    kept = call(
+    kept = pl.pallas_call(
         backward_local_kernel,
-        [VMEM, VMEM, ANY],
-        shape((ROWS, WIDTH), F32),
-        held + [pltpu.SemaphoreType.DMA],
-        "scatter_local",
-    )(keys_s, active, keys_v, own, spread)
+        grid_spec=pltpu.PrefetchScalarGridSpec(
+            num_scalar_prefetch=3,
+            grid=(),
+            in_specs=[VMEM] * 3 + [ANY] * 4,
+            out_specs=VMEM,
+            scratch_shapes=[
+                pltpu.VMEM((PADDED, WIDTH), BF16),
+                pltpu.VMEM((CHUNK, WIDTH), F32),
+                pltpu.SemaphoreType.DMA((4,)),
+            ],
+        ),
+        out_shape=shape((ROWS, WIDTH), F32),
+        compiler_params=params(10),
+        name="scatter_local",
+    )(keys_s, active, order, keys_v, up, w_self, scaled, prev, follow, far)
     total = pl.pallas_call(
         combine_kernel,
         in_specs=[VMEM] * 3,
         out_specs=HBM,
         out_shape=pltpu.HBM((ROWS, WIDTH), F32),
         scratch_shapes=[pltpu.VMEM((ROWS, WIDTH), F32), pltpu.SemaphoreType.DMA((4,))],
-        compiler_params=PARAMS,
+        compiler_params=params(8),
         name="combine",
     )(send_rows.reshape(peers * capacity // 128, 1, 128), returned, kept)
     return acts, total

time: 184 us -> 174 us (0.946)
  the two profiles are of different devices: /device:TPU:33 before, /device:TPU:39 now
where the time goes in v3:
time: 174 us; the launch traced here: 173 us
  Pallas kernels  58.1 us (33%)
  waiting for transfers between devices  50.8 us (29%)
  starting transfers between devices  50.5 us (29%)
  other arithmetic  7.63 us (4%)
  local copies, waits for them, and re-layouts  4.4 us (3%)
    ppermute x6, waiting for transfers between devices, shifted(): return lax.ppermute(x, 'src', [(j, (j + k) % 4) for j in range(4)])  22 us
    all_to_all x1, waiting for transfers between devices, local(): lax.all_to_all(outgoing.reshape(peers, capacity, WIDTH), 'dom', split_axi...  21.6 us
    all_to_all x1, starting transfers between devices, local(): lax.all_to_all(picked, 'dom', split_axis=0, concat_axis=0, tiled=True)  19.5 us
    ppermute x6, starting transfers between devices, shifted(): return lax.ppermute(x, 'src', [(j, (j + k) % 4) for j in range(4)])  17.5 us
    pallas_call x1, Pallas kernels, local(): pl.pallas_call(prepare_kernel, grid_spec=pltpu.PrefetchScalarGridSpec(num...  17.1 us
    all_to_all x1, starting transfers between devices, local(): lax.all_to_all(outgoing.reshape(peers, capacity, WIDTH), 'dom', split_axi...  13.5 us
    pallas_call x3, Pallas kernels, partials(): pl.pallas_call(functools.partial(forward_remote_kernel, shifts), grid_spe...  11.4 us
    pallas_call x1, Pallas kernels, local(): pl.pallas_call(backward_local_kernel, grid_spec=pltpu.PrefetchScalarGridS...  9.67 us
  transfers between devices with their start and end apart: 8, of which 7 were waited for; matrix products, arithmetic and copies ran while one was open for 5% of the time, Pallas kernels for 25%

profile of v3, /device:TPU:39, one launch (start us, length us, event | category | flops | bytes accessed | tf_op | source)
XLA Modules:
  0.0 173.1 jit_solution(50245266255699275)
XLA Ops:
  0.6 2.9 %pick_rows.1 = bf16[128,8,256]{2,1,0:T(8,128)(2,1)} custom-call(s32[8,128]{1,0:T(8,128)} %bitcast.23, bf16[1024,256]{1,0:T(8,128)(2,1)} %feats.1), custom_call_target="tpu_custom_call" | custom-call | tf_op jit(solution)/shard_map/pick_rows/pallas_call | solution.py:346
  3.6 19.5 %all-to-all-start = ((bf16[128,8,256]{2,1,0:T(8,128)(2,1)}), bf16[128,8,256]{2,1,0:T(8,128)(2,1)S(1)}, u32[]{:S(2)}, u32[]{:S(2)}) async-start(bf16[128,8,256]{2,1,0:T(8,128)(2,1)} %pick_rows.1), calls=%async_computation | async-start | bytes 1048576 | tf_op jit(solution)/shard_map/all_to_all | solution.py:359
  23.7 0.8 and_add_fusion
  24.6 6.8 %sort.10 = (s32[8192]{0:T(1024)S(1)}, s32[8192]{0:T(1024)}) sort(s32[8192]{0:T(1024)S(1)} %fusion, s32[8192]{0:T(1024)S(1)} %iota.11), dimensions={0}, to_apply=%region_0.1 | sort | flops 106496 | bytes 131072 | tf_op jit(solution)/shard_map/sort | solution.py:366
  31.4 1.0 copy-done
  32.4 17.1 %prepare.1 = (bf16[4096,1024]{1,0:T(8,128)(2,1)}, f32[4096,256]{1,0:T(8,128)}, bf16[4,16,256]{2,1,0:T(8,128)(2,1)S(1)}) custom-call(s32[8192]{0:T(1024)S(1)} %get-tuple-element.16.keys_s, s32[1]{0:T(128)} %bitcast.13.active_s, s32[64,1,128]{2,1,0:T(1,128)S(1)} %bitcast.19, bf16[1024,256]{1,0:T(8,128)(2,1)S(1)} %copy-done), custom_call_target="tpu_custom_call" | custom-call | tf_op jit(solution)/shard_map/prepare/pallas_call | solution.py:369
  49.5 7.1 %all-to-all-done = bf16[128,8,256]{2,1,0:T(8,128)(2,1)S(1)} async-done(((bf16[128,8,256]{2,1,0:T(8,128)(2,1)}), bf16[128,8,256]{2,1,0:T(8,128)(2,1)S(1)}, u32[]{:S(2)}, u32[]{:S(2)}) %all-to-all-start) | async-done | bytes 524320 | tf_op jit(solution)/shard_map/all_to_all | solution.py:359
  56.6 3.3 %aggregate_remote_2.1 = bf16[1040,256]{1,0:T(8,128)(2,1)S(1)} custom-call(s32[4]{0:T(128)S(1)} %and_select_fusion.owner_s, bf16[1024,256]{1,0:T(8,128)(2,1)S(1)} %bitcast.15, bf16[4,16,256]{2,1,0:T(8,128)(2,1)S(1)} %get-tuple-element.17.counts, bf16[4096,1024]{1,0:T(8,128)(2,1)} %get-tuple-element.18.adj_hbm.adj, f32[4096,256]{1,0:T(8,128)} %get-tuple-element.19.local_hbm), custom_call_target="tpu_custom_call" | custom-call | tf_op jit(solution)/shard_map/aggregate_remote_2/pallas_call | solution.py:400
  60.0 3.0 %collective-permute-start.2 = (bf16[1040,256]{1,0:T(8,128)(2,1)S(1)}, bf16[1040,256]{1,0:T(8,128)(2,1)S(1)}, u32[]{:S(2)}, u32[]{:S(2)}) collective-permute-start(bf16[1040,256]{1,0:T(8,128)(2,1)S(1)} %aggregate_remote_2.1), channel_id=1, source_target_pairs={{0,2},{1,3},{2,0},{3,1},{4,6},{5,7},{6,4},{7,5},{8,10},{9,11},{10,... | collective-permute-start | bytes 1597448 | tf_op jit(solution)/shard_map/ppermute | solution.py:396
  63.0 4.7 %aggregate_remote_1_3.1 = (bf16[1040,256]{1,0:T(8,128)(2,1)S(1)}, bf16[1040,256]{1,0:T(8,128)(2,1)S(1)}) custom-call(s32[4]{0:T(128)S(1)} %and_select_fusion.owner_s, bf16[1024,256]{1,0:T(8,128)(2,1)S(1)} %bitcast.16, bf16[4,16,256]{2,1,0:T(8,128)(2,1)S(1)} %get-tuple-element.17.counts, bf16[4096,1024]{1,0:T(8,128)(2,1)} %get-tuple-element.18.adj_hbm.adj, ...), custom_call_target="tpu_custom_call" | custom-call | tf_op jit(solution)/shard_map/aggregate_remote_1_3/pallas_call | solution.py:400
  67.8 3.7 %collective-permute-start = (bf16[1040,256]{1,0:T(8,128)(2,1)S(1)}, bf16[1040,256]{1,0:T(8,128)(2,1)S(1)}, u32[]{:S(2)}, u32[]{:S(2)}) collective-permute-start(bf16[1040,256]{1,0:T(8,128)(2,1)S(1)} %get-tuple-element.21), channel_id=1, source_target_pairs={{0,1},{1,2},{2,3},{3,0},{4,5},{5,6},{6,7},{7,4},{8,9},{9,10},{10,1... | collective-permute-start | bytes 1597448 | tf_op jit(solution)/shard_map/ppermute | solution.py:396
  71.5 0.0 copy-start.10
  71.5 1.9 %collective-permute-start.1 = (bf16[1040,256]{1,0:T(8,128)(2,1)S(1)}, bf16[1040,256]{1,0:T(8,128)(2,1)S(1)}, u32[]{:S(2)}, u32[]{:S(2)}) collective-permute-start(bf16[1040,256]{1,0:T(8,128)(2,1)S(1)} %get-tuple-element.23), channel_id=1, source_target_pairs={{0,3},{1,0},{2,1},{3,2},{4,7},{5,4},{6,5},{7,6},{8,11},{9,8},{10,9... | collective-permute-start | bytes 1597448 | tf_op jit(solution)/shard_map/ppermute | solution.py:396
  73.5 6.8 %adjacency_transposed.1.adj = bf16[8,1024,512]{2,1,0:T(8,128)(2,1)S(1)} custom-call(bf16[4096,1024]{1,0:T(8,128)(2,1)} %get-tuple-element.18.adj_hbm.adj), custom_call_target="tpu_custom_call" | custom-call | tf_op jit(solution)/shard_map/adjacency_transposed/pallas_call | solution.py:427
  80.3 0.0 copy-done.10
  80.3 0.0 copy-start.1
  80.3 0.0 copy-start.6
  80.3 0.0 copy-start.8
  80.3 3.3 %aggregate_remote_0.1.refs_0_.refs_4_ = bf16[1040,256]{1,0:T(8,128)(2,1)S(1)} custom-call(s32[4]{0:T(128)S(1)} %and_select_fusion.owner_s, bf16[1024,256]{1,0:T(8,128)(2,1)S(1)} %bitcast.17, bf16[4,16,256]{2,1,0:T(8,128)(2,1)S(1)} %get-tuple-element.17.counts, bf16[4096,1024]{1,0:T(8,128)(2,1)} %get-tuple-element.18.adj_hbm.adj, ...), custom_call_target="tpu_custom_call" | custom-call | tf_op jit(solution)/shard_map/aggregate_remote_0/pallas_call | solution.py:400
  83.7 0.0 collective-permute-done.2.refs_3_.refs_7_
  83.7 2.8 %collective-permute-done.refs_1_.refs_5_ = bf16[1040,256]{1,0:T(8,128)(2,1)S(1)} collective-permute-done((bf16[1040,256]{1,0:T(8,128)(2,1)S(1)}, bf16[1040,256]{1,0:T(8,128)(2,1)S(1)}, u32[]{:S(2)}, u32[]{:S(2)}) %collective-permute-start) | collective-permute-done | bytes 532512 | tf_op jit(solution)/shard_map/ppermute | solution.py:396
  86.5 1.9 %collective-permute-done.1.refs_2_.refs_6_ = bf16[1040,256]{1,0:T(8,128)(2,1)S(1)} collective-permute-done((bf16[1040,256]{1,0:T(8,128)(2,1)S(1)}, bf16[1040,256]{1,0:T(8,128)(2,1)S(1)}, u32[]{:S(2)}, u32[]{:S(2)}) %collective-permute-start.1) | collective-permute-done | bytes 532512 | tf_op jit(solution)/shard_map/ppermute | solution.py:396
  88.4 0.0 copy-done.1
  88.4 0.0 copy-done.6
  88.4 0.0 copy-done.8
  88.4 4.2 %dense_layer.1 = (bf16[1024,256]{1,0:T(8,128)(2,1)}, bf16[1024,256]{1,0:T(8,128)(2,1)}, bf16[1024,256]{1,0:T(8,128)(2,1)}) custom-call(bf16[1024,256]{1,0:T(8,128)(2,1)S(1)} %copy-done.1, bf16[1024,256]{1,0:T(8,128)(2,1)} %cots.1, bf16[256,256]{1,0:T(8,128)(2,1)S(1)} %copy-done.6, bf16[256,256]{1,0:T(8,128)(2,1)S(1)} %copy-done.8, ...), custom_call_target="tpu_custom_call" | custom-call | tf_op jit(solution)/shard_map/dense_layer/pallas_call | solution.py:443
  92.6 2.6 %collective-permute-start.4 = (bf16[1024,256]{1,0:T(8,128)(2,1)}, bf16[1024,256]{1,0:T(8,128)(2,1)S(1)}, u32[]{:S(2)}, u32[]{:S(2)}) collective-permute-start(bf16[1024,256]{1,0:T(8,128)(2,1)} %get-tuple-element.26.own.p0), channel_id=1, source_target_pairs={{0,1},{1,2},{2,3},{3,0},{4,5},{5,6},{6,7},{7,4},{8,9},{9,10},{10,1... | collective-permute-start | bytes 1572872 | tf_op jit(solution)/shard_map/ppermute | solution.py:396
  95.2 2.7 %collective-permute-start.5 = (bf16[1024,256]{1,0:T(8,128)(2,1)}, bf16[1024,256]{1,0:T(8,128)(2,1)S(1)}, u32[]{:S(2)}, u32[]{:S(2)}) collective-permute-start(bf16[1024,256]{1,0:T(8,128)(2,1)} %get-tuple-element.26.own.p0), channel_id=1, source_target_pairs={{0,3},{1,0},{2,1},{3,2},{4,7},{5,4},{6,5},{7,6},{8,11},{9,8},{10,9... | collective-permute-start | bytes 1572872 | tf_op jit(solution)/shard_map/ppermute | solution.py:396
  97.9 3.5 %collective-permute-start.3 = (bf16[1024,256]{1,0:T(8,128)(2,1)}, bf16[1024,256]{1,0:T(8,128)(2,1)S(1)}, u32[]{:S(2)}, u32[]{:S(2)}) collective-permute-start(bf16[1024,256]{1,0:T(8,128)(2,1)} %get-tuple-element.26.own.p0), channel_id=1, source_target_pairs={{0,2},{1,3},{2,0},{3,1},{4,6},{5,7},{6,4},{7,5},{8,10},{9,11},{10,... | collective-permute-start | bytes 1572872 | tf_op jit(solution)/shard_map/ppermute | solution.py:396
  101.4 5.8 %collective-permute-done.4.left.p1 = bf16[1024,256]{1,0:T(8,128)(2,1)S(1)} collective-permute-done((bf16[1024,256]{1,0:T(8,128)(2,1)}, bf16[1024,256]{1,0:T(8,128)(2,1)S(1)}, u32[]{:S(2)}, u32[]{:S(2)}) %collective-permute-start.4) | collective-permute-done | bytes 524320 | tf_op jit(solution)/shard_map/ppermute | solution.py:396
  107.2 4.3 %collective-permute-done.5.right.p2 = bf16[1024,256]{1,0:T(8,128)(2,1)S(1)} collective-permute-done((bf16[1024,256]{1,0:T(8,128)(2,1)}, bf16[1024,256]{1,0:T(8,128)(2,1)S(1)}, u32[]{:S(2)}, u32[]{:S(2)}) %collective-permute-start.5) | collective-permute-done | bytes 524320 | tf_op jit(solution)/shard_map/ppermute | solution.py:396
  111.5 1.0 copy-done.2
  112.5 2.3 %scatter_near.1.near = f32[1024,256]{1,0:T(8,128)S(1)} custom-call(s32[4]{0:T(128)S(1)} %and_select_fusion.owner_s, bf16[1024,256]{1,0:T(8,128)(2,1)S(1)} %copy-done.2, bf16[1024,256]{1,0:T(8,128)(2,1)S(1)} %collective-permute-done.4.left.p1, bf16[1024,256]{1,0:T(8,128)(2,1)S(1)} %collective-permute-done.5.right.p2, ...), custom_call_target="tpu_custom_call" | custom-call | tf_op jit(solution)/shard_map/scatter_near/pallas_call | solution.py:460
  114.8 0.0 copy-start.9
  114.9 0.0 copy-start.3
  114.9 7.3 %collective-permute-done.3.far.p3 = bf16[1024,256]{1,0:T(8,128)(2,1)S(1)} collective-permute-done((bf16[1024,256]{1,0:T(8,128)(2,1)}, bf16[1024,256]{1,0:T(8,128)(2,1)S(1)}, u32[]{:S(2)}, u32[]{:S(2)}) %collective-permute-start.3) | collective-permute-done | bytes 524320 | tf_op jit(solution)/shard_map/ppermute | solution.py:396
  122.2 2.0 %scatter_far.1 = bf16[1024,256]{1,0:T(8,128)(2,1)} custom-call(s32[4]{0:T(128)S(1)} %and_select_fusion.owner_s, bf16[1024,256]{1,0:T(8,128)(2,1)S(1)} %collective-permute-done.3.far.p3, f32[1024,256]{1,0:T(8,128)S(1)} %scatter_near.1.near, bf16[8,1024,512]{2,1,0:T(8,128)(2,1)S(1)} %adjacency_transposed.1.adj), custom_call_target="tpu_custom_call" | custom-call | tf_op jit(solution)/shard_map/scatter_far/pallas_call | solution.py:460
  124.2 13.5 %all-to-all-start.1 = ((bf16[128,8,256]{2,1,0:T(8,128)(2,1)}), bf16[128,8,256]{2,1,0:T(8,128)(2,1)S(1)}, u32[]{:S(2)}, u32[]{:S(2)}) async-start(bf16[128,8,256]{2,1,0:T(8,128)(2,1)} %bitcast.8), calls=%async_computation.1 | async-start | bytes 1048576 | tf_op jit(solution)/shard_map/all_to_all | solution.py:472
  137.7 0.0 copy-done.9
  137.8 0.1 copy.12
  137.9 0.1 reshape.47
  137.9 0.0 copy-done.3
  138.0 0.0 copy-start.5
  138.0 1.0 copy-done.5
  139.0 1.0 copy-done.7
  140.0 9.7 %scatter_local.1.kept = f32[1024,256]{1,0:T(8,128)S(1)} custom-call(s32[8192]{0:T(1024)S(1)} %get-tuple-element.16.keys_s, s32[1]{0:T(128)} %bitcast.14.active_s, s32[4]{0:T(128)S(1)} %and_select_fusion.owner_s, s32[64,1,128]{2,1,0:T(1,128)S(1)} %bitcast.20, bf16[1024,256]{1,0:T(8,128)(2,1)S(1)} %copy-done.7, bf16[256,256]{1,0:T(8,128)(2,1)S(1)} %copy-done.6, ...), custom_call_target="tpu_custom_call" | custom-call | tf_op jit(solution)/shard_map/scatter_local/pallas_call | solution.py:475
  149.7 21.6 %all-to-all-done.1 = bf16[128,8,256]{2,1,0:T(8,128)(2,1)S(1)} async-done(((bf16[128,8,256]{2,1,0:T(8,128)(2,1)}), bf16[128,8,256]{2,1,0:T(8,128)(2,1)S(1)}, u32[]{:S(2)}, u32[]{:S(2)}) %all-to-all-start.1) | async-done | bytes 524320 | tf_op jit(solution)/shard_map/all_to_all | solution.py:472
  171.3 1.6 combine.1
  (9 shorter events, 0.0 us)
Async XLA Ops:
  3.6 53.1 %all-to-all-start = ((bf16[128,8,256]{2,1,0:T(8,128)(2,1)}), bf16[128,8,256]{2,1,0:T(8,128)(2,1)S(1)}, u32[]{:S(2)}, u32[]{:S(2)}) async-start(bf16[128,8,256]{2,1,0:T(8,128)(2,1)} %pick_rows.1), calls=%async_computation | async-start | bytes 1048576 | tf_op jit(solution)/shard_map/all_to_all | solution.py:359
  31.4 1.0 copy-start
  60.0 23.7 %collective-permute-start.2 = (bf16[1040,256]{1,0:T(8,128)(2,1)S(1)}, bf16[1040,256]{1,0:T(8,128)(2,1)S(1)}, u32[]{:S(2)}, u32[]{:S(2)}) collective-permute-start(bf16[1040,256]{1,0:T(8,128)(2,1)S(1)} %aggregate_remote_2.1), channel_id=1, source_target_pairs={{0,2},{1,3},{2,0},{3,1},{4,6},{5,7},{6,4},{7,5},{8,10},{9,11},{10,... | collective-permute-start | bytes 1597448 | tf_op jit(solution)/shard_map/ppermute | solution.py:396
  67.8 18.7 %collective-permute-start = (bf16[1040,256]{1,0:T(8,128)(2,1)S(1)}, bf16[1040,256]{1,0:T(8,128)(2,1)S(1)}, u32[]{:S(2)}, u32[]{:S(2)}) collective-permute-start(bf16[1040,256]{1,0:T(8,128)(2,1)S(1)} %get-tuple-element.21), channel_id=1, source_target_pairs={{0,1},{1,2},{2,3},{3,0},{4,5},{5,6},{6,7},{7,4},{8,9},{9,10},{10,1... | collective-permute-start | bytes 1597448 | tf_op jit(solution)/shard_map/ppermute | solution.py:396
  71.5 8.8 %copy-start.10 = (bf16[256]{0:T(256)(128)(2,1)S(1)}, bf16[256]{0:T(256)(128)(2,1)}, u32[]{:S(2)}) copy-start(bf16[256]{0:T(256)(128)(2,1)} %param.13) | copy-start | bytes 1540
  71.5 16.9 %collective-permute-start.1 = (bf16[1040,256]{1,0:T(8,128)(2,1)S(1)}, bf16[1040,256]{1,0:T(8,128)(2,1)S(1)}, u32[]{:S(2)}, u32[]{:S(2)}) collective-permute-start(bf16[1040,256]{1,0:T(8,128)(2,1)S(1)} %get-tuple-element.23), channel_id=1, source_target_pairs={{0,3},{1,0},{2,1},{3,2},{4,7},{5,4},{6,5},{7,6},{8,11},{9,8},{10,9... | collective-permute-start | bytes 1597448 | tf_op jit(solution)/shard_map/ppermute | solution.py:396
  80.3 8.1 %copy-start.1 = (bf16[1024,256]{1,0:T(8,128)(2,1)S(1)}, bf16[1024,256]{1,0:T(8,128)(2,1)}, u32[]{:S(2)}) copy-start(bf16[1024,256]{1,0:T(8,128)(2,1)} %feats.1) | copy-start | bytes 1572868
  80.3 8.1 %copy-start.6 = (bf16[256,256]{1,0:T(8,128)(2,1)S(1)}, bf16[256,256]{1,0:T(8,128)(2,1)}, u32[]{:S(2)}) copy-start(bf16[256,256]{1,0:T(8,128)(2,1)} %w_self.3) | copy-start | bytes 393220
  80.3 8.1 %copy-start.8 = (bf16[256,256]{1,0:T(8,128)(2,1)S(1)}, bf16[256,256]{1,0:T(8,128)(2,1)}, u32[]{:S(2)}) copy-start(bf16[256,256]{1,0:T(8,128)(2,1)} %w_neigh.1) | copy-start | bytes 393220
  92.6 14.5 %collective-permute-start.4 = (bf16[1024,256]{1,0:T(8,128)(2,1)}, bf16[1024,256]{1,0:T(8,128)(2,1)S(1)}, u32[]{:S(2)}, u32[]{:S(2)}) collective-permute-start(bf16[1024,256]{1,0:T(8,128)(2,1)} %get-tuple-element.26.own.p0), channel_id=1, source_target_pairs={{0,1},{1,2},{2,3},{3,0},{4,5},{5,6},{6,7},{7,4},{8,9},{9,10},{10,1... | collective-permute-start | bytes 1572872 | tf_op jit(solution)/shard_map/ppermute | solution.py:396
  95.2 16.3 %collective-permute-start.5 = (bf16[1024,256]{1,0:T(8,128)(2,1)}, bf16[1024,256]{1,0:T(8,128)(2,1)S(1)}, u32[]{:S(2)}, u32[]{:S(2)}) collective-permute-start(bf16[1024,256]{1,0:T(8,128)(2,1)} %get-tuple-element.26.own.p0), channel_id=1, source_target_pairs={{0,3},{1,0},{2,1},{3,2},{4,7},{5,4},{6,5},{7,6},{8,11},{9,8},{10,9... | collective-permute-start | bytes 1572872 | tf_op jit(solution)/shard_map/ppermute | solution.py:396
  97.9 24.2 %collective-permute-start.3 = (bf16[1024,256]{1,0:T(8,128)(2,1)}, bf16[1024,256]{1,0:T(8,128)(2,1)S(1)}, u32[]{:S(2)}, u32[]{:S(2)}) collective-permute-start(bf16[1024,256]{1,0:T(8,128)(2,1)} %get-tuple-element.26.own.p0), channel_id=1, source_target_pairs={{0,2},{1,3},{2,0},{3,1},{4,6},{5,7},{6,4},{7,5},{8,10},{9,11},{10,... | collective-permute-start | bytes 1572872 | tf_op jit(solution)/shard_map/ppermute | solution.py:396
  111.5 1.0 copy-start.2
  114.8 22.9 %copy-start.9 = (s32[1,1,128,8]{2,3,1,0:T(8,128)S(1)}, s32[1,1,128,8]{2,3,1,0:T(8,128)}, u32[]{:S(2)}) copy-start(s32[1,1,128,8]{2,3,1,0:T(8,128)} %param.14) | copy-start | bytes 12292
  114.9 23.1 %copy-start.3 = (bf16[1024,256]{1,0:T(8,128)(2,1)S(1)}, bf16[1024,256]{1,0:T(8,128)(2,1)}, u32[]{:S(2)}) copy-start(bf16[1024,256]{1,0:T(8,128)(2,1)} %get-tuple-element.26.own.p0) | copy-start | bytes 1572868
  122.2 2.1 %copy-start.4 = (bf16[1024,256]{1,0:T(8,128)(2,1)}, bf16[1024,256]{1,0:T(8,128)(2,1)S(1)}, u32[]{:S(2)}) copy-start(bf16[1024,256]{1,0:T(8,128)(2,1)S(1)} %collective-permute-done.3.far.p3) | copy-start | bytes 1572868
  124.2 47.1 %all-to-all-start.1 = ((bf16[128,8,256]{2,1,0:T(8,128)(2,1)}), bf16[128,8,256]{2,1,0:T(8,128)(2,1)S(1)}, u32[]{:S(2)}, u32[]{:S(2)}) async-start(bf16[128,8,256]{2,1,0:T(8,128)(2,1)} %bitcast.8), calls=%async_computation.1 | async-start | bytes 1048576 | tf_op jit(solution)/shard_map/all_to_all | solution.py:472
  138.0 1.0 copy-start.5
  139.0 1.0 copy-start.7

commit v4 on v3

--- a/solution.py
+++ b/solution.py
@@ -15,6 +15,7 @@
 UNROLL = 4
 SUB = 256
 WIN = 384
+SPAN = 512
 PADDED = PART + WIN
 CNT = 16
 LOCAL_END = 1 << 22
@@ -101,37 +102,29 @@
             lax.fori_loop(1, item[1], window, 0)
 
 
-def build_adjacency(keys_s, keys_v, adj, lo, hi):
-    def tile(t, carry):
+def tiles(lo, hi, body):
+    first = lo // SUB
+    count = (hi + SUB - 1) // SUB - first
+
+    def wide(t, carry):
+        body(first + t * UNROLL, UNROLL)
+        return carry
+
+    def narrow(t, carry):
+        body(first + (count // UNROLL) * UNROLL + t, 1)
+        return carry
+
+    lax.fori_loop(0, count // UNROLL, wide, 0)
+    lax.fori_loop(0, count % UNROLL, narrow, 0)
+
+
+def aggregate(keys_s, keys_v, table, acc, lo, hi, remote):
+    def tile(first_sub, unroll):
+        rows = [keys_v[2 * first_sub + j] for j in range(2 * unroll)]
+        got = jnp.dot(pick_of(rows, remote), table[...], preferred_element_type=F32).astype(BF16)
         todo = []
-        for u in range(UNROLL):
-            rows = [keys_v[2 * UNROLL * t + 2 * u + j] for j in range(2)]
-            base, count = sub_range(keys_s, (t * UNROLL + u) * SUB, lo, hi)
-            base = pl.multiple_of(base, 16)
-            targets = [target_of(r) for r in rows]
-            first = jnp.dot(place_of(targets, base), pick_of(rows, 1), preferred_element_type=F32).astype(BF16)
-            todo.append((base, count, targets, rows, first))
-        for base, count, targets, rows, first in todo:
-            adj[pl.ds(base, WIN), :] += first
-
-        def run(item, off):
-            more = jnp.dot(place_of(item[2], off), pick_of(item[3], 1), preferred_element_type=F32)
-            adj[pl.ds(off, WIN), :] += more.astype(BF16)
-
-        further_windows(todo, run)
-        return carry
-
-    size = SUB * UNROLL
-    lax.fori_loop(lo // size, (hi + size - 1) // size, tile, 0)
-
-
-def aggregate_local(keys_s, keys_v, table, acc, lo, hi):
-    def tile(t, carry):
-        rows = [keys_v[2 * UNROLL * t + j] for j in range(2 * UNROLL)]
-        got = jnp.dot(pick_of(rows, 0), table[...], preferred_element_type=F32).astype(BF16)
-        todo = []
-        for u in range(UNROLL):
-            base, count = sub_range(keys_s, (t * UNROLL + u) * SUB, lo, hi)
+        for u in range(unroll):
+            base, count = sub_range(keys_s, (first_sub + u) * SUB, lo, hi)
             base = pl.multiple_of(base, 16)
             targets = [target_of(r) for r in rows[2 * u : 2 * u + 2]]
             piece = got[SUB * u : SUB * u + SUB]
@@ -144,68 +137,93 @@
             acc[pl.ds(off, WIN), :] += jnp.dot(place_of(item[2], off), item[3], preferred_element_type=F32)
 
         further_windows(todo, run)
-        return carry
-
-    size = SUB * UNROLL
-    lax.fori_loop(lo // size, (hi + size - 1) // size, tile, 0)
-
-
-def prepare_kernel(keys_s, active_s, keys_v, table, adj_out, local_out, counts, adj, acc, sems):
+
+    tiles(lo, hi, tile)
+
+
+def prepare_kernel(keys_s, active_s, keys_v, table_hbm, local_out, counts, table, acc, sems):
+    load = pltpu.make_async_copy(table_hbm, table, sems.at[0])
+    load.start()
+    acc[...] = jnp.zeros_like(acc)
     boundary = local_edges(keys_s)
-    adj[...] = jnp.zeros_like(adj)
-    build_adjacency(keys_s, keys_v, adj, boundary, active_s[0] * 128)
-    save_adj = pltpu.make_async_copy(adj.at[pl.ds(0, PART), :], adj_out, sems.at[0])
-    save_adj.start()
-    acc[...] = jnp.zeros_like(acc)
-    aggregate_local(keys_s, keys_v, table, acc, 0, boundary)
-    save_acc = pltpu.make_async_copy(acc.at[pl.ds(0, PART), :], local_out, sems.at[1])
-    save_acc.start()
+    load.wait()
+    aggregate(keys_s, keys_v, table, acc, 0, boundary, 0)
+    save = pltpu.make_async_copy(acc.at[pl.ds(0, PART), :], local_out, sems.at[1])
+    save.start()
 
     def tally(t, total):
-        keys = [keys_v[8 * t + j] for j in range(8)]
+        keys = [keys_v[32 * t + j] for j in range(32)]
         high = jnp.concatenate(
             [one_hot((iota((32, 128), 0) == (target_of(k) >> 7)) & (k < ACTIVE_END)) for k in keys], axis=1
         )
         low = jnp.concatenate([one_hot(iota((128, 128), 0) == (target_of(k) & 127)) for k in keys], axis=1)
         return total + lax.dot_general(high, low, (((1,), (1,)), ((), ())), preferred_element_type=F32)
 
-    total = lax.fori_loop(0, EDGES // 1024, tally, jnp.zeros((32, 128), F32))
+    total = lax.fori_loop(0, EDGES // 4096, tally, jnp.zeros((32, 128), F32))
     upper = jnp.floor(total * (1.0 / 256.0))
     lower = total - upper * 256.0
     for s in range(4):
         both = jnp.concatenate([upper[8 * s : 8 * s + 8], lower[8 * s : 8 * s + 8]], axis=1)
         counts[s] = jnp.concatenate([both, jnp.zeros((8, WIDTH), F32)], axis=0).astype(BF16)
-    save_adj.wait()
-    save_acc.wait()
-
-
-def transpose_kernel(adj, out):
-    out[0] = jnp.transpose(adj[...])
-
-
-def forward_remote_kernel(shifts, owner_s, table, counts, adj_hbm, local_hbm, *refs):
-    outs, (adj, local_part, sems) = refs[:-3], refs[-3:]
-    halves = ROWS // CHUNK
-    loads = []
-    for n in range(len(outs)):
-        for h in range(halves):
-            rows = pl.ds(pl.multiple_of(owner_s[shifts[n]] * ROWS + h * CHUNK, CHUNK), CHUNK)
-            i = n * halves + h
-            pair = (
-                pltpu.make_async_copy(adj_hbm.at[rows, :], adj.at[i], sems.at[0, i]),
-                pltpu.make_async_copy(local_hbm.at[rows, :], local_part.at[i], sems.at[1, i]),
-            )
-            for copy in pair:
-                copy.start()
-            loads.append(pair)
-    for n, out in enumerate(outs):
-        out[ROWS:, :] = counts[owner_s[shifts[n]]]
-        for h in range(halves):
-            i = n * halves + h
-            for copy in loads[i]:
-                copy.wait()
-            total = local_part[i] + jnp.dot(adj[i], table[...], preferred_element_type=F32)
-            out[h * CHUNK : h * CHUNK + CHUNK, :] = total.astype(BF16)
+    save.wait()
+
+
+def forward_remote_kernel(keys_s, active_s, owner_s, keys_v, table, counts, local_hbm, *refs):
+    outs, (local_part, acc, sem) = refs[:4], refs[4:]
+    load = pltpu.make_async_copy(local_hbm, local_part, sem)
+    load.start()
+    acc[...] = jnp.zeros_like(acc)
+    aggregate(keys_s, keys_v, table, acc, local_edges(keys_s), active_s[0] * 128, 1)
+    load.wait()
+    for shift, out in enumerate(outs):
+        owner = owner_s[shift]
+        rows = pl.ds(pl.multiple_of(owner * ROWS, ROWS), ROWS)
+        out[:ROWS, :] = (acc[rows, :] + local_part[rows, :]).astype(BF16)
+        out[ROWS:, :] = counts[owner]
+
+
+def transposed_kernel(keys_s, active_s, keys_v, adj):
+    adj[...] = jnp.zeros_like(adj)
+    lo, hi = local_edges(keys_s), active_s[0] * 128
+    blocks = SPAN // 128
+
+    def product(rows, block):
+        place = jnp.concatenate([one_hot(iota((ROWS, 128), 0) == source_of(r, 1)) for r in rows], axis=1)
+        match = jnp.concatenate(
+            [one_hot(iota((SPAN, 128), 0) + block * 128 == target_of(r)) for r in rows], axis=1
+        )
+        return lax.dot_general(place, match, (((1,), (1,)), ((), ())), preferred_element_type=F32).astype(BF16)
+
+    def add(block, value):
+        for k in range(blocks):
+            adj[block + k] += value[:, 128 * k : 128 * k + 128]
+
+    def tile(first_sub, unroll):
+        todo = []
+        for u in range(unroll):
+            first = jnp.maximum((first_sub + u) * SUB, lo)
+            last = jnp.minimum((first_sub + u) * SUB + SUB - 1, hi - 1)
+            block = target_of(keys_s[first]) >> 7
+            final = target_of(keys_s[last]) >> 7
+            rows = [keys_v[2 * (first_sub + u) + j] for j in range(2)]
+            todo.append((block, (final - block) // blocks + 1, rows, product(rows, block)))
+        for block, count, rows, value in todo:
+            add(block, value)
+        most = todo[0][1]
+        for item in todo[1:]:
+            most = jnp.maximum(most, item[1])
+
+        @pl.when(most > 1)
+        def _():
+            for block, count, rows, value in todo:
+
+                def window(w, c):
+                    add(block + w * blocks, product(rows, block + w * blocks))
+                    return c
+
+                lax.fori_loop(1, count, window, 0)
+
+    tiles(lo, hi, tile)
 
 
 def pick_kernel(senders, table, out, acc):
@@ -302,12 +320,12 @@
 
 
 def piece_sum(owner_s, pieces, adj, start):
-    halves = ROWS // CHUNK
     total = start
     for shift, piece in pieces:
-        for h in range(halves):
-            rows = piece[h * CHUNK : h * CHUNK + CHUNK, :]
-            part = jnp.dot(adj[owner_s[shift] * halves + h], rows, preferred_element_type=F32)
+        for h in range(ROWS // SUB):
+            block = owner_s[shift] * (ROWS // 128) + 2 * h
+            both = jnp.concatenate([adj[block], adj[block + 1]], axis=1)
+            part = jnp.dot(both, piece[h * SUB : h * SUB + SUB, :], preferred_element_type=F32)
             total = part if total is None else total + part
     return total
 
@@ -366,75 +384,58 @@
     keys_s = lax.sort(jnp.where(live, keys, ACTIVE_END))
     keys_v = keys_s.reshape(EDGES // 128, 1, 128)
 
-    adj, before, counts = pl.pallas_call(
+    before, counts = pl.pallas_call(
         prepare_kernel,
         grid_spec=pltpu.PrefetchScalarGridSpec(
             num_scalar_prefetch=2,
             grid=(),
-            in_specs=[VMEM, VMEM],
-            out_specs=(HBM, HBM, VMEM),
+            in_specs=[VMEM, HBM],
+            out_specs=(HBM, VMEM),
             scratch_shapes=[
-                pltpu.VMEM((PADDED, ROWS), BF16),
+                pltpu.VMEM((ROWS, WIDTH), BF16),
                 pltpu.VMEM((PADDED, WIDTH), F32),
                 pltpu.SemaphoreType.DMA((2,)),
             ],
         ),
-        out_shape=(
-            pltpu.HBM((PART, ROWS), BF16),
-            pltpu.HBM((PART, WIDTH), F32),
-            shape((4, CNT, WIDTH), BF16),
-        ),
-        compiler_params=params(30),
+        out_shape=(pltpu.HBM((PART, WIDTH), F32), shape((4, CNT, WIDTH), BF16)),
+        compiler_params=params(20),
         name="prepare",
-    )(keys_s, active, keys_v, features)
-    chunks = PART // CHUNK
+    )(keys_s, active, keys_v, in_hbm(features))
     rank = lax.axis_index("src")
-
     order = lax.optimization_barrier((rank + jnp.arange(4, dtype=jnp.int32)) % 4)
 
     def shifted(x, k):
         return lax.ppermute(x, "src", [(j, (j + k) % 4) for j in range(4)])
 
-    def partials(table, *shifts):
-        count = len(shifts)
-        return pl.pallas_call(
-            functools.partial(forward_remote_kernel, shifts),
-            grid_spec=pltpu.PrefetchScalarGridSpec(
-                num_scalar_prefetch=1,
-                grid=(),
-                in_specs=[VMEM, VMEM, HBM, HBM],
-                out_specs=[VMEM] * count,
-                scratch_shapes=[
-                    pltpu.VMEM((2 * count, CHUNK, ROWS), BF16),
-                    pltpu.VMEM((2 * count, CHUNK, WIDTH), F32),
-                    pltpu.SemaphoreType.DMA((2, 2 * count)),
-                ],
-            ),
-            out_shape=[shape((ROWS + CNT, WIDTH), BF16)] * count,
-            compiler_params=params(12),
-            name="aggregate_remote_" + "_".join(str(k) for k in shifts),
-        )(order, table, counts, in_hbm(adj), in_hbm(before))
-
-    (partial_far,) = partials(remote, 2)
+    partial_own, partial_next, partial_far, partial_prev = pl.pallas_call(
+        forward_remote_kernel,
+        grid_spec=pltpu.PrefetchScalarGridSpec(
+            num_scalar_prefetch=3,
+            grid=(),
+            in_specs=[VMEM, VMEM, VMEM, HBM],
+            out_specs=[VMEM] * 4,
+            scratch_shapes=[
+                pltpu.VMEM((PART, WIDTH), F32),
+                pltpu.VMEM((PADDED, WIDTH), F32),
+                pltpu.SemaphoreType.DMA,
+            ],
+        ),
+        out_shape=[shape((ROWS + CNT, WIDTH), BF16)] * 4,
+        compiler_params=params(24),
+        name="aggregate_remote",
+    )(keys_s, active, order, keys_v, remote, counts, in_hbm(before))
     from_far = shifted(partial_far, 2)
-    remote, partial_far = lax.optimization_barrier((remote, partial_far))
-    partial_next, partial_prev = partials(remote, 1, 3)
     from_prev = shifted(partial_next, 1)
     from_next = shifted(partial_prev, 3)
-    remote, partial = lax.optimization_barrier((remote, partial_next))
-    (partial_own,) = partials(remote, 0)
-    adj, partial = lax.optimization_barrier((adj, partial))
+    keys_s, partial_own = lax.optimization_barrier((keys_s, partial_own))
     adj_t = pl.pallas_call(
-        transpose_kernel,
-        grid=(chunks,),
-        in_specs=[pl.BlockSpec((CHUNK, ROWS), lambda i: (i, 0))],
-        out_specs=pl.BlockSpec((1, ROWS, CHUNK), lambda i: (i, 0, 0)),
-        out_shape=shape((chunks, ROWS, CHUNK), BF16),
+        transposed_kernel,
+        grid_spec=pltpu.PrefetchScalarGridSpec(num_scalar_prefetch=2, grid=(), in_specs=[VMEM], out_specs=VMEM),
+        out_shape=shape(((PART + SPAN) // 128, ROWS, 128), BF16),
         compiler_params=params(10),
         name="adjacency_transposed",
-    )(in_hbm(adj))
-    adj_t, from_far = lax.optimization_barrier((adj_t, from_far))
-
+    )(keys_s, active, keys_v)
+    adj_t, from_next = lax.optimization_barrier((adj_t, from_next))
     block = ROWS // 4
     tile = pl.BlockSpec((block, WIDTH), lambda i: (i, 0))
     whole = pl.BlockSpec((WIDTH, WIDTH), lambda i: (0, 0))

time: 174 us -> 180 us (1.034)
  waiting for transfers between devices: 50.8 us -> 65.8 us
  Pallas kernels: 58.1 us -> 46.7 us
  starting transfers between devices: 50.5 us -> 53.5 us
    all_to_all x1, waiting for transfers between devices: 7.12 us -> 15.4 us  [local(): lax.all_to_all(picked, 'dom', split_axis=0, concat_axis=0, tiled=True)]
    pallas_call x1, Pallas kernels: 17.1 us -> 9.9 us  [local(): pl.pallas_call(prepare_kernel, grid_spec=pltpu.PrefetchScalarGridSpec(num...]
    ppermute x6, waiting for transfers between devices: 22 us -> 27.9 us  [shifted(): return lax.ppermute(x, 'src', [(j, (j + k) % 4) for j in range(4)])]
    pallas_call x4 -> x2, Pallas kernels: 18.2 us -> 14.8 us  [the longest x1 7.62 us: local(): pl.pallas_call(transposed_kernel, grid_spec=pltpu.PrefetchScalarGridSpec(...]
    ppermute x6, starting transfers between devices: 17.5 us -> 19.8 us  [shifted(): return lax.ppermute(x, 'src', [(j, (j + k) % 4) for j in range(4)])]
    unnamed x23 -> x19, local copies, waits for them, and re-layouts: 4.3 us -> 3.25 us
  transfers between devices with their start and end apart: 8 -> 8, of which waited for: 7 -> 6; matrix products, arithmetic and copies ran while one was open for 5% -> 5% of each run, Pallas kernels for 25% -> 16%
where the time goes in v4:
time: 180 us; the launch traced here: 179 us
  waiting for transfers between devices  65.8 us (37%)
  starting transfers between devices  53.5 us (30%)
  Pallas kernels  46.7 us (26%)
  other arithmetic  7.63 us (4%)
  local copies, waits for them, and re-layouts  4.01 us (2%)
    ppermute x6, waiting for transfers between devices, shifted(): return lax.ppermute(x, 'src', [(j, (j + k) % 4) for j in range(4)])  27.9 us
    all_to_all x1, waiting for transfers between devices, local(): lax.all_to_all(outgoing.reshape(peers, capacity, WIDTH), 'dom', split_axi...  22.6 us
    ppermute x6, starting transfers between devices, shifted(): return lax.ppermute(x, 'src', [(j, (j + k) % 4) for j in range(4)])  19.8 us
    all_to_all x1, starting transfers between devices, local(): lax.all_to_all(picked, 'dom', split_axis=0, concat_axis=0, tiled=True)  19.5 us
    all_to_all x1, waiting for transfers between devices, local(): lax.all_to_all(picked, 'dom', split_axis=0, concat_axis=0, tiled=True)  15.4 us
    all_to_all x1, starting transfers between devices, local(): lax.all_to_all(outgoing.reshape(peers, capacity, WIDTH), 'dom', split_axi...  14.2 us
    pallas_call x1, Pallas kernels, local(): pl.pallas_call(prepare_kernel, grid_spec=pltpu.PrefetchScalarGridSpec(num...  9.9 us
    pallas_call x1, Pallas kernels, local(): pl.pallas_call(backward_local_kernel, grid_spec=pltpu.PrefetchScalarGridS...  8.72 us
  transfers between devices with their start and end apart: 8, of which 6 were waited for; matrix products, arithmetic and copies ran while one was open for 5% of the time, Pallas kernels for 16%

profile of v4, /device:TPU:39, one launch (start us, length us, event | category | flops | bytes accessed | tf_op | source)
XLA Modules:
  0.0 179.3 jit_solution(17978384327112936548)
XLA Ops:
  0.6 0.0 copy-start
  0.6 0.0 copy-start.5
  0.7 0.0 copy-start.7
  0.7 3.0 %pick_rows.1 = bf16[128,8,256]{2,1,0:T(8,128)(2,1)} custom-call(s32[8,128]{1,0:T(8,128)} %bitcast.25, bf16[1024,256]{1,0:T(8,128)(2,1)} %feats.1), custom_call_target="tpu_custom_call" | custom-call | tf_op jit(solution)/shard_map/pick_rows/pallas_call | solution.py:364
  3.7 19.5 %all-to-all-start = ((bf16[128,8,256]{2,1,0:T(8,128)(2,1)}), bf16[128,8,256]{2,1,0:T(8,128)(2,1)S(1)}, u32[]{:S(2)}, u32[]{:S(2)}) async-start(bf16[128,8,256]{2,1,0:T(8,128)(2,1)} %pick_rows.1), calls=%async_computation | async-start | bytes 1048576 | tf_op jit(solution)/shard_map/all_to_all | solution.py:377
  23.8 0.8 and_add_fusion
  24.7 6.8 %sort.10 = (s32[8192]{0:T(1024)S(1)}, s32[8192]{0:T(1024)}) sort(s32[8192]{0:T(1024)S(1)} %fusion, s32[8192]{0:T(1024)S(1)} %iota.10), dimensions={0}, to_apply=%region_0.1 | sort | flops 106496 | bytes 131072 | tf_op jit(solution)/shard_map/sort | solution.py:384
  31.5 9.9 %prepare.1 = (f32[4096,256]{1,0:T(8,128)}, bf16[4,16,256]{2,1,0:T(8,128)(2,1)S(1)}) custom-call(s32[8192]{0:T(1024)S(1)} %get-tuple-element.23.keys_s, s32[1]{0:T(128)} %bitcast.13.active_s, s32[64,1,128]{2,1,0:T(1,128)S(1)} %bitcast.17, bf16[1024,256]{1,0:T(8,128)(2,1)} %feats.1), custom_call_target="tpu_custom_call" | custom-call | tf_op jit(solution)/shard_map/prepare/pallas_call | solution.py:387
  41.4 15.4 %all-to-all-done = bf16[128,8,256]{2,1,0:T(8,128)(2,1)S(1)} async-done(((bf16[128,8,256]{2,1,0:T(8,128)(2,1)}), bf16[128,8,256]{2,1,0:T(8,128)(2,1)S(1)}, u32[]{:S(2)}, u32[]{:S(2)}) %all-to-all-start) | async-done | bytes 524320 | tf_op jit(solution)/shard_map/all_to_all | solution.py:377
  56.7 7.2 %aggregate_remote.1 = (bf16[1040,256]{1,0:T(8,128)(2,1)S(1)}, bf16[1040,256]{1,0:T(8,128)(2,1)S(1)}, bf16[1040,256]{1,0:T(8,128)(2,1)S(1)}, bf16[1040,256]{1,0:T(8,128)(2,1)S(1)}) custom-call(s32[8192]{0:T(1024)S(1)} %get-tuple-element.23.keys_s, s32[1]{0:T(128)} %bitcast.14.active_s, s32[4]{0:T(128)S(1)} %and_select_fusion.owner_s, ...), custom_call_target="tpu_custom_call" | custom-call | tf_op jit(solution)/shard_map/aggregate_remote/pallas_call | solution.py:410
  64.0 2.9 %collective-permute-start.1 = (bf16[1040,256]{1,0:T(8,128)(2,1)S(1)}, bf16[1040,256]{1,0:T(8,128)(2,1)S(1)}, u32[]{:S(2)}, u32[]{:S(2)}) collective-permute-start(bf16[1040,256]{1,0:T(8,128)(2,1)S(1)} %get-tuple-element.24), channel_id=1, source_target_pairs={{0,3},{1,0},{2,1},{3,2},{4,7},{5,4},{6,5},{7,6},{8,11},{9,8},{10,9... | collective-permute-start | bytes 1597448 | tf_op jit(solution)/shard_map/ppermute | solution.py:408
  66.9 3.6 %collective-permute-start = (bf16[1040,256]{1,0:T(8,128)(2,1)S(1)}, bf16[1040,256]{1,0:T(8,128)(2,1)S(1)}, u32[]{:S(2)}, u32[]{:S(2)}) collective-permute-start(bf16[1040,256]{1,0:T(8,128)(2,1)S(1)} %get-tuple-element.22), channel_id=1, source_target_pairs={{0,1},{1,2},{2,3},{3,0},{4,5},{5,6},{6,7},{7,4},{8,9},{9,10},{10,1... | collective-permute-start | bytes 1597448 | tf_op jit(solution)/shard_map/ppermute | solution.py:408
  70.5 2.0 %collective-permute-start.2 = (bf16[1040,256]{1,0:T(8,128)(2,1)S(1)}, bf16[1040,256]{1,0:T(8,128)(2,1)S(1)}, u32[]{:S(2)}, u32[]{:S(2)}) collective-permute-start(bf16[1040,256]{1,0:T(8,128)(2,1)S(1)} %get-tuple-element.26), channel_id=1, source_target_pairs={{0,2},{1,3},{2,0},{3,1},{4,6},{5,7},{6,4},{7,5},{8,10},{9,11},{10,... | collective-permute-start | bytes 1597448 | tf_op jit(solution)/shard_map/ppermute | solution.py:408
  72.5 0.7 reshape.42.bias
  73.2 7.6 %adjacency_transposed.1.adj = bf16[36,1024,128]{2,1,0:T(8,128)(2,1)S(1)} custom-call(s32[8192]{0:T(1024)S(1)} %get-tuple-element.23.keys_s, s32[1]{0:T(128)} %bitcast.15.active_s, s32[64,1,128]{2,1,0:T(1,128)S(1)} %bitcast.19), custom_call_target="tpu_custom_call" | custom-call | tf_op jit(solution)/shard_map/adjacency_transposed/pallas_call | solution.py:431
  80.8 11.1 %collective-permute-done.1.refs_2_.refs_6_ = bf16[1040,256]{1,0:T(8,128)(2,1)S(1)} collective-permute-done((bf16[1040,256]{1,0:T(8,128)(2,1)S(1)}, bf16[1040,256]{1,0:T(8,128)(2,1)S(1)}, u32[]{:S(2)}, u32[]{:S(2)}) %collective-permute-start.1) | collective-permute-done | bytes 532512 | tf_op jit(solution)/shard_map/ppermute | solution.py:408
  91.9 0.0 collective-permute-done.refs_1_.refs_5_
  91.9 0.0 collective-permute-done.2.refs_3_.refs_7_
  91.9 0.0 copy-done
  91.9 0.0 copy-done.5
  91.9 0.0 copy-done.7
  91.9 0.0 copy-start.8
  91.9 4.2 %dense_layer.1 = (bf16[1024,256]{1,0:T(8,128)(2,1)}, bf16[1024,256]{1,0:T(8,128)(2,1)}, bf16[1024,256]{1,0:T(8,128)(2,1)}) custom-call(bf16[1024,256]{1,0:T(8,128)(2,1)S(1)} %copy-done, bf16[1024,256]{1,0:T(8,128)(2,1)} %cots.1, bf16[256,256]{1,0:T(8,128)(2,1)S(1)} %copy-done.5, bf16[256,256]{1,0:T(8,128)(2,1)S(1)} %copy-done.7, ...), custom_call_target="tpu_custom_call" | custom-call | tf_op jit(solution)/shard_map/dense_layer/pallas_call | solution.py:444
  96.2 6.2 %collective-permute-start.4 = (bf16[1024,256]{1,0:T(8,128)(2,1)}, bf16[1024,256]{1,0:T(8,128)(2,1)S(1)}, u32[]{:S(2)}, u32[]{:S(2)}) collective-permute-start(bf16[1024,256]{1,0:T(8,128)(2,1)} %get-tuple-element.28.own.p0), channel_id=1, source_target_pairs={{0,1},{1,2},{2,3},{3,0},{4,5},{5,6},{6,7},{7,4},{8,9},{9,10},{10,1... | collective-permute-start | bytes 1572872 | tf_op jit(solution)/shard_map/ppermute | solution.py:408
  102.4 1.9 %collective-permute-start.5 = (bf16[1024,256]{1,0:T(8,128)(2,1)}, bf16[1024,256]{1,0:T(8,128)(2,1)S(1)}, u32[]{:S(2)}, u32[]{:S(2)}) collective-permute-start(bf16[1024,256]{1,0:T(8,128)(2,1)} %get-tuple-element.28.own.p0), channel_id=1, source_target_pairs={{0,3},{1,0},{2,1},{3,2},{4,7},{5,4},{6,5},{7,6},{8,11},{9,8},{10,9... | collective-permute-start | bytes 1572872 | tf_op jit(solution)/shard_map/ppermute | solution.py:408
  104.3 3.1 %collective-permute-start.3 = (bf16[1024,256]{1,0:T(8,128)(2,1)}, bf16[1024,256]{1,0:T(8,128)(2,1)S(1)}, u32[]{:S(2)}, u32[]{:S(2)}) collective-permute-start(bf16[1024,256]{1,0:T(8,128)(2,1)} %get-tuple-element.28.own.p0), channel_id=1, source_target_pairs={{0,2},{1,3},{2,0},{3,1},{4,6},{5,7},{6,4},{7,5},{8,10},{9,11},{10,... | collective-permute-start | bytes 1572872 | tf_op jit(solution)/shard_map/ppermute | solution.py:408
  107.4 6.7 %collective-permute-done.4.left.p1 = bf16[1024,256]{1,0:T(8,128)(2,1)S(1)} collective-permute-done((bf16[1024,256]{1,0:T(8,128)(2,1)}, bf16[1024,256]{1,0:T(8,128)(2,1)S(1)}, u32[]{:S(2)}, u32[]{:S(2)}) %collective-permute-start.4) | collective-permute-done | bytes 524320 | tf_op jit(solution)/shard_map/ppermute | solution.py:408
  114.2 4.6 %collective-permute-done.5.right.p2 = bf16[1024,256]{1,0:T(8,128)(2,1)S(1)} collective-permute-done((bf16[1024,256]{1,0:T(8,128)(2,1)}, bf16[1024,256]{1,0:T(8,128)(2,1)S(1)}, u32[]{:S(2)}, u32[]{:S(2)}) %collective-permute-start.5) | collective-permute-done | bytes 524320 | tf_op jit(solution)/shard_map/ppermute | solution.py:408
  118.7 0.0 copy-start.1
  118.7 1.0 copy-done.1
  119.8 0.0 copy-start.2
  119.8 2.3 %scatter_near.1.near = f32[1024,256]{1,0:T(8,128)S(1)} custom-call(s32[4]{0:T(128)S(1)} %and_select_fusion.owner_s, bf16[1024,256]{1,0:T(8,128)(2,1)S(1)} %copy-done.1, bf16[1024,256]{1,0:T(8,128)(2,1)S(1)} %collective-permute-done.4.left.p1, bf16[1024,256]{1,0:T(8,128)(2,1)S(1)} %collective-permute-done.5.right.p2, ...), custom_call_target="tpu_custom_call" | custom-call | tf_op jit(solution)/shard_map/scatter_near/pallas_call | solution.py:461
  122.1 5.5 %collective-permute-done.3.far.p3 = bf16[1024,256]{1,0:T(8,128)(2,1)S(1)} collective-permute-done((bf16[1024,256]{1,0:T(8,128)(2,1)}, bf16[1024,256]{1,0:T(8,128)(2,1)S(1)}, u32[]{:S(2)}, u32[]{:S(2)}) %collective-permute-start.3) | collective-permute-done | bytes 524320 | tf_op jit(solution)/shard_map/ppermute | solution.py:408
  127.6 0.0 copy-start.3
  127.6 2.1 %scatter_far.1 = bf16[1024,256]{1,0:T(8,128)(2,1)} custom-call(s32[4]{0:T(128)S(1)} %and_select_fusion.owner_s, bf16[1024,256]{1,0:T(8,128)(2,1)S(1)} %collective-permute-done.3.far.p3, f32[1024,256]{1,0:T(8,128)S(1)} %scatter_near.1.near, bf16[36,1024,128]{2,1,0:T(8,128)(2,1)S(1)} %adjacency_transposed.1.adj), custom_call_target="tpu_custom_call" | custom-call | tf_op jit(solution)/shard_map/scatter_far/pallas_call | solution.py:461
  129.7 0.0 copy-done.3
  129.7 14.2 %all-to-all-start.1 = ((bf16[128,8,256]{2,1,0:T(8,128)(2,1)}), bf16[128,8,256]{2,1,0:T(8,128)(2,1)S(1)}, u32[]{:S(2)}, u32[]{:S(2)}) async-start(bf16[128,8,256]{2,1,0:T(8,128)(2,1)} %bitcast.8), calls=%async_computation.1 | async-start | bytes 1048576 | tf_op jit(solution)/shard_map/all_to_all | solution.py:473
  143.9 0.0 copy-done.8
  143.9 0.1 copy.12
  144.0 0.1 reshape.47
  144.1 0.0 copy-done.2
  144.1 0.0 copy-start.4
  144.1 1.0 copy-done.4
  145.2 0.0 copy-start.6
  145.2 1.0 copy-done.6
  146.2 8.7 %scatter_local.1.kept = f32[1024,256]{1,0:T(8,128)S(1)} custom-call(s32[8192]{0:T(1024)S(1)} %get-tuple-element.23.keys_s, s32[1]{0:T(128)} %bitcast.16.active_s, s32[4]{0:T(128)S(1)} %and_select_fusion.owner_s, s32[64,1,128]{2,1,0:T(1,128)S(1)} %bitcast.20, bf16[1024,256]{1,0:T(8,128)(2,1)S(1)} %copy-done.6, bf16[256,256]{1,0:T(8,128)(2,1)S(1)} %copy-done.5, ...), custom_call_target="tpu_custom_call" | custom-call | tf_op jit(solution)/shard_map/scatter_local/pallas_call | solution.py:476
  154.9 22.6 %all-to-all-done.1 = bf16[128,8,256]{2,1,0:T(8,128)(2,1)S(1)} async-done(((bf16[128,8,256]{2,1,0:T(8,128)(2,1)}), bf16[128,8,256]{2,1,0:T(8,128)(2,1)S(1)}, u32[]{:S(2)}, u32[]{:S(2)}) %all-to-all-start.1) | async-done | bytes 524320 | tf_op jit(solution)/shard_map/all_to_all | solution.py:473
  177.5 1.6 combine.1
  (3 shorter events, 0.0 us)
Async XLA Ops:
  0.6 91.3 %copy-start = (bf16[1024,256]{1,0:T(8,128)(2,1)S(1)}, bf16[1024,256]{1,0:T(8,128)(2,1)}, u32[]{:S(2)}) copy-start(bf16[1024,256]{1,0:T(8,128)(2,1)} %feats.1) | copy-start | bytes 1572868
  0.6 91.3 %copy-start.5 = (bf16[256,256]{1,0:T(8,128)(2,1)S(1)}, bf16[256,256]{1,0:T(8,128)(2,1)}, u32[]{:S(2)}) copy-start(bf16[256,256]{1,0:T(8,128)(2,1)} %w_self.3) | copy-start | bytes 393220
  0.7 91.3 %copy-start.7 = (bf16[256,256]{1,0:T(8,128)(2,1)S(1)}, bf16[256,256]{1,0:T(8,128)(2,1)}, u32[]{:S(2)}) copy-start(bf16[256,256]{1,0:T(8,128)(2,1)} %w_neigh.1) | copy-start | bytes 393220
  3.7 53.1 %all-to-all-start = ((bf16[128,8,256]{2,1,0:T(8,128)(2,1)}), bf16[128,8,256]{2,1,0:T(8,128)(2,1)S(1)}, u32[]{:S(2)}, u32[]{:S(2)}) async-start(bf16[128,8,256]{2,1,0:T(8,128)(2,1)} %pick_rows.1), calls=%async_computation | async-start | bytes 1048576 | tf_op jit(solution)/shard_map/all_to_all | solution.py:377
  64.0 27.9 %collective-permute-start.1 = (bf16[1040,256]{1,0:T(8,128)(2,1)S(1)}, bf16[1040,256]{1,0:T(8,128)(2,1)S(1)}, u32[]{:S(2)}, u32[]{:S(2)}) collective-permute-start(bf16[1040,256]{1,0:T(8,128)(2,1)S(1)} %get-tuple-element.24), channel_id=1, source_target_pairs={{0,3},{1,0},{2,1},{3,2},{4,7},{5,4},{6,5},{7,6},{8,11},{9,8},{10,9... | collective-permute-start | bytes 1597448 | tf_op jit(solution)/shard_map/ppermute | solution.py:408
  66.9 25.0 %collective-permute-start = (bf16[1040,256]{1,0:T(8,128)(2,1)S(1)}, bf16[1040,256]{1,0:T(8,128)(2,1)S(1)}, u32[]{:S(2)}, u32[]{:S(2)}) collective-permute-start(bf16[1040,256]{1,0:T(8,128)(2,1)S(1)} %get-tuple-element.22), channel_id=1, source_target_pairs={{0,1},{1,2},{2,3},{3,0},{4,5},{5,6},{6,7},{7,4},{8,9},{9,10},{10,1... | collective-permute-start | bytes 1597448 | tf_op jit(solution)/shard_map/ppermute | solution.py:408
  70.5 21.4 %collective-permute-start.2 = (bf16[1040,256]{1,0:T(8,128)(2,1)S(1)}, bf16[1040,256]{1,0:T(8,128)(2,1)S(1)}, u32[]{:S(2)}, u32[]{:S(2)}) collective-permute-start(bf16[1040,256]{1,0:T(8,128)(2,1)S(1)} %get-tuple-element.26), channel_id=1, source_target_pairs={{0,2},{1,3},{2,0},{3,1},{4,6},{5,7},{6,4},{7,5},{8,10},{9,11},{10,... | collective-permute-start | bytes 1597448 | tf_op jit(solution)/shard_map/ppermute | solution.py:408
  91.9 52.0 %copy-start.8 = (s32[1,1,128,8]{2,3,1,0:T(8,128)S(1)}, s32[1,1,128,8]{2,3,1,0:T(8,128)}, u32[]{:S(2)}) copy-start(s32[1,1,128,8]{2,3,1,0:T(8,128)} %param.14) | copy-start | bytes 12292
  96.2 18.0 %collective-permute-start.4 = (bf16[1024,256]{1,0:T(8,128)(2,1)}, bf16[1024,256]{1,0:T(8,128)(2,1)S(1)}, u32[]{:S(2)}, u32[]{:S(2)}) collective-permute-start(bf16[1024,256]{1,0:T(8,128)(2,1)} %get-tuple-element.28.own.p0), channel_id=1, source_target_pairs={{0,1},{1,2},{2,3},{3,0},{4,5},{5,6},{6,7},{7,4},{8,9},{9,10},{10,1... | collective-permute-start | bytes 1572872 | tf_op jit(solution)/shard_map/ppermute | solution.py:408
  102.4 16.3 %collective-permute-start.5 = (bf16[1024,256]{1,0:T(8,128)(2,1)}, bf16[1024,256]{1,0:T(8,128)(2,1)S(1)}, u32[]{:S(2)}, u32[]{:S(2)}) collective-permute-start(bf16[1024,256]{1,0:T(8,128)(2,1)} %get-tuple-element.28.own.p0), channel_id=1, source_target_pairs={{0,3},{1,0},{2,1},{3,2},{4,7},{5,4},{6,5},{7,6},{8,11},{9,8},{10,9... | collective-permute-start | bytes 1572872 | tf_op jit(solution)/shard_map/ppermute | solution.py:408
  104.3 23.3 %collective-permute-start.3 = (bf16[1024,256]{1,0:T(8,128)(2,1)}, bf16[1024,256]{1,0:T(8,128)(2,1)S(1)}, u32[]{:S(2)}, u32[]{:S(2)}) collective-permute-start(bf16[1024,256]{1,0:T(8,128)(2,1)} %get-tuple-element.28.own.p0), channel_id=1, source_target_pairs={{0,2},{1,3},{2,0},{3,1},{4,6},{5,7},{6,4},{7,5},{8,10},{9,11},{10,... | collective-permute-start | bytes 1572872 | tf_op jit(solution)/shard_map/ppermute | solution.py:408
  118.7 1.0 copy-start.1
  119.8 24.3 %copy-start.2 = (bf16[1024,256]{1,0:T(8,128)(2,1)S(1)}, bf16[1024,256]{1,0:T(8,128)(2,1)}, u32[]{:S(2)}) copy-start(bf16[1024,256]{1,0:T(8,128)(2,1)} %get-tuple-element.28.own.p0) | copy-start | bytes 1572868
  127.6 2.1 %copy-start.3 = (bf16[1024,256]{1,0:T(8,128)(2,1)}, bf16[1024,256]{1,0:T(8,128)(2,1)S(1)}, u32[]{:S(2)}) copy-start(bf16[1024,256]{1,0:T(8,128)(2,1)S(1)} %collective-permute-done.3.far.p3) | copy-start | bytes 1572868
  129.7 47.8 %all-to-all-start.1 = ((bf16[128,8,256]{2,1,0:T(8,128)(2,1)}), bf16[128,8,256]{2,1,0:T(8,128)(2,1)S(1)}, u32[]{:S(2)}, u32[]{:S(2)}) async-start(bf16[128,8,256]{2,1,0:T(8,128)(2,1)} %bitcast.8), calls=%async_computation.1 | async-start | bytes 1048576 | tf_op jit(solution)/shard_map/all_to_all | solution.py:473
  144.1 1.0 copy-start.4
  145.2 1.0 copy-start.6

commit v5 on v3

--- a/solution.py
+++ b/solution.py
@@ -101,12 +101,28 @@
             lax.fori_loop(1, item[1], window, 0)
 
 
+def tiles(lo, hi, body):
+    first = lo // SUB
+    count = (hi + SUB - 1) // SUB - first
+
+    def wide(t, carry):
+        body(first + t * UNROLL, UNROLL)
+        return carry
+
+    def narrow(t, carry):
+        body(first + (count // UNROLL) * UNROLL + t, 1)
+        return carry
+
+    lax.fori_loop(0, count // UNROLL, wide, 0)
+    lax.fori_loop(0, count % UNROLL, narrow, 0)
+
+
 def build_adjacency(keys_s, keys_v, adj, lo, hi):
-    def tile(t, carry):
+    def tile(first_sub, unroll):
         todo = []
-        for u in range(UNROLL):
-            rows = [keys_v[2 * UNROLL * t + 2 * u + j] for j in range(2)]
-            base, count = sub_range(keys_s, (t * UNROLL + u) * SUB, lo, hi)
+        for u in range(unroll):
+            rows = [keys_v[2 * (first_sub + u) + j] for j in range(2)]
+            base, count = sub_range(keys_s, (first_sub + u) * SUB, lo, hi)
             base = pl.multiple_of(base, 16)
             targets = [target_of(r) for r in rows]
             first = jnp.dot(place_of(targets, base), pick_of(rows, 1), preferred_element_type=F32).astype(BF16)
@@ -119,19 +135,17 @@
             adj[pl.ds(off, WIN), :] += more.astype(BF16)
 
         further_windows(todo, run)
-        return carry
-
-    size = SUB * UNROLL
-    lax.fori_loop(lo // size, (hi + size - 1) // size, tile, 0)
+
+    tiles(lo, hi, tile)
 
 
 def aggregate_local(keys_s, keys_v, table, acc, lo, hi):
-    def tile(t, carry):
-        rows = [keys_v[2 * UNROLL * t + j] for j in range(2 * UNROLL)]
+    def tile(first_sub, unroll):
+        rows = [keys_v[2 * first_sub + j] for j in range(2 * unroll)]
         got = jnp.dot(pick_of(rows, 0), table[...], preferred_element_type=F32).astype(BF16)
         todo = []
-        for u in range(UNROLL):
-            base, count = sub_range(keys_s, (t * UNROLL + u) * SUB, lo, hi)
+        for u in range(unroll):
+            base, count = sub_range(keys_s, (first_sub + u) * SUB, lo, hi)
             base = pl.multiple_of(base, 16)
             targets = [target_of(r) for r in rows[2 * u : 2 * u + 2]]
             piece = got[SUB * u : SUB * u + SUB]
@@ -144,32 +158,33 @@
             acc[pl.ds(off, WIN), :] += jnp.dot(place_of(item[2], off), item[3], preferred_element_type=F32)
 
         further_windows(todo, run)
-        return carry
-
-    size = SUB * UNROLL
-    lax.fori_loop(lo // size, (hi + size - 1) // size, tile, 0)
-
-
-def prepare_kernel(keys_s, active_s, keys_v, table, adj_out, local_out, counts, adj, acc, sems):
+
+    tiles(lo, hi, tile)
+
+
+def prepare_kernel(keys_s, active_s, keys_v, table_hbm, adj_out, local_out, counts, adj, acc, table, sems):
+    load = pltpu.make_async_copy(table_hbm, table, sems.at[2])
+    load.start()
     boundary = local_edges(keys_s)
     adj[...] = jnp.zeros_like(adj)
     build_adjacency(keys_s, keys_v, adj, boundary, active_s[0] * 128)
     save_adj = pltpu.make_async_copy(adj.at[pl.ds(0, PART), :], adj_out, sems.at[0])
     save_adj.start()
     acc[...] = jnp.zeros_like(acc)
+    load.wait()
     aggregate_local(keys_s, keys_v, table, acc, 0, boundary)
     save_acc = pltpu.make_async_copy(acc.at[pl.ds(0, PART), :], local_out, sems.at[1])
     save_acc.start()
 
     def tally(t, total):
-        keys = [keys_v[8 * t + j] for j in range(8)]
+        keys = [keys_v[32 * t + j] for j in range(32)]
         high = jnp.concatenate(
             [one_hot((iota((32, 128), 0) == (target_of(k) >> 7)) & (k < ACTIVE_END)) for k in keys], axis=1
         )
         low = jnp.concatenate([one_hot(iota((128, 128), 0) == (target_of(k) & 127)) for k in keys], axis=1)
         return total + lax.dot_general(high, low, (((1,), (1,)), ((), ())), preferred_element_type=F32)
 
-    total = lax.fori_loop(0, EDGES // 1024, tally, jnp.zeros((32, 128), F32))
+    total = lax.fori_loop(0, EDGES // 4096, tally, jnp.zeros((32, 128), F32))
     upper = jnp.floor(total * (1.0 / 256.0))
     lower = total - upper * 256.0
     for s in range(4):
@@ -243,7 +258,7 @@
         for r in range(8):
             inv_ref[r] = inv[r : r + 1]
 
-    cols = [key_column(inv_ref[2 * i + r]) for r in range(2)]
+    cols = [key_column(inv_ref[4 * i + r]) for r in range(4)]
     inverse = jnp.concatenate([jnp.concatenate([c, c], axis=1) for c in cols], axis=0)
     totals = parts[0][...].astype(F32)
     for s in range(1, 4):
@@ -371,12 +386,13 @@
         grid_spec=pltpu.PrefetchScalarGridSpec(
             num_scalar_prefetch=2,
             grid=(),
-            in_specs=[VMEM, VMEM],
+            in_specs=[VMEM, HBM],
             out_specs=(HBM, HBM, VMEM),
             scratch_shapes=[
                 pltpu.VMEM((PADDED, ROWS), BF16),
                 pltpu.VMEM((PADDED, WIDTH), F32),
-                pltpu.SemaphoreType.DMA((2,)),
+                pltpu.VMEM((ROWS, WIDTH), BF16),
+                pltpu.SemaphoreType.DMA((3,)),
             ],
         ),
         out_shape=(
@@ -386,7 +402,7 @@
         ),
         compiler_params=params(30),
         name="prepare",
-    )(keys_s, active, keys_v, features)
+    )(keys_s, active, keys_v, in_hbm(features))
     chunks = PART // CHUNK
     rank = lax.axis_index("src")
 
@@ -435,21 +451,21 @@
     )(in_hbm(adj))
     adj_t, from_far = lax.optimization_barrier((adj_t, from_far))
 
-    block = ROWS // 4
+    block = ROWS // 2
     tile = pl.BlockSpec((block, WIDTH), lambda i: (i, 0))
     whole = pl.BlockSpec((WIDTH, WIDTH), lambda i: (0, 0))
     count_rows = pl.BlockSpec((CNT, WIDTH), lambda i: (ROWS // CNT, 0))
     received = (partial_own, from_prev, from_next, from_far)
     acts, scaled, up = pl.pallas_call(
         dense_kernel,
-        grid=(4,),
+        grid=(2,),
         in_specs=[tile, tile, whole, whole, pl.BlockSpec((1, WIDTH), lambda i: (0, 0))]
         + [tile] * 4
         + [count_rows] * 4,
         out_specs=(tile, tile, tile),
         out_shape=(shape((ROWS, WIDTH), BF16), pltpu.HBM((ROWS, WIDTH), BF16), pltpu.HBM((ROWS, WIDTH), BF16)),
         scratch_shapes=[pltpu.VMEM((8, 1, 128), F32)],
-        compiler_params=params(10),
+        compiler_params=params(14),
         name="dense_layer",
     )(features, in_hbm(cotangent), w_self, w_neigh, bias.reshape(1, WIDTH), *received, *received)
     far = shifted(scaled, 2)

time: 174 us -> 173 us (level)
  the two profiles are of different devices: /device:TPU:39 before, /device:TPU:35 now
where the time goes in v5:
time: 173 us; the launch traced here: 172 us
  Pallas kernels  54.6 us (32%)
  waiting for transfers between devices  53.7 us (31%)
  starting transfers between devices  50.9 us (29%)
  other arithmetic  7.63 us (4%)
  local copies, waits for them, and re-layouts  3.36 us (2%)
    all_to_all x1, waiting for transfers between devices, local(): lax.all_to_all(outgoing.reshape(peers, capacity, WIDTH), 'dom', split_axi...  22.5 us
    ppermute x6, waiting for transfers between devices, shifted(): return lax.ppermute(x, 'src', [(j, (j + k) % 4) for j in range(4)])  21.6 us
    all_to_all x1, starting transfers between devices, local(): lax.all_to_all(picked, 'dom', split_axis=0, concat_axis=0, tiled=True)  19.5 us
    ppermute x6, starting transfers between devices, shifted(): return lax.ppermute(x, 'src', [(j, (j + k) % 4) for j in range(4)])  17.6 us
    pallas_call x1, Pallas kernels, local(): pl.pallas_call(prepare_kernel, grid_spec=pltpu.PrefetchScalarGridSpec(num...  15.7 us
    all_to_all x1, starting transfers between devices, local(): lax.all_to_all(outgoing.reshape(peers, capacity, WIDTH), 'dom', split_axi...  13.8 us
    pallas_call x3, Pallas kernels, partials(): pl.pallas_call(functools.partial(forward_remote_kernel, shifts), grid_spe...  11.4 us
    all_to_all x1, waiting for transfers between devices, local(): lax.all_to_all(picked, 'dom', split_axis=0, concat_axis=0, tiled=True)  9.58 us
  transfers between devices with their start and end apart: 8, of which 7 were waited for; matrix products, arithmetic and copies ran while one was open for 5% of the time, Pallas kernels for 24%

profile of v5, /device:TPU:35, one launch (start us, length us, event | category | flops | bytes accessed | tf_op | source)
XLA Modules:
  0.0 171.9 jit_solution(8358941068546151718)
XLA Ops:
  0.6 2.9 %pick_rows.1 = bf16[128,8,256]{2,1,0:T(8,128)(2,1)} custom-call(s32[8,128]{1,0:T(8,128)} %bitcast.23, bf16[1024,256]{1,0:T(8,128)(2,1)} %feats.1), custom_call_target="tpu_custom_call" | custom-call | tf_op jit(solution)/shard_map/pick_rows/pallas_call | solution.py:361
  3.6 19.5 %all-to-all-start = ((bf16[128,8,256]{2,1,0:T(8,128)(2,1)}), bf16[128,8,256]{2,1,0:T(8,128)(2,1)S(1)}, u32[]{:S(2)}, u32[]{:S(2)}) async-start(bf16[128,8,256]{2,1,0:T(8,128)(2,1)} %pick_rows.1), calls=%async_computation | async-start | bytes 1048576 | tf_op jit(solution)/shard_map/all_to_all | solution.py:374
  23.7 0.8 and_add_fusion
  24.6 6.8 %sort.10 = (s32[8192]{0:T(1024)S(1)}, s32[8192]{0:T(1024)}) sort(s32[8192]{0:T(1024)S(1)} %fusion, s32[8192]{0:T(1024)S(1)} %iota.11), dimensions={0}, to_apply=%region_0.1 | sort | flops 106496 | bytes 131072 | tf_op jit(solution)/shard_map/sort | solution.py:381
  31.4 15.7 %prepare.1 = (bf16[4096,1024]{1,0:T(8,128)(2,1)}, f32[4096,256]{1,0:T(8,128)}, bf16[4,16,256]{2,1,0:T(8,128)(2,1)S(1)}) custom-call(s32[8192]{0:T(1024)S(1)} %get-tuple-element.16.keys_s, s32[1]{0:T(128)} %bitcast.13.active_s, s32[64,1,128]{2,1,0:T(1,128)S(1)} %bitcast.19, bf16[1024,256]{1,0:T(8,128)(2,1)} %feats.1), custom_call_target="tpu_custom_call" | custom-call | tf_op jit(solution)/shard_map/prepare/pallas_call | solution.py:384
  47.0 9.6 %all-to-all-done = bf16[128,8,256]{2,1,0:T(8,128)(2,1)S(1)} async-done(((bf16[128,8,256]{2,1,0:T(8,128)(2,1)}), bf16[128,8,256]{2,1,0:T(8,128)(2,1)S(1)}, u32[]{:S(2)}, u32[]{:S(2)}) %all-to-all-start) | async-done | bytes 524320 | tf_op jit(solution)/shard_map/all_to_all | solution.py:374
  56.6 3.3 %aggregate_remote_2.1 = bf16[1040,256]{1,0:T(8,128)(2,1)S(1)} custom-call(s32[4]{0:T(128)S(1)} %and_select_fusion.owner_s, bf16[1024,256]{1,0:T(8,128)(2,1)S(1)} %bitcast.15, bf16[4,16,256]{2,1,0:T(8,128)(2,1)S(1)} %get-tuple-element.17.counts, bf16[4096,1024]{1,0:T(8,128)(2,1)} %get-tuple-element.18.adj_hbm.adj, f32[4096,256]{1,0:T(8,128)} %get-tuple-element.19.local_hbm), custom_call_target="tpu_custom_call" | custom-call | tf_op jit(solution)/shard_map/aggregate_remote_2/pallas_call | solution.py:416
  60.0 3.8 %collective-permute-start.2 = (bf16[1040,256]{1,0:T(8,128)(2,1)S(1)}, bf16[1040,256]{1,0:T(8,128)(2,1)S(1)}, u32[]{:S(2)}, u32[]{:S(2)}) collective-permute-start(bf16[1040,256]{1,0:T(8,128)(2,1)S(1)} %aggregate_remote_2.1), channel_id=1, source_target_pairs={{0,2},{1,3},{2,0},{3,1},{4,6},{5,7},{6,4},{7,5},{8,10},{9,11},{10,... | collective-permute-start | bytes 1597448 | tf_op jit(solution)/shard_map/ppermute | solution.py:412
  63.7 4.7 %aggregate_remote_1_3.1 = (bf16[1040,256]{1,0:T(8,128)(2,1)S(1)}, bf16[1040,256]{1,0:T(8,128)(2,1)S(1)}) custom-call(s32[4]{0:T(128)S(1)} %and_select_fusion.owner_s, bf16[1024,256]{1,0:T(8,128)(2,1)S(1)} %bitcast.16, bf16[4,16,256]{2,1,0:T(8,128)(2,1)S(1)} %get-tuple-element.17.counts, bf16[4096,1024]{1,0:T(8,128)(2,1)} %get-tuple-element.18.adj_hbm.adj, ...), custom_call_target="tpu_custom_call" | custom-call | tf_op jit(solution)/shard_map/aggregate_remote_1_3/pallas_call | solution.py:416
  68.5 1.9 %collective-permute-start = (bf16[1040,256]{1,0:T(8,128)(2,1)S(1)}, bf16[1040,256]{1,0:T(8,128)(2,1)S(1)}, u32[]{:S(2)}, u32[]{:S(2)}) collective-permute-start(bf16[1040,256]{1,0:T(8,128)(2,1)S(1)} %get-tuple-element.21), channel_id=1, source_target_pairs={{0,1},{1,2},{2,3},{3,0},{4,5},{5,6},{6,7},{7,4},{8,9},{9,10},{10,1... | collective-permute-start | bytes 1597448 | tf_op jit(solution)/shard_map/ppermute | solution.py:412
  70.4 0.0 copy-start.9
  70.4 3.4 %collective-permute-start.1 = (bf16[1040,256]{1,0:T(8,128)(2,1)S(1)}, bf16[1040,256]{1,0:T(8,128)(2,1)S(1)}, u32[]{:S(2)}, u32[]{:S(2)}) collective-permute-start(bf16[1040,256]{1,0:T(8,128)(2,1)S(1)} %get-tuple-element.23), channel_id=1, source_target_pairs={{0,3},{1,0},{2,1},{3,2},{4,7},{5,4},{6,5},{7,6},{8,11},{9,8},{10,9... | collective-permute-start | bytes 1597448 | tf_op jit(solution)/shard_map/ppermute | solution.py:412
  73.8 6.8 %adjacency_transposed.1.adj = bf16[8,1024,512]{2,1,0:T(8,128)(2,1)S(1)} custom-call(bf16[4096,1024]{1,0:T(8,128)(2,1)} %get-tuple-element.18.adj_hbm.adj), custom_call_target="tpu_custom_call" | custom-call | tf_op jit(solution)/shard_map/adjacency_transposed/pallas_call | solution.py:443
  80.6 0.0 copy-done.9
  80.6 0.0 copy-start
  80.6 0.0 copy-start.5
  80.7 0.0 copy-start.7
  80.7 3.3 %aggregate_remote_0.1.refs_0_.refs_4_ = bf16[1040,256]{1,0:T(8,128)(2,1)S(1)} custom-call(s32[4]{0:T(128)S(1)} %and_select_fusion.owner_s, bf16[1024,256]{1,0:T(8,128)(2,1)S(1)} %bitcast.17, bf16[4,16,256]{2,1,0:T(8,128)(2,1)S(1)} %get-tuple-element.17.counts, bf16[4096,1024]{1,0:T(8,128)(2,1)} %get-tuple-element.18.adj_hbm.adj, ...), custom_call_target="tpu_custom_call" | custom-call | tf_op jit(solution)/shard_map/aggregate_remote_0/pallas_call | solution.py:416
  84.0 0.0 collective-permute-done.2.refs_3_.refs_7_
  84.0 4.6 %collective-permute-done.refs_1_.refs_5_ = bf16[1040,256]{1,0:T(8,128)(2,1)S(1)} collective-permute-done((bf16[1040,256]{1,0:T(8,128)(2,1)S(1)}, bf16[1040,256]{1,0:T(8,128)(2,1)S(1)}, u32[]{:S(2)}, u32[]{:S(2)}) %collective-permute-start) | collective-permute-done | bytes 532512 | tf_op jit(solution)/shard_map/ppermute | solution.py:412
  88.7 0.2 collective-permute-done.1.refs_2_.refs_6_
  88.8 0.0 copy-done
  88.8 0.0 copy-done.5
  88.8 0.0 copy-done.7
  88.9 3.1 %dense_layer.1 = (bf16[1024,256]{1,0:T(8,128)(2,1)}, bf16[1024,256]{1,0:T(8,128)(2,1)}, bf16[1024,256]{1,0:T(8,128)(2,1)}) custom-call(bf16[1024,256]{1,0:T(8,128)(2,1)S(1)} %copy-done, bf16[1024,256]{1,0:T(8,128)(2,1)} %cots.1, bf16[256,256]{1,0:T(8,128)(2,1)S(1)} %copy-done.5, bf16[256,256]{1,0:T(8,128)(2,1)S(1)} %copy-done.7, ...), custom_call_target="tpu_custom_call" | custom-call | tf_op jit(solution)/shard_map/dense_layer/pallas_call | solution.py:459
  91.9 3.1 %collective-permute-start.4 = (bf16[1024,256]{1,0:T(8,128)(2,1)}, bf16[1024,256]{1,0:T(8,128)(2,1)S(1)}, u32[]{:S(2)}, u32[]{:S(2)}) collective-permute-start(bf16[1024,256]{1,0:T(8,128)(2,1)} %get-tuple-element.26.own.p0), channel_id=1, source_target_pairs={{0,1},{1,2},{2,3},{3,0},{4,5},{5,6},{6,7},{7,4},{8,9},{9,10},{10,1... | collective-permute-start | bytes 1572872 | tf_op jit(solution)/shard_map/ppermute | solution.py:412
  95.1 2.1 %collective-permute-start.5 = (bf16[1024,256]{1,0:T(8,128)(2,1)}, bf16[1024,256]{1,0:T(8,128)(2,1)S(1)}, u32[]{:S(2)}, u32[]{:S(2)}) collective-permute-start(bf16[1024,256]{1,0:T(8,128)(2,1)} %get-tuple-element.26.own.p0), channel_id=1, source_target_pairs={{0,3},{1,0},{2,1},{3,2},{4,7},{5,4},{6,5},{7,6},{8,11},{9,8},{10,9... | collective-permute-start | bytes 1572872 | tf_op jit(solution)/shard_map/ppermute | solution.py:412
  97.2 3.3 %collective-permute-start.3 = (bf16[1024,256]{1,0:T(8,128)(2,1)}, bf16[1024,256]{1,0:T(8,128)(2,1)S(1)}, u32[]{:S(2)}, u32[]{:S(2)}) collective-permute-start(bf16[1024,256]{1,0:T(8,128)(2,1)} %get-tuple-element.26.own.p0), channel_id=1, source_target_pairs={{0,2},{1,3},{2,0},{3,1},{4,6},{5,7},{6,4},{7,5},{8,10},{9,11},{10,... | collective-permute-start | bytes 1572872 | tf_op jit(solution)/shard_map/ppermute | solution.py:412
  100.5 6.5 %collective-permute-done.4.left.p1 = bf16[1024,256]{1,0:T(8,128)(2,1)S(1)} collective-permute-done((bf16[1024,256]{1,0:T(8,128)(2,1)}, bf16[1024,256]{1,0:T(8,128)(2,1)S(1)}, u32[]{:S(2)}, u32[]{:S(2)}) %collective-permute-start.4) | collective-permute-done | bytes 524320 | tf_op jit(solution)/shard_map/ppermute | solution.py:412
  107.0 3.4 %collective-permute-done.5.right.p2 = bf16[1024,256]{1,0:T(8,128)(2,1)S(1)} collective-permute-done((bf16[1024,256]{1,0:T(8,128)(2,1)}, bf16[1024,256]{1,0:T(8,128)(2,1)S(1)}, u32[]{:S(2)}, u32[]{:S(2)}) %collective-permute-start.5) | collective-permute-done | bytes 524320 | tf_op jit(solution)/shard_map/ppermute | solution.py:412
  110.4 1.0 copy-done.1
  111.4 2.3 %scatter_near.1.near = f32[1024,256]{1,0:T(8,128)S(1)} custom-call(s32[4]{0:T(128)S(1)} %and_select_fusion.owner_s, bf16[1024,256]{1,0:T(8,128)(2,1)S(1)} %copy-done.1, bf16[1024,256]{1,0:T(8,128)(2,1)S(1)} %collective-permute-done.4.left.p1, bf16[1024,256]{1,0:T(8,128)(2,1)S(1)} %collective-permute-done.5.right.p2, ...), custom_call_target="tpu_custom_call" | custom-call | tf_op jit(solution)/shard_map/scatter_near/pallas_call | solution.py:476
  113.7 0.0 copy-start.8
  113.8 0.0 copy-start.2
  113.8 6.9 %collective-permute-done.3.far.p3 = bf16[1024,256]{1,0:T(8,128)(2,1)S(1)} collective-permute-done((bf16[1024,256]{1,0:T(8,128)(2,1)}, bf16[1024,256]{1,0:T(8,128)(2,1)S(1)}, u32[]{:S(2)}, u32[]{:S(2)}) %collective-permute-start.3) | collective-permute-done | bytes 524320 | tf_op jit(solution)/shard_map/ppermute | solution.py:412
  120.7 2.0 %scatter_far.1 = bf16[1024,256]{1,0:T(8,128)(2,1)} custom-call(s32[4]{0:T(128)S(1)} %and_select_fusion.owner_s, bf16[1024,256]{1,0:T(8,128)(2,1)S(1)} %collective-permute-done.3.far.p3, f32[1024,256]{1,0:T(8,128)S(1)} %scatter_near.1.near, bf16[8,1024,512]{2,1,0:T(8,128)(2,1)S(1)} %adjacency_transposed.1.adj), custom_call_target="tpu_custom_call" | custom-call | tf_op jit(solution)/shard_map/scatter_far/pallas_call | solution.py:476
  122.7 0.0 copy-done.3
  122.7 13.8 %all-to-all-start.1 = ((bf16[128,8,256]{2,1,0:T(8,128)(2,1)}), bf16[128,8,256]{2,1,0:T(8,128)(2,1)S(1)}, u32[]{:S(2)}, u32[]{:S(2)}) async-start(bf16[128,8,256]{2,1,0:T(8,128)(2,1)} %bitcast.8), calls=%async_computation.1 | async-start | bytes 1048576 | tf_op jit(solution)/shard_map/all_to_all | solution.py:488
  136.6 0.0 copy-done.8
  136.6 0.1 copy.12
  136.7 0.1 reshape.47
  136.8 0.0 copy-done.2
  136.8 0.0 copy-start.4
  136.8 1.0 copy-done.4
  137.8 1.0 copy-done.6
  138.9 8.8 %scatter_local.1.kept = f32[1024,256]{1,0:T(8,128)S(1)} custom-call(s32[8192]{0:T(1024)S(1)} %get-tuple-element.16.keys_s, s32[1]{0:T(128)} %bitcast.14.active_s, s32[4]{0:T(128)S(1)} %and_select_fusion.owner_s, s32[64,1,128]{2,1,0:T(1,128)S(1)} %bitcast.20, bf16[1024,256]{1,0:T(8,128)(2,1)S(1)} %copy-done.6, bf16[256,256]{1,0:T(8,128)(2,1)S(1)} %copy-done.5, ...), custom_call_target="tpu_custom_call" | custom-call | tf_op jit(solution)/shard_map/scatter_local/pallas_call | solution.py:491
  147.7 22.5 %all-to-all-done.1 = bf16[128,8,256]{2,1,0:T(8,128)(2,1)S(1)} async-done(((bf16[128,8,256]{2,1,0:T(8,128)(2,1)}), bf16[128,8,256]{2,1,0:T(8,128)(2,1)S(1)}, u32[]{:S(2)}, u32[]{:S(2)}) %all-to-all-start.1) | async-done | bytes 524320 | tf_op jit(solution)/shard_map/all_to_all | solution.py:488
  170.1 1.6 combine.1
  (7 shorter events, 0.0 us)
Async XLA Ops:
  3.6 53.1 %all-to-all-start = ((bf16[128,8,256]{2,1,0:T(8,128)(2,1)}), bf16[128,8,256]{2,1,0:T(8,128)(2,1)S(1)}, u32[]{:S(2)}, u32[]{:S(2)}) async-start(bf16[128,8,256]{2,1,0:T(8,128)(2,1)} %pick_rows.1), calls=%async_computation | async-start | bytes 1048576 | tf_op jit(solution)/shard_map/all_to_all | solution.py:374
  60.0 24.1 %collective-permute-start.2 = (bf16[1040,256]{1,0:T(8,128)(2,1)S(1)}, bf16[1040,256]{1,0:T(8,128)(2,1)S(1)}, u32[]{:S(2)}, u32[]{:S(2)}) collective-permute-start(bf16[1040,256]{1,0:T(8,128)(2,1)S(1)} %aggregate_remote_2.1), channel_id=1, source_target_pairs={{0,2},{1,3},{2,0},{3,1},{4,6},{5,7},{6,4},{7,5},{8,10},{9,11},{10,... | collective-permute-start | bytes 1597448 | tf_op jit(solution)/shard_map/ppermute | solution.py:412
  68.5 20.2 %collective-permute-start = (bf16[1040,256]{1,0:T(8,128)(2,1)S(1)}, bf16[1040,256]{1,0:T(8,128)(2,1)S(1)}, u32[]{:S(2)}, u32[]{:S(2)}) collective-permute-start(bf16[1040,256]{1,0:T(8,128)(2,1)S(1)} %get-tuple-element.21), channel_id=1, source_target_pairs={{0,1},{1,2},{2,3},{3,0},{4,5},{5,6},{6,7},{7,4},{8,9},{9,10},{10,1... | collective-permute-start | bytes 1597448 | tf_op jit(solution)/shard_map/ppermute | solution.py:412
  70.4 10.2 %copy-start.9 = (bf16[256]{0:T(256)(128)(2,1)S(1)}, bf16[256]{0:T(256)(128)(2,1)}, u32[]{:S(2)}) copy-start(bf16[256]{0:T(256)(128)(2,1)} %param.13) | copy-start | bytes 1540
  70.4 18.4 %collective-permute-start.1 = (bf16[1040,256]{1,0:T(8,128)(2,1)S(1)}, bf16[1040,256]{1,0:T(8,128)(2,1)S(1)}, u32[]{:S(2)}, u32[]{:S(2)}) collective-permute-start(bf16[1040,256]{1,0:T(8,128)(2,1)S(1)} %get-tuple-element.23), channel_id=1, source_target_pairs={{0,3},{1,0},{2,1},{3,2},{4,7},{5,4},{6,5},{7,6},{8,11},{9,8},{10,9... | collective-permute-start | bytes 1597448 | tf_op jit(solution)/shard_map/ppermute | solution.py:412
  80.6 8.2 %copy-start = (bf16[1024,256]{1,0:T(8,128)(2,1)S(1)}, bf16[1024,256]{1,0:T(8,128)(2,1)}, u32[]{:S(2)}) copy-start(bf16[1024,256]{1,0:T(8,128)(2,1)} %feats.1) | copy-start | bytes 1572868
  80.6 8.2 %copy-start.5 = (bf16[256,256]{1,0:T(8,128)(2,1)S(1)}, bf16[256,256]{1,0:T(8,128)(2,1)}, u32[]{:S(2)}) copy-start(bf16[256,256]{1,0:T(8,128)(2,1)} %w_self.3) | copy-start | bytes 393220
  80.7 8.2 %copy-start.7 = (bf16[256,256]{1,0:T(8,128)(2,1)S(1)}, bf16[256,256]{1,0:T(8,128)(2,1)}, u32[]{:S(2)}) copy-start(bf16[256,256]{1,0:T(8,128)(2,1)} %w_neigh.1) | copy-start | bytes 393220
  91.9 15.1 %collective-permute-start.4 = (bf16[1024,256]{1,0:T(8,128)(2,1)}, bf16[1024,256]{1,0:T(8,128)(2,1)S(1)}, u32[]{:S(2)}, u32[]{:S(2)}) collective-permute-start(bf16[1024,256]{1,0:T(8,128)(2,1)} %get-tuple-element.26.own.p0), channel_id=1, source_target_pairs={{0,1},{1,2},{2,3},{3,0},{4,5},{5,6},{6,7},{7,4},{8,9},{9,10},{10,1... | collective-permute-start | bytes 1572872 | tf_op jit(solution)/shard_map/ppermute | solution.py:412
  95.1 15.3 %collective-permute-start.5 = (bf16[1024,256]{1,0:T(8,128)(2,1)}, bf16[1024,256]{1,0:T(8,128)(2,1)S(1)}, u32[]{:S(2)}, u32[]{:S(2)}) collective-permute-start(bf16[1024,256]{1,0:T(8,128)(2,1)} %get-tuple-element.26.own.p0), channel_id=1, source_target_pairs={{0,3},{1,0},{2,1},{3,2},{4,7},{5,4},{6,5},{7,6},{8,11},{9,8},{10,9... | collective-permute-start | bytes 1572872 | tf_op jit(solution)/shard_map/ppermute | solution.py:412
  97.2 23.5 %collective-permute-start.3 = (bf16[1024,256]{1,0:T(8,128)(2,1)}, bf16[1024,256]{1,0:T(8,128)(2,1)S(1)}, u32[]{:S(2)}, u32[]{:S(2)}) collective-permute-start(bf16[1024,256]{1,0:T(8,128)(2,1)} %get-tuple-element.26.own.p0), channel_id=1, source_target_pairs={{0,2},{1,3},{2,0},{3,1},{4,6},{5,7},{6,4},{7,5},{8,10},{9,11},{10,... | collective-permute-start | bytes 1572872 | tf_op jit(solution)/shard_map/ppermute | solution.py:412
  110.4 1.0 copy-start.1
  113.7 22.8 %copy-start.8 = (s32[1,1,128,8]{2,3,1,0:T(8,128)S(1)}, s32[1,1,128,8]{2,3,1,0:T(8,128)}, u32[]{:S(2)}) copy-start(s32[1,1,128,8]{2,3,1,0:T(8,128)} %param.14) | copy-start | bytes 12292
  113.8 23.0 %copy-start.2 = (bf16[1024,256]{1,0:T(8,128)(2,1)S(1)}, bf16[1024,256]{1,0:T(8,128)(2,1)}, u32[]{:S(2)}) copy-start(bf16[1024,256]{1,0:T(8,128)(2,1)} %get-tuple-element.26.own.p0) | copy-start | bytes 1572868
  120.7 2.1 %copy-start.3 = (bf16[1024,256]{1,0:T(8,128)(2,1)}, bf16[1024,256]{1,0:T(8,128)(2,1)S(1)}, u32[]{:S(2)}) copy-start(bf16[1024,256]{1,0:T(8,128)(2,1)S(1)} %collective-permute-done.3.far.p3) | copy-start | bytes 1572868
  122.7 47.4 %all-to-all-start.1 = ((bf16[128,8,256]{2,1,0:T(8,128)(2,1)}), bf16[128,8,256]{2,1,0:T(8,128)(2,1)S(1)}, u32[]{:S(2)}, u32[]{:S(2)}) async-start(bf16[128,8,256]{2,1,0:T(8,128)(2,1)} %bitcast.8), calls=%async_computation.1 | async-start | bytes 1048576 | tf_op jit(solution)/shard_map/all_to_all | solution.py:488
  136.8 1.0 copy-start.4
  137.8 1.0 copy-start.6

commit v6 on v5

--- a/solution.py
+++ b/solution.py
@@ -14,8 +14,10 @@
 CHUNK = 512
 UNROLL = 4
 SUB = 256
-WIN = 384
-PADDED = PART + WIN
+WIN = 320
+BACK = 384
+FINE = 256
+PADDED = PART + BACK
 CNT = 16
 LOCAL_END = 1 << 22
 ACTIVE_END = 1 << 23
@@ -63,11 +65,11 @@
     return 0, boundary
 
 
-def sub_range(keys_s, start, lo, hi):
+def sub_range(keys_s, start, lo, hi, win=WIN):
     first = jnp.maximum(start, lo)
     last = jnp.minimum(start + SUB - 1, hi - 1)
     base = (target_of(keys_s[first]) // 16) * 16
-    count = jnp.where(last >= first, (target_of(keys_s[last]) - base) // WIN + 1, 0)
+    count = jnp.where(last >= first, (target_of(keys_s[last]) - base) // win + 1, 0)
     return base, count
 
 
@@ -200,11 +202,11 @@
 
 def forward_remote_kernel(shifts, owner_s, table, counts, adj_hbm, local_hbm, *refs):
     outs, (adj, local_part, sems) = refs[:-3], refs[-3:]
-    halves = ROWS // CHUNK
+    halves = ROWS // FINE
     loads = []
     for n in range(len(outs)):
         for h in range(halves):
-            rows = pl.ds(pl.multiple_of(owner_s[shifts[n]] * ROWS + h * CHUNK, CHUNK), CHUNK)
+            rows = pl.ds(pl.multiple_of(owner_s[shifts[n]] * ROWS + h * FINE, FINE), FINE)
             i = n * halves + h
             pair = (
                 pltpu.make_async_copy(adj_hbm.at[rows, :], adj.at[i], sems.at[0, i]),
@@ -220,7 +222,7 @@
             for copy in loads[i]:
                 copy.wait()
             total = local_part[i] + jnp.dot(adj[i], table[...], preferred_element_type=F32)
-            out[h * CHUNK : h * CHUNK + CHUNK, :] = total.astype(BF16)
+            out[h * FINE : h * FINE + FINE, :] = total.astype(BF16)
 
 
 def pick_kernel(senders, table, out, acc):
@@ -284,21 +286,21 @@
     def tile(t, carry):
         rows = [keys_v[4 * t + j] for j in range(4)]
         for sub in range(CHUNK // SUB):
-            base, count = sub_range(keys_s, t * CHUNK + sub * SUB, lo, hi)
+            base, count = sub_range(keys_s, t * CHUNK + sub * SUB, lo, hi, BACK)
             cols = [target_of(key_column(rows[2 * sub + j])) for j in range(2)]
 
             def window(w):
-                off = pl.multiple_of(base + w * WIN, 16)
+                off = pl.multiple_of(base + w * BACK, 16)
                 pick = jnp.concatenate(
                     [
                         jnp.concatenate(
-                            [one_hot(c - off == iota((128, 128), 1) + 128 * k) for k in range(WIN // 128)], axis=1
+                            [one_hot(c - off == iota((128, 128), 1) + 128 * k) for k in range(BACK // 128)], axis=1
                         )
                         for c in cols
                     ],
                     axis=0,
                 )
-                return jnp.dot(pick, spread[pl.ds(off, WIN), :], preferred_element_type=F32)
+                return jnp.dot(pick, spread[pl.ds(off, BACK), :], preferred_element_type=F32)
 
             rows_ref[sub * SUB : (sub + 1) * SUB, :] = window(0)
 
@@ -327,12 +329,12 @@
     return total
 
 
-def backward_near_kernel(owner_s, own, left, right, adj, out):
-    out[...] = piece_sum(owner_s, ((0, own), (3, left), (1, right)), adj, None)
-
-
-def backward_far_kernel(owner_s, far, near, adj, out):
-    out[...] = piece_sum(owner_s, ((2, far),), adj, near[...]).astype(BF16)
+def backward_near_kernel(owner_s, own, left, adj, out):
+    out[...] = piece_sum(owner_s, ((0, own), (3, left)), adj, None)
+
+
+def backward_far_kernel(owner_s, right, far, near, adj, out):
+    out[...] = piece_sum(owner_s, ((1, right), (2, far)), adj, near[...]).astype(BF16)
 
 
 def backward_local_kernel(keys_s, active_s, owner_s, keys_v, up, w_self, p0, p1, p2, p3, out, spread, rows_ref, sems):
@@ -341,7 +343,7 @@
         rows = pl.ds(pl.multiple_of(owner_s[shift] * ROWS, ROWS), ROWS)
         loads.append(pltpu.make_async_copy(piece, spread.at[rows, :], sems.at[n]))
         loads[n].start()
-    spread[PART:, :] = jnp.zeros((WIN, WIDTH), BF16)
+    spread[PART:, :] = jnp.zeros((BACK, WIDTH), BF16)
     out[...] = lax.dot_general(up[...], w_self[...], (((1,), (1,)), ((), ())), preferred_element_type=F32)
     for copy in loads:
         copy.wait()
@@ -421,9 +423,9 @@
                 in_specs=[VMEM, VMEM, HBM, HBM],
                 out_specs=[VMEM] * count,
                 scratch_shapes=[
-                    pltpu.VMEM((2 * count, CHUNK, ROWS), BF16),
-                    pltpu.VMEM((2 * count, CHUNK, WIDTH), F32),
-                    pltpu.SemaphoreType.DMA((2, 2 * count)),
+                    pltpu.VMEM((ROWS // FINE * count, FINE, ROWS), BF16),
+                    pltpu.VMEM((ROWS // FINE * count, FINE, WIDTH), F32),
+                    pltpu.SemaphoreType.DMA((2, ROWS // FINE * count)),
                 ],
             ),
             out_shape=[shape((ROWS + CNT, WIDTH), BF16)] * count,
@@ -483,8 +485,8 @@
             name=name,
         )(order, *pieces, adj_t)
 
-    near = backward(backward_near_kernel, (scaled, prev, follow), F32, "scatter_near")
-    outgoing = backward(backward_far_kernel, (far, near), BF16, "scatter_far")
+    near = backward(backward_near_kernel, (scaled, prev), F32, "scatter_near")
+    outgoing = backward(backward_far_kernel, (follow, far, near), BF16, "scatter_far")
     returned = lax.all_to_all(
         outgoing.reshape(peers, capacity, WIDTH), "dom", split_axis=0, concat_axis=0, tiled=True
     ).reshape(peers * capacity, WIDTH)

time: 173 us -> 169 us (0.977)
  the two profiles are of different devices: /device:TPU:35 before, /device:TPU:33 now
where the time goes in v6:
time: 169 us
  Pallas kernels  54.7 us (32%)
  starting transfers between devices  52 us (31%)
  waiting for transfers between devices  49.2 us (29%)
  other arithmetic  7.63 us (5%)
  local copies, waits for them, and re-layouts  3.36 us (2%)
  between operations  1.7 us (1%)
    all_to_all x1, waiting for transfers between devices, local(): lax.all_to_all(outgoing.reshape(peers, capacity, WIDTH), 'dom', split_axi...  22.6 us
    ppermute x6, starting transfers between devices, shifted(): return lax.ppermute(x, 'src', [(j, (j + k) % 4) for j in range(4)])  21.1 us
    all_to_all x1, starting transfers between devices, local(): lax.all_to_all(picked, 'dom', split_axis=0, concat_axis=0, tiled=True)  19.5 us
    ppermute x6, waiting for transfers between devices, shifted(): return lax.ppermute(x, 'src', [(j, (j + k) % 4) for j in range(4)])  16.6 us
    pallas_call x1, Pallas kernels, local(): pl.pallas_call(prepare_kernel, grid_spec=pltpu.PrefetchScalarGridSpec(num...  15.3 us
    pallas_call x3, Pallas kernels, partials(): pl.pallas_call(functools.partial(forward_remote_kernel, shifts), grid_spe...  12 us
    all_to_all x1, starting transfers between devices, local(): lax.all_to_all(outgoing.reshape(peers, capacity, WIDTH), 'dom', split_axi...  11.4 us
    all_to_all x1, waiting for transfers between devices, local(): lax.all_to_all(picked, 'dom', split_axis=0, concat_axis=0, tiled=True)  10 us
  transfers between devices with their start and end apart: 8, of which 5 were waited for; matrix products, arithmetic and copies ran while one was open for 5% of the time, Pallas kernels for 24%

profile of v6, /device:TPU:33, one launch (start us, length us, event | category | flops | bytes accessed | tf_op | source)
XLA Modules:
  0.0 168.6 jit_solution(1646034638298198568)
XLA Ops:
  0.6 2.9 %pick_rows.1 = bf16[128,8,256]{2,1,0:T(8,128)(2,1)} custom-call(s32[8,128]{1,0:T(8,128)} %bitcast.23, bf16[1024,256]{1,0:T(8,128)(2,1)} %feats.1), custom_call_target="tpu_custom_call" | custom-call | tf_op jit(solution)/shard_map/pick_rows/pallas_call | solution.py:363
  3.6 19.5 %all-to-all-start = ((bf16[128,8,256]{2,1,0:T(8,128)(2,1)}), bf16[128,8,256]{2,1,0:T(8,128)(2,1)S(1)}, u32[]{:S(2)}, u32[]{:S(2)}) async-start(bf16[128,8,256]{2,1,0:T(8,128)(2,1)} %pick_rows.1), calls=%async_computation | async-start | bytes 1048576 | tf_op jit(solution)/shard_map/all_to_all | solution.py:376
  23.7 0.8 and_add_fusion
  24.6 6.8 %sort.10 = (s32[8192]{0:T(1024)S(1)}, s32[8192]{0:T(1024)}) sort(s32[8192]{0:T(1024)S(1)} %fusion, s32[8192]{0:T(1024)S(1)} %iota.11), dimensions={0}, to_apply=%region_0.1 | sort | flops 106496 | bytes 131072 | tf_op jit(solution)/shard_map/sort | solution.py:383
  31.4 15.3 %prepare.1 = (bf16[4096,1024]{1,0:T(8,128)(2,1)}, f32[4096,256]{1,0:T(8,128)}, bf16[4,16,256]{2,1,0:T(8,128)(2,1)S(1)}) custom-call(s32[8192]{0:T(1024)S(1)} %get-tuple-element.16.keys_s, s32[1]{0:T(128)} %bitcast.13.active_s, s32[64,1,128]{2,1,0:T(1,128)S(1)} %bitcast.19, bf16[1024,256]{1,0:T(8,128)(2,1)} %feats.1), custom_call_target="tpu_custom_call" | custom-call | tf_op jit(solution)/shard_map/prepare/pallas_call | solution.py:386
  46.6 10.0 %all-to-all-done = bf16[128,8,256]{2,1,0:T(8,128)(2,1)S(1)} async-done(((bf16[128,8,256]{2,1,0:T(8,128)(2,1)}), bf16[128,8,256]{2,1,0:T(8,128)(2,1)S(1)}, u32[]{:S(2)}, u32[]{:S(2)}) %all-to-all-start) | async-done | bytes 524320 | tf_op jit(solution)/shard_map/all_to_all | solution.py:376
  56.6 3.4 %aggregate_remote_2.1 = bf16[1040,256]{1,0:T(8,128)(2,1)S(1)} custom-call(s32[4]{0:T(128)S(1)} %and_select_fusion.owner_s, bf16[1024,256]{1,0:T(8,128)(2,1)S(1)} %bitcast.15, bf16[4,16,256]{2,1,0:T(8,128)(2,1)S(1)} %get-tuple-element.17.counts, bf16[4096,1024]{1,0:T(8,128)(2,1)} %get-tuple-element.18.adj_hbm.adj, f32[4096,256]{1,0:T(8,128)} %get-tuple-element.19.local_hbm), custom_call_target="tpu_custom_call" | custom-call | tf_op jit(solution)/shard_map/aggregate_remote_2/pallas_call | solution.py:418
  60.1 4.6 %collective-permute-start.2 = (bf16[1040,256]{1,0:T(8,128)(2,1)S(1)}, bf16[1040,256]{1,0:T(8,128)(2,1)S(1)}, u32[]{:S(2)}, u32[]{:S(2)}) collective-permute-start(bf16[1040,256]{1,0:T(8,128)(2,1)S(1)} %aggregate_remote_2.1), channel_id=1, source_target_pairs={{0,2},{1,3},{2,0},{3,1},{4,6},{5,7},{6,4},{7,5},{8,10},{9,11},{10,... | collective-permute-start | bytes 1597448 | tf_op jit(solution)/shard_map/ppermute | solution.py:414
  64.7 5.2 %aggregate_remote_1_3.1 = (bf16[1040,256]{1,0:T(8,128)(2,1)S(1)}, bf16[1040,256]{1,0:T(8,128)(2,1)S(1)}) custom-call(s32[4]{0:T(128)S(1)} %and_select_fusion.owner_s, bf16[1024,256]{1,0:T(8,128)(2,1)S(1)} %bitcast.16, bf16[4,16,256]{2,1,0:T(8,128)(2,1)S(1)} %get-tuple-element.17.counts, bf16[4096,1024]{1,0:T(8,128)(2,1)} %get-tuple-element.18.adj_hbm.adj, ...), custom_call_target="tpu_custom_call" | custom-call | tf_op jit(solution)/shard_map/aggregate_remote_1_3/pallas_call | solution.py:418
  69.9 2.2 %collective-permute-start = (bf16[1040,256]{1,0:T(8,128)(2,1)S(1)}, bf16[1040,256]{1,0:T(8,128)(2,1)S(1)}, u32[]{:S(2)}, u32[]{:S(2)}) collective-permute-start(bf16[1040,256]{1,0:T(8,128)(2,1)S(1)} %get-tuple-element.21), channel_id=1, source_target_pairs={{0,1},{1,2},{2,3},{3,0},{4,5},{5,6},{6,7},{7,4},{8,9},{9,10},{10,1... | collective-permute-start | bytes 1597448 | tf_op jit(solution)/shard_map/ppermute | solution.py:414
  72.1 0.0 copy-start.9
  72.2 4.3 %collective-permute-start.1 = (bf16[1040,256]{1,0:T(8,128)(2,1)S(1)}, bf16[1040,256]{1,0:T(8,128)(2,1)S(1)}, u32[]{:S(2)}, u32[]{:S(2)}) collective-permute-start(bf16[1040,256]{1,0:T(8,128)(2,1)S(1)} %get-tuple-element.23), channel_id=1, source_target_pairs={{0,3},{1,0},{2,1},{3,2},{4,7},{5,4},{6,5},{7,6},{8,11},{9,8},{10,9... | collective-permute-start | bytes 1597448 | tf_op jit(solution)/shard_map/ppermute | solution.py:414
  76.4 6.8 %adjacency_transposed.1.adj = bf16[8,1024,512]{2,1,0:T(8,128)(2,1)S(1)} custom-call(bf16[4096,1024]{1,0:T(8,128)(2,1)} %get-tuple-element.18.adj_hbm.adj), custom_call_target="tpu_custom_call" | custom-call | tf_op jit(solution)/shard_map/adjacency_transposed/pallas_call | solution.py:445
  83.2 0.0 copy-done.9
  83.3 0.0 copy-start
  83.3 0.0 copy-start.5
  83.3 0.0 copy-start.7
  83.3 3.4 %aggregate_remote_0.1.refs_0_.refs_4_ = bf16[1040,256]{1,0:T(8,128)(2,1)S(1)} custom-call(s32[4]{0:T(128)S(1)} %and_select_fusion.owner_s, bf16[1024,256]{1,0:T(8,128)(2,1)S(1)} %bitcast.17, bf16[4,16,256]{2,1,0:T(8,128)(2,1)S(1)} %get-tuple-element.17.counts, bf16[4096,1024]{1,0:T(8,128)(2,1)} %get-tuple-element.18.adj_hbm.adj, ...), custom_call_target="tpu_custom_call" | custom-call | tf_op jit(solution)/shard_map/aggregate_remote_0/pallas_call | solution.py:418
  86.7 0.0 collective-permute-done.2.refs_3_.refs_7_
  86.7 2.2 %collective-permute-done.refs_1_.refs_5_ = bf16[1040,256]{1,0:T(8,128)(2,1)S(1)} collective-permute-done((bf16[1040,256]{1,0:T(8,128)(2,1)S(1)}, bf16[1040,256]{1,0:T(8,128)(2,1)S(1)}, u32[]{:S(2)}, u32[]{:S(2)}) %collective-permute-start) | collective-permute-done | bytes 532512 | tf_op jit(solution)/shard_map/ppermute | solution.py:414
  88.9 0.0 collective-permute-done.1.refs_2_.refs_6_
  88.9 0.0 copy-done
  88.9 0.0 copy-done.5
  88.9 0.0 copy-done.7
  89.0 3.1 %dense_layer.1 = (bf16[1024,256]{1,0:T(8,128)(2,1)}, bf16[1024,256]{1,0:T(8,128)(2,1)}, bf16[1024,256]{1,0:T(8,128)(2,1)}) custom-call(bf16[1024,256]{1,0:T(8,128)(2,1)S(1)} %copy-done, bf16[1024,256]{1,0:T(8,128)(2,1)} %cots.1, bf16[256,256]{1,0:T(8,128)(2,1)S(1)} %copy-done.5, bf16[256,256]{1,0:T(8,128)(2,1)S(1)} %copy-done.7, ...), custom_call_target="tpu_custom_call" | custom-call | tf_op jit(solution)/shard_map/dense_layer/pallas_call | solution.py:461
  92.0 3.1 %collective-permute-start.5 = (bf16[1024,256]{1,0:T(8,128)(2,1)}, bf16[1024,256]{1,0:T(8,128)(2,1)S(1)}, u32[]{:S(2)}, u32[]{:S(2)}) collective-permute-start(bf16[1024,256]{1,0:T(8,128)(2,1)} %get-tuple-element.26.own.p0), channel_id=1, source_target_pairs={{0,1},{1,2},{2,3},{3,0},{4,5},{5,6},{6,7},{7,4},{8,9},{9,10},{10,1... | collective-permute-start | bytes 1572872 | tf_op jit(solution)/shard_map/ppermute | solution.py:414
  95.1 3.4 %collective-permute-start.3 = (bf16[1024,256]{1,0:T(8,128)(2,1)}, bf16[1024,256]{1,0:T(8,128)(2,1)S(1)}, u32[]{:S(2)}, u32[]{:S(2)}) collective-permute-start(bf16[1024,256]{1,0:T(8,128)(2,1)} %get-tuple-element.26.own.p0), channel_id=1, source_target_pairs={{0,3},{1,0},{2,1},{3,2},{4,7},{5,4},{6,5},{7,6},{8,11},{9,8},{10,9... | collective-permute-start | bytes 1572872 | tf_op jit(solution)/shard_map/ppermute | solution.py:414
  98.5 3.5 %collective-permute-start.4 = (bf16[1024,256]{1,0:T(8,128)(2,1)}, bf16[1024,256]{1,0:T(8,128)(2,1)S(1)}, u32[]{:S(2)}, u32[]{:S(2)}) collective-permute-start(bf16[1024,256]{1,0:T(8,128)(2,1)} %get-tuple-element.26.own.p0), channel_id=1, source_target_pairs={{0,2},{1,3},{2,0},{3,1},{4,6},{5,7},{6,4},{7,5},{8,10},{9,11},{10,... | collective-permute-start | bytes 1572872 | tf_op jit(solution)/shard_map/ppermute | solution.py:414
  102.0 6.5 %collective-permute-done.5.left.p1 = bf16[1024,256]{1,0:T(8,128)(2,1)S(1)} collective-permute-done((bf16[1024,256]{1,0:T(8,128)(2,1)}, bf16[1024,256]{1,0:T(8,128)(2,1)S(1)}, u32[]{:S(2)}, u32[]{:S(2)}) %collective-permute-start.5) | collective-permute-done | bytes 524320 | tf_op jit(solution)/shard_map/ppermute | solution.py:414
  108.5 1.0 copy-done.1
  109.5 1.8 %scatter_near.1.near = f32[1024,256]{1,0:T(8,128)S(1)} custom-call(s32[4]{0:T(128)S(1)} %and_select_fusion.owner_s, bf16[1024,256]{1,0:T(8,128)(2,1)S(1)} %copy-done.1, bf16[1024,256]{1,0:T(8,128)(2,1)S(1)} %collective-permute-done.5.left.p1, bf16[8,1024,512]{2,1,0:T(8,128)(2,1)S(1)} %adjacency_transposed.1.adj), custom_call_target="tpu_custom_call" | custom-call | tf_op jit(solution)/shard_map/scatter_near/pallas_call | solution.py:478
  111.3 0.0 copy-start.8
  111.3 0.0 copy-start.2
  111.4 0.0 collective-permute-done.3.right.p2
  111.4 7.9 %collective-permute-done.4.far.p3 = bf16[1024,256]{1,0:T(8,128)(2,1)S(1)} collective-permute-done((bf16[1024,256]{1,0:T(8,128)(2,1)}, bf16[1024,256]{1,0:T(8,128)(2,1)S(1)}, u32[]{:S(2)}, u32[]{:S(2)}) %collective-permute-start.4) | collective-permute-done | bytes 524320 | tf_op jit(solution)/shard_map/ppermute | solution.py:414
  119.3 2.6 %scatter_far.1 = bf16[1024,256]{1,0:T(8,128)(2,1)} custom-call(s32[4]{0:T(128)S(1)} %and_select_fusion.owner_s, bf16[1024,256]{1,0:T(8,128)(2,1)S(1)} %collective-permute-done.3.right.p2, bf16[1024,256]{1,0:T(8,128)(2,1)S(1)} %collective-permute-done.4.far.p3, f32[1024,256]{1,0:T(8,128)S(1)} %scatter_near.1.near, ...), custom_call_target="tpu_custom_call" | custom-call | tf_op jit(solution)/shard_map/scatter_far/pallas_call | solution.py:478
  121.9 0.0 copy-done.3
  121.9 11.4 %all-to-all-start.1 = ((bf16[128,8,256]{2,1,0:T(8,128)(2,1)}), bf16[128,8,256]{2,1,0:T(8,128)(2,1)S(1)}, u32[]{:S(2)}, u32[]{:S(2)}) async-start(bf16[128,8,256]{2,1,0:T(8,128)(2,1)} %bitcast.8), calls=%async_computation.1 | async-start | bytes 1048576 | tf_op jit(solution)/shard_map/all_to_all | solution.py:490
  133.3 0.0 copy-done.8
  133.3 0.1 copy.12
  133.4 0.1 reshape.47
  133.5 0.0 copy-done.2
  133.5 0.0 copy-start.4
  133.5 1.0 copy-done.4
  134.5 1.0 copy-done.6
  135.6 8.7 %scatter_local.1.kept = f32[1024,256]{1,0:T(8,128)S(1)} custom-call(s32[8192]{0:T(1024)S(1)} %get-tuple-element.16.keys_s, s32[1]{0:T(128)} %bitcast.14.active_s, s32[4]{0:T(128)S(1)} %and_select_fusion.owner_s, s32[64,1,128]{2,1,0:T(1,128)S(1)} %bitcast.20, bf16[1024,256]{1,0:T(8,128)(2,1)S(1)} %copy-done.6, bf16[256,256]{1,0:T(8,128)(2,1)S(1)} %copy-done.5, ...), custom_call_target="tpu_custom_call" | custom-call | tf_op jit(solution)/shard_map/scatter_local/pallas_call | solution.py:493
  144.3 22.6 %all-to-all-done.1 = bf16[128,8,256]{2,1,0:T(8,128)(2,1)S(1)} async-done(((bf16[128,8,256]{2,1,0:T(8,128)(2,1)}), bf16[128,8,256]{2,1,0:T(8,128)(2,1)S(1)}, u32[]{:S(2)}, u32[]{:S(2)}) %all-to-all-start.1) | async-done | bytes 524320 | tf_op jit(solution)/shard_map/all_to_all | solution.py:490
  166.9 1.6 combine.1
  (7 shorter events, 0.0 us)
Async XLA Ops:
  3.6 53.1 %all-to-all-start = ((bf16[128,8,256]{2,1,0:T(8,128)(2,1)}), bf16[128,8,256]{2,1,0:T(8,128)(2,1)S(1)}, u32[]{:S(2)}, u32[]{:S(2)}) async-start(bf16[128,8,256]{2,1,0:T(8,128)(2,1)} %pick_rows.1), calls=%async_computation | async-start | bytes 1048576 | tf_op jit(solution)/shard_map/all_to_all | solution.py:376
  60.1 26.7 %collective-permute-start.2 = (bf16[1040,256]{1,0:T(8,128)(2,1)S(1)}, bf16[1040,256]{1,0:T(8,128)(2,1)S(1)}, u32[]{:S(2)}, u32[]{:S(2)}) collective-permute-start(bf16[1040,256]{1,0:T(8,128)(2,1)S(1)} %aggregate_remote_2.1), channel_id=1, source_target_pairs={{0,2},{1,3},{2,0},{3,1},{4,6},{5,7},{6,4},{7,5},{8,10},{9,11},{10,... | collective-permute-start | bytes 1597448 | tf_op jit(solution)/shard_map/ppermute | solution.py:414
  69.9 19.0 %collective-permute-start = (bf16[1040,256]{1,0:T(8,128)(2,1)S(1)}, bf16[1040,256]{1,0:T(8,128)(2,1)S(1)}, u32[]{:S(2)}, u32[]{:S(2)}) collective-permute-start(bf16[1040,256]{1,0:T(8,128)(2,1)S(1)} %get-tuple-element.21), channel_id=1, source_target_pairs={{0,1},{1,2},{2,3},{3,0},{4,5},{5,6},{6,7},{7,4},{8,9},{9,10},{10,1... | collective-permute-start | bytes 1597448 | tf_op jit(solution)/shard_map/ppermute | solution.py:414
  72.1 11.1 %copy-start.9 = (bf16[256]{0:T(256)(128)(2,1)S(1)}, bf16[256]{0:T(256)(128)(2,1)}, u32[]{:S(2)}) copy-start(bf16[256]{0:T(256)(128)(2,1)} %param.13) | copy-start | bytes 1540
  72.2 16.8 %collective-permute-start.1 = (bf16[1040,256]{1,0:T(8,128)(2,1)S(1)}, bf16[1040,256]{1,0:T(8,128)(2,1)S(1)}, u32[]{:S(2)}, u32[]{:S(2)}) collective-permute-start(bf16[1040,256]{1,0:T(8,128)(2,1)S(1)} %get-tuple-element.23), channel_id=1, source_target_pairs={{0,3},{1,0},{2,1},{3,2},{4,7},{5,4},{6,5},{7,6},{8,11},{9,8},{10,9... | collective-permute-start | bytes 1597448 | tf_op jit(solution)/shard_map/ppermute | solution.py:414
  83.3 5.7 %copy-start = (bf16[1024,256]{1,0:T(8,128)(2,1)S(1)}, bf16[1024,256]{1,0:T(8,128)(2,1)}, u32[]{:S(2)}) copy-start(bf16[1024,256]{1,0:T(8,128)(2,1)} %feats.1) | copy-start | bytes 1572868
  83.3 5.7 %copy-start.5 = (bf16[256,256]{1,0:T(8,128)(2,1)S(1)}, bf16[256,256]{1,0:T(8,128)(2,1)}, u32[]{:S(2)}) copy-start(bf16[256,256]{1,0:T(8,128)(2,1)} %w_self.3) | copy-start | bytes 393220
  83.3 5.7 %copy-start.7 = (bf16[256,256]{1,0:T(8,128)(2,1)S(1)}, bf16[256,256]{1,0:T(8,128)(2,1)}, u32[]{:S(2)}) copy-start(bf16[256,256]{1,0:T(8,128)(2,1)} %w_neigh.1) | copy-start | bytes 393220
  92.0 16.5 %collective-permute-start.5 = (bf16[1024,256]{1,0:T(8,128)(2,1)}, bf16[1024,256]{1,0:T(8,128)(2,1)S(1)}, u32[]{:S(2)}, u32[]{:S(2)}) collective-permute-start(bf16[1024,256]{1,0:T(8,128)(2,1)} %get-tuple-element.26.own.p0), channel_id=1, source_target_pairs={{0,1},{1,2},{2,3},{3,0},{4,5},{5,6},{6,7},{7,4},{8,9},{9,10},{10,1... | collective-permute-start | bytes 1572872 | tf_op jit(solution)/shard_map/ppermute | solution.py:414
  95.1 16.2 %collective-permute-start.3 = (bf16[1024,256]{1,0:T(8,128)(2,1)}, bf16[1024,256]{1,0:T(8,128)(2,1)S(1)}, u32[]{:S(2)}, u32[]{:S(2)}) collective-permute-start(bf16[1024,256]{1,0:T(8,128)(2,1)} %get-tuple-element.26.own.p0), channel_id=1, source_target_pairs={{0,3},{1,0},{2,1},{3,2},{4,7},{5,4},{6,5},{7,6},{8,11},{9,8},{10,9... | collective-permute-start | bytes 1572872 | tf_op jit(solution)/shard_map/ppermute | solution.py:414
  98.5 20.8 %collective-permute-start.4 = (bf16[1024,256]{1,0:T(8,128)(2,1)}, bf16[1024,256]{1,0:T(8,128)(2,1)S(1)}, u32[]{:S(2)}, u32[]{:S(2)}) collective-permute-start(bf16[1024,256]{1,0:T(8,128)(2,1)} %get-tuple-element.26.own.p0), channel_id=1, source_target_pairs={{0,2},{1,3},{2,0},{3,1},{4,6},{5,7},{6,4},{7,5},{8,10},{9,11},{10,... | collective-permute-start | bytes 1572872 | tf_op jit(solution)/shard_map/ppermute | solution.py:414
  108.5 1.0 copy-start.1
  109.5 12.3 %copy-start.3 = (bf16[1024,256]{1,0:T(8,128)(2,1)}, bf16[1024,256]{1,0:T(8,128)(2,1)S(1)}, u32[]{:S(2)}) copy-start(bf16[1024,256]{1,0:T(8,128)(2,1)S(1)} %collective-permute-done.5.left.p1) | copy-start | bytes 1572868
  111.3 21.9 %copy-start.8 = (s32[1,1,128,8]{2,3,1,0:T(8,128)S(1)}, s32[1,1,128,8]{2,3,1,0:T(8,128)}, u32[]{:S(2)}) copy-start(s32[1,1,128,8]{2,3,1,0:T(8,128)} %param.14) | copy-start | bytes 12292
  111.3 22.1 %copy-start.2 = (bf16[1024,256]{1,0:T(8,128)(2,1)S(1)}, bf16[1024,256]{1,0:T(8,128)(2,1)}, u32[]{:S(2)}) copy-start(bf16[1024,256]{1,0:T(8,128)(2,1)} %get-tuple-element.26.own.p0) | copy-start | bytes 1572868
  121.9 45.0 %all-to-all-start.1 = ((bf16[128,8,256]{2,1,0:T(8,128)(2,1)}), bf16[128,8,256]{2,1,0:T(8,128)(2,1)S(1)}, u32[]{:S(2)}, u32[]{:S(2)}) async-start(bf16[128,8,256]{2,1,0:T(8,128)(2,1)} %bitcast.8), calls=%async_computation.1 | async-start | bytes 1048576 | tf_op jit(solution)/shard_map/all_to_all | solution.py:490
  133.5 1.0 copy-start.4
  134.5 1.0 copy-start.6

commit v7 on v6

--- a/solution.py
+++ b/solution.py
@@ -225,12 +225,29 @@
             out[h * FINE : h * FINE + FINE, :] = total.astype(BF16)
 
 
-def pick_kernel(senders, table, out, acc):
-    for c in range(8):
-        col = key_column(senders[c : c + 1, :])
-        pick = jnp.concatenate([one_hot(col == iota((128, 128), 1) + 128 * k) for k in range(ROWS // 128)], axis=1)
-        acc[:, c, :] = jnp.dot(pick, table[...], preferred_element_type=F32)
-    out[...] = acc[...].astype(BF16)
+def pick_kernel(senders, table_hbm, out_hbm, table, out, acc, sems):
+    load = pltpu.make_async_copy(table_hbm, table, sems.at[0])
+    load.start()
+    cols = [key_column(senders[c : c + 1, :]) for c in range(8)]
+    saves = []
+    for h in range(2):
+        peers = slice(64 * h, 64 * h + 64)
+        picks = [
+            jnp.concatenate([one_hot(col[peers] == iota((64, 128), 1) + 128 * k) for k in range(ROWS // 128)], axis=1)
+            for col in cols
+        ]
+        pick = jnp.concatenate(picks, axis=0)
+        if h == 0:
+            load.wait()
+        got = jnp.dot(pick, table[...], preferred_element_type=F32)
+        for c in range(8):
+            acc[peers, c, :] = got[64 * c : 64 * c + 64]
+        out[peers] = acc[peers].astype(BF16)
+        half = pl.ds(64 * h, 64)
+        saves.append(pltpu.make_async_copy(out.at[half], out_hbm.at[half], sems.at[1 + h]))
+        saves[h].start()
+    for copy in saves:
+        copy.wait()
 
 
 def combine_kernel(senders, returned, kept, out_hbm, out, sems):
@@ -363,14 +380,16 @@
     picked = pl.pallas_call(
         pick_kernel,
         grid=(1,),
-        in_specs=[
-            pl.BlockSpec((capacity, peers), lambda i: (0, 0)),
-            pl.BlockSpec((ROWS, WIDTH), lambda i: (0, 0)),
+        in_specs=[pl.BlockSpec((capacity, peers), lambda i: (0, 0)), HBM],
+        out_specs=HBM,
+        out_shape=pltpu.HBM((peers, capacity, WIDTH), BF16),
+        scratch_shapes=[
+            pltpu.VMEM((ROWS, WIDTH), BF16),
+            pltpu.VMEM((peers, capacity, WIDTH), BF16),
+            pltpu.VMEM((peers, capacity, WIDTH), F32),
+            pltpu.SemaphoreType.DMA((3,)),
         ],
-        out_specs=pl.BlockSpec((peers, capacity, WIDTH), lambda i: (0, 0, 0)),
-        out_shape=shape((peers, capacity, WIDTH), BF16),
-        scratch_shapes=[pltpu.VMEM((peers, capacity, WIDTH), F32)],
-        compiler_params=params(8),
+        compiler_params=params(12),
         name="pick_rows",
     )(in_hbm(jnp.transpose(send_rows.reshape(peers, capacity))), in_hbm(features))
     remote = lax.all_to_all(picked, "dom", split_axis=0, concat_axis=0, tiled=True).reshape(peers * capacity, WIDTH)

time: 169 us -> 172 us (1.018)
  starting transfers between devices: 52 us -> 54 us
  Pallas kernels: 54.7 us -> 56.5 us
    all_to_all x1, starting transfers between devices: 11.4 us -> 13.4 us  [local(): lax.all_to_all(outgoing.reshape(peers, capacity, WIDTH), 'dom', split_axi...]
  transfers between devices with their start and end apart: 8 -> 8, of which waited for: 5 -> 5; matrix products, arithmetic and copies ran while one was open for 5% -> 5% of each run, Pallas kernels for 24% -> 25%
where the time goes in v7:
time: 172 us; the launch traced here: 171 us
  Pallas kernels  56.5 us (33%)
  starting transfers between devices  54 us (31%)
  waiting for transfers between devices  48.1 us (28%)
  other arithmetic  7.63 us (4%)
  local copies, waits for them, and re-layouts  3.36 us (2%)
    all_to_all x1, waiting for transfers between devices, local(): lax.all_to_all(outgoing.reshape(peers, capacity, WIDTH), 'dom', split_axi...  21.6 us
    ppermute x6, starting transfers between devices, shifted(): return lax.ppermute(x, 'src', [(j, (j + k) % 4) for j in range(4)])  21.1 us
    all_to_all x1, starting transfers between devices, local(): lax.all_to_all(picked, 'dom', split_axis=0, concat_axis=0, tiled=True)  19.5 us
    ppermute x6, waiting for transfers between devices, shifted(): return lax.ppermute(x, 'src', [(j, (j + k) % 4) for j in range(4)])  16.6 us
    pallas_call x1, Pallas kernels, local(): pl.pallas_call(prepare_kernel, grid_spec=pltpu.PrefetchScalarGridSpec(num...  15.5 us
    all_to_all x1, starting transfers between devices, local(): lax.all_to_all(outgoing.reshape(peers, capacity, WIDTH), 'dom', split_axi...  13.4 us
    pallas_call x3, Pallas kernels, partials(): pl.pallas_call(functools.partial(forward_remote_kernel, shifts), grid_spe...  12 us
    all_to_all x1, waiting for transfers between devices, local(): lax.all_to_all(picked, 'dom', split_axis=0, concat_axis=0, tiled=True)  9.8 us
  transfers between devices with their start and end apart: 8, of which 5 were waited for; matrix products, arithmetic and copies ran while one was open for 5% of the time, Pallas kernels for 25%

profile of v7, /device:TPU:33, one launch (start us, length us, event | category | flops | bytes accessed | tf_op | source)
XLA Modules:
  0.0 171.3 jit_solution(11986142879185682084)
XLA Ops:
  0.6 3.5 %pick_rows.1 = bf16[128,8,256]{2,1,0:T(8,128)(2,1)} custom-call(s32[8,128]{1,0:T(8,128)} %bitcast.23, bf16[1024,256]{1,0:T(8,128)(2,1)} %feats.1), custom_call_target="tpu_custom_call" | custom-call | tf_op jit(solution)/shard_map/pick_rows/pallas_call | solution.py:380
  4.2 19.5 %all-to-all-start = ((bf16[128,8,256]{2,1,0:T(8,128)(2,1)}), bf16[128,8,256]{2,1,0:T(8,128)(2,1)S(1)}, u32[]{:S(2)}, u32[]{:S(2)}) async-start(bf16[128,8,256]{2,1,0:T(8,128)(2,1)} %pick_rows.1), calls=%async_computation | async-start | bytes 1048576 | tf_op jit(solution)/shard_map/all_to_all | solution.py:395
  24.3 0.8 and_add_fusion
  25.2 6.8 %sort.10 = (s32[8192]{0:T(1024)S(1)}, s32[8192]{0:T(1024)}) sort(s32[8192]{0:T(1024)S(1)} %fusion, s32[8192]{0:T(1024)S(1)} %iota.11), dimensions={0}, to_apply=%region_0.1 | sort | flops 106496 | bytes 131072 | tf_op jit(solution)/shard_map/sort | solution.py:402
  32.0 15.5 %prepare.1 = (bf16[4096,1024]{1,0:T(8,128)(2,1)}, f32[4096,256]{1,0:T(8,128)}, bf16[4,16,256]{2,1,0:T(8,128)(2,1)S(1)}) custom-call(s32[8192]{0:T(1024)S(1)} %get-tuple-element.16.keys_s, s32[1]{0:T(128)} %bitcast.13.active_s, s32[64,1,128]{2,1,0:T(1,128)S(1)} %bitcast.19, bf16[1024,256]{1,0:T(8,128)(2,1)} %feats.1), custom_call_target="tpu_custom_call" | custom-call | tf_op jit(solution)/shard_map/prepare/pallas_call | solution.py:405
  47.5 9.8 %all-to-all-done = bf16[128,8,256]{2,1,0:T(8,128)(2,1)S(1)} async-done(((bf16[128,8,256]{2,1,0:T(8,128)(2,1)}), bf16[128,8,256]{2,1,0:T(8,128)(2,1)S(1)}, u32[]{:S(2)}, u32[]{:S(2)}) %all-to-all-start) | async-done | bytes 524320 | tf_op jit(solution)/shard_map/all_to_all | solution.py:395
  57.3 3.4 %aggregate_remote_2.1 = bf16[1040,256]{1,0:T(8,128)(2,1)S(1)} custom-call(s32[4]{0:T(128)S(1)} %and_select_fusion.owner_s, bf16[1024,256]{1,0:T(8,128)(2,1)S(1)} %bitcast.15, bf16[4,16,256]{2,1,0:T(8,128)(2,1)S(1)} %get-tuple-element.17.counts, bf16[4096,1024]{1,0:T(8,128)(2,1)} %get-tuple-element.18.adj_hbm.adj, f32[4096,256]{1,0:T(8,128)} %get-tuple-element.19.local_hbm), custom_call_target="tpu_custom_call" | custom-call | tf_op jit(solution)/shard_map/aggregate_remote_2/pallas_call | solution.py:437
  60.7 4.6 %collective-permute-start.2 = (bf16[1040,256]{1,0:T(8,128)(2,1)S(1)}, bf16[1040,256]{1,0:T(8,128)(2,1)S(1)}, u32[]{:S(2)}, u32[]{:S(2)}) collective-permute-start(bf16[1040,256]{1,0:T(8,128)(2,1)S(1)} %aggregate_remote_2.1), channel_id=1, source_target_pairs={{0,2},{1,3},{2,0},{3,1},{4,6},{5,7},{6,4},{7,5},{8,10},{9,11},{10,... | collective-permute-start | bytes 1597448 | tf_op jit(solution)/shard_map/ppermute | solution.py:433
  65.3 5.2 %aggregate_remote_1_3.1 = (bf16[1040,256]{1,0:T(8,128)(2,1)S(1)}, bf16[1040,256]{1,0:T(8,128)(2,1)S(1)}) custom-call(s32[4]{0:T(128)S(1)} %and_select_fusion.owner_s, bf16[1024,256]{1,0:T(8,128)(2,1)S(1)} %bitcast.16, bf16[4,16,256]{2,1,0:T(8,128)(2,1)S(1)} %get-tuple-element.17.counts, bf16[4096,1024]{1,0:T(8,128)(2,1)} %get-tuple-element.18.adj_hbm.adj, ...), custom_call_target="tpu_custom_call" | custom-call | tf_op jit(solution)/shard_map/aggregate_remote_1_3/pallas_call | solution.py:437
  70.5 2.2 %collective-permute-start = (bf16[1040,256]{1,0:T(8,128)(2,1)S(1)}, bf16[1040,256]{1,0:T(8,128)(2,1)S(1)}, u32[]{:S(2)}, u32[]{:S(2)}) collective-permute-start(bf16[1040,256]{1,0:T(8,128)(2,1)S(1)} %get-tuple-element.21), channel_id=1, source_target_pairs={{0,1},{1,2},{2,3},{3,0},{4,5},{5,6},{6,7},{7,4},{8,9},{9,10},{10,1... | collective-permute-start | bytes 1597448 | tf_op jit(solution)/shard_map/ppermute | solution.py:433
  72.8 0.0 copy-start.9
  72.8 4.3 %collective-permute-start.1 = (bf16[1040,256]{1,0:T(8,128)(2,1)S(1)}, bf16[1040,256]{1,0:T(8,128)(2,1)S(1)}, u32[]{:S(2)}, u32[]{:S(2)}) collective-permute-start(bf16[1040,256]{1,0:T(8,128)(2,1)S(1)} %get-tuple-element.23), channel_id=1, source_target_pairs={{0,3},{1,0},{2,1},{3,2},{4,7},{5,4},{6,5},{7,6},{8,11},{9,8},{10,9... | collective-permute-start | bytes 1597448 | tf_op jit(solution)/shard_map/ppermute | solution.py:433
  77.1 6.8 %adjacency_transposed.1.adj = bf16[8,1024,512]{2,1,0:T(8,128)(2,1)S(1)} custom-call(bf16[4096,1024]{1,0:T(8,128)(2,1)} %get-tuple-element.18.adj_hbm.adj), custom_call_target="tpu_custom_call" | custom-call | tf_op jit(solution)/shard_map/adjacency_transposed/pallas_call | solution.py:464
  83.9 0.0 copy-done.9
  83.9 0.0 copy-start
  83.9 0.0 copy-start.5
  83.9 0.0 copy-start.7
  83.9 3.4 %aggregate_remote_0.1.refs_0_.refs_4_ = bf16[1040,256]{1,0:T(8,128)(2,1)S(1)} custom-call(s32[4]{0:T(128)S(1)} %and_select_fusion.owner_s, bf16[1024,256]{1,0:T(8,128)(2,1)S(1)} %bitcast.17, bf16[4,16,256]{2,1,0:T(8,128)(2,1)S(1)} %get-tuple-element.17.counts, bf16[4096,1024]{1,0:T(8,128)(2,1)} %get-tuple-element.18.adj_hbm.adj, ...), custom_call_target="tpu_custom_call" | custom-call | tf_op jit(solution)/shard_map/aggregate_remote_0/pallas_call | solution.py:437
  87.3 0.0 collective-permute-done.2.refs_3_.refs_7_
  87.4 2.2 %collective-permute-done.refs_1_.refs_5_ = bf16[1040,256]{1,0:T(8,128)(2,1)S(1)} collective-permute-done((bf16[1040,256]{1,0:T(8,128)(2,1)S(1)}, bf16[1040,256]{1,0:T(8,128)(2,1)S(1)}, u32[]{:S(2)}, u32[]{:S(2)}) %collective-permute-start) | collective-permute-done | bytes 532512 | tf_op jit(solution)/shard_map/ppermute | solution.py:433
  89.5 0.0 collective-permute-done.1.refs_2_.refs_6_
  89.6 0.0 copy-done
  89.6 0.0 copy-done.5
  89.6 0.0 copy-done.7
  89.6 3.1 %dense_layer.1 = (bf16[1024,256]{1,0:T(8,128)(2,1)}, bf16[1024,256]{1,0:T(8,128)(2,1)}, bf16[1024,256]{1,0:T(8,128)(2,1)}) custom-call(bf16[1024,256]{1,0:T(8,128)(2,1)S(1)} %copy-done, bf16[1024,256]{1,0:T(8,128)(2,1)} %cots.1, bf16[256,256]{1,0:T(8,128)(2,1)S(1)} %copy-done.5, bf16[256,256]{1,0:T(8,128)(2,1)S(1)} %copy-done.7, ...), custom_call_target="tpu_custom_call" | custom-call | tf_op jit(solution)/shard_map/dense_layer/pallas_call | solution.py:480
  92.6 3.1 %collective-permute-start.5 = (bf16[1024,256]{1,0:T(8,128)(2,1)}, bf16[1024,256]{1,0:T(8,128)(2,1)S(1)}, u32[]{:S(2)}, u32[]{:S(2)}) collective-permute-start(bf16[1024,256]{1,0:T(8,128)(2,1)} %get-tuple-element.26.own.p0), channel_id=1, source_target_pairs={{0,1},{1,2},{2,3},{3,0},{4,5},{5,6},{6,7},{7,4},{8,9},{9,10},{10,1... | collective-permute-start | bytes 1572872 | tf_op jit(solution)/shard_map/ppermute | solution.py:433
  95.7 3.4 %collective-permute-start.3 = (bf16[1024,256]{1,0:T(8,128)(2,1)}, bf16[1024,256]{1,0:T(8,128)(2,1)S(1)}, u32[]{:S(2)}, u32[]{:S(2)}) collective-permute-start(bf16[1024,256]{1,0:T(8,128)(2,1)} %get-tuple-element.26.own.p0), channel_id=1, source_target_pairs={{0,3},{1,0},{2,1},{3,2},{4,7},{5,4},{6,5},{7,6},{8,11},{9,8},{10,9... | collective-permute-start | bytes 1572872 | tf_op jit(solution)/shard_map/ppermute | solution.py:433
  99.1 3.5 %collective-permute-start.4 = (bf16[1024,256]{1,0:T(8,128)(2,1)}, bf16[1024,256]{1,0:T(8,128)(2,1)S(1)}, u32[]{:S(2)}, u32[]{:S(2)}) collective-permute-start(bf16[1024,256]{1,0:T(8,128)(2,1)} %get-tuple-element.26.own.p0), channel_id=1, source_target_pairs={{0,2},{1,3},{2,0},{3,1},{4,6},{5,7},{6,4},{7,5},{8,10},{9,11},{10,... | collective-permute-start | bytes 1572872 | tf_op jit(solution)/shard_map/ppermute | solution.py:433
  102.6 6.5 %collective-permute-done.5.left.p1 = bf16[1024,256]{1,0:T(8,128)(2,1)S(1)} collective-permute-done((bf16[1024,256]{1,0:T(8,128)(2,1)}, bf16[1024,256]{1,0:T(8,128)(2,1)S(1)}, u32[]{:S(2)}, u32[]{:S(2)}) %collective-permute-start.5) | collective-permute-done | bytes 524320 | tf_op jit(solution)/shard_map/ppermute | solution.py:433
  109.1 1.0 copy-done.1
  110.2 1.8 %scatter_near.1.near = f32[1024,256]{1,0:T(8,128)S(1)} custom-call(s32[4]{0:T(128)S(1)} %and_select_fusion.owner_s, bf16[1024,256]{1,0:T(8,128)(2,1)S(1)} %copy-done.1, bf16[1024,256]{1,0:T(8,128)(2,1)S(1)} %collective-permute-done.5.left.p1, bf16[8,1024,512]{2,1,0:T(8,128)(2,1)S(1)} %adjacency_transposed.1.adj), custom_call_target="tpu_custom_call" | custom-call | tf_op jit(solution)/shard_map/scatter_near/pallas_call | solution.py:497
  112.0 0.0 copy-start.8
  112.0 0.0 copy-start.2
  112.0 0.0 collective-permute-done.3.right.p2
  112.0 7.9 %collective-permute-done.4.far.p3 = bf16[1024,256]{1,0:T(8,128)(2,1)S(1)} collective-permute-done((bf16[1024,256]{1,0:T(8,128)(2,1)}, bf16[1024,256]{1,0:T(8,128)(2,1)S(1)}, u32[]{:S(2)}, u32[]{:S(2)}) %collective-permute-start.4) | collective-permute-done | bytes 524320 | tf_op jit(solution)/shard_map/ppermute | solution.py:433
  119.9 2.6 %scatter_far.1 = bf16[1024,256]{1,0:T(8,128)(2,1)} custom-call(s32[4]{0:T(128)S(1)} %and_select_fusion.owner_s, bf16[1024,256]{1,0:T(8,128)(2,1)S(1)} %collective-permute-done.3.right.p2, bf16[1024,256]{1,0:T(8,128)(2,1)S(1)} %collective-permute-done.4.far.p3, f32[1024,256]{1,0:T(8,128)S(1)} %scatter_near.1.near, ...), custom_call_target="tpu_custom_call" | custom-call | tf_op jit(solution)/shard_map/scatter_far/pallas_call | solution.py:497
  122.5 0.0 copy-done.3
  122.5 13.4 %all-to-all-start.1 = ((bf16[128,8,256]{2,1,0:T(8,128)(2,1)}), bf16[128,8,256]{2,1,0:T(8,128)(2,1)S(1)}, u32[]{:S(2)}, u32[]{:S(2)}) async-start(bf16[128,8,256]{2,1,0:T(8,128)(2,1)} %bitcast.8), calls=%async_computation.1 | async-start | bytes 1048576 | tf_op jit(solution)/shard_map/all_to_all | solution.py:509
  135.9 0.0 copy-done.8
  136.0 0.1 copy.12
  136.1 0.1 reshape.47
  136.2 0.0 copy-done.2
  136.2 0.0 copy-start.4
  136.2 1.0 copy-done.4
  137.2 1.0 copy-done.6
  138.2 9.7 %scatter_local.1.kept = f32[1024,256]{1,0:T(8,128)S(1)} custom-call(s32[8192]{0:T(1024)S(1)} %get-tuple-element.16.keys_s, s32[1]{0:T(128)} %bitcast.14.active_s, s32[4]{0:T(128)S(1)} %and_select_fusion.owner_s, s32[64,1,128]{2,1,0:T(1,128)S(1)} %bitcast.20, bf16[1024,256]{1,0:T(8,128)(2,1)S(1)} %copy-done.6, bf16[256,256]{1,0:T(8,128)(2,1)S(1)} %copy-done.5, ...), custom_call_target="tpu_custom_call" | custom-call | tf_op jit(solution)/shard_map/scatter_local/pallas_call | solution.py:512
  147.9 21.6 %all-to-all-done.1 = bf16[128,8,256]{2,1,0:T(8,128)(2,1)S(1)} async-done(((bf16[128,8,256]{2,1,0:T(8,128)(2,1)}), bf16[128,8,256]{2,1,0:T(8,128)(2,1)S(1)}, u32[]{:S(2)}, u32[]{:S(2)}) %all-to-all-start.1) | async-done | bytes 524320 | tf_op jit(solution)/shard_map/all_to_all | solution.py:509
  169.5 1.6 combine.1
  (7 shorter events, 0.0 us)
Async XLA Ops:
  4.2 53.1 %all-to-all-start = ((bf16[128,8,256]{2,1,0:T(8,128)(2,1)}), bf16[128,8,256]{2,1,0:T(8,128)(2,1)S(1)}, u32[]{:S(2)}, u32[]{:S(2)}) async-start(bf16[128,8,256]{2,1,0:T(8,128)(2,1)} %pick_rows.1), calls=%async_computation | async-start | bytes 1048576 | tf_op jit(solution)/shard_map/all_to_all | solution.py:395
  60.7 26.7 %collective-permute-start.2 = (bf16[1040,256]{1,0:T(8,128)(2,1)S(1)}, bf16[1040,256]{1,0:T(8,128)(2,1)S(1)}, u32[]{:S(2)}, u32[]{:S(2)}) collective-permute-start(bf16[1040,256]{1,0:T(8,128)(2,1)S(1)} %aggregate_remote_2.1), channel_id=1, source_target_pairs={{0,2},{1,3},{2,0},{3,1},{4,6},{5,7},{6,4},{7,5},{8,10},{9,11},{10,... | collective-permute-start | bytes 1597448 | tf_op jit(solution)/shard_map/ppermute | solution.py:433
  70.5 19.0 %collective-permute-start = (bf16[1040,256]{1,0:T(8,128)(2,1)S(1)}, bf16[1040,256]{1,0:T(8,128)(2,1)S(1)}, u32[]{:S(2)}, u32[]{:S(2)}) collective-permute-start(bf16[1040,256]{1,0:T(8,128)(2,1)S(1)} %get-tuple-element.21), channel_id=1, source_target_pairs={{0,1},{1,2},{2,3},{3,0},{4,5},{5,6},{6,7},{7,4},{8,9},{9,10},{10,1... | collective-permute-start | bytes 1597448 | tf_op jit(solution)/shard_map/ppermute | solution.py:433
  72.8 11.1 %copy-start.9 = (bf16[256]{0:T(256)(128)(2,1)S(1)}, bf16[256]{0:T(256)(128)(2,1)}, u32[]{:S(2)}) copy-start(bf16[256]{0:T(256)(128)(2,1)} %param.13) | copy-start | bytes 1540
  72.8 16.8 %collective-permute-start.1 = (bf16[1040,256]{1,0:T(8,128)(2,1)S(1)}, bf16[1040,256]{1,0:T(8,128)(2,1)S(1)}, u32[]{:S(2)}, u32[]{:S(2)}) collective-permute-start(bf16[1040,256]{1,0:T(8,128)(2,1)S(1)} %get-tuple-element.23), channel_id=1, source_target_pairs={{0,3},{1,0},{2,1},{3,2},{4,7},{5,4},{6,5},{7,6},{8,11},{9,8},{10,9... | collective-permute-start | bytes 1597448 | tf_op jit(solution)/shard_map/ppermute | solution.py:433
  83.9 5.7 %copy-start = (bf16[1024,256]{1,0:T(8,128)(2,1)S(1)}, bf16[1024,256]{1,0:T(8,128)(2,1)}, u32[]{:S(2)}) copy-start(bf16[1024,256]{1,0:T(8,128)(2,1)} %feats.1) | copy-start | bytes 1572868
  83.9 5.7 %copy-start.5 = (bf16[256,256]{1,0:T(8,128)(2,1)S(1)}, bf16[256,256]{1,0:T(8,128)(2,1)}, u32[]{:S(2)}) copy-start(bf16[256,256]{1,0:T(8,128)(2,1)} %w_self.3) | copy-start | bytes 393220
  83.9 5.7 %copy-start.7 = (bf16[256,256]{1,0:T(8,128)(2,1)S(1)}, bf16[256,256]{1,0:T(8,128)(2,1)}, u32[]{:S(2)}) copy-start(bf16[256,256]{1,0:T(8,128)(2,1)} %w_neigh.1) | copy-start | bytes 393220
  92.6 16.5 %collective-permute-start.5 = (bf16[1024,256]{1,0:T(8,128)(2,1)}, bf16[1024,256]{1,0:T(8,128)(2,1)S(1)}, u32[]{:S(2)}, u32[]{:S(2)}) collective-permute-start(bf16[1024,256]{1,0:T(8,128)(2,1)} %get-tuple-element.26.own.p0), channel_id=1, source_target_pairs={{0,1},{1,2},{2,3},{3,0},{4,5},{5,6},{6,7},{7,4},{8,9},{9,10},{10,1... | collective-permute-start | bytes 1572872 | tf_op jit(solution)/shard_map/ppermute | solution.py:433
  95.7 16.2 %collective-permute-start.3 = (bf16[1024,256]{1,0:T(8,128)(2,1)}, bf16[1024,256]{1,0:T(8,128)(2,1)S(1)}, u32[]{:S(2)}, u32[]{:S(2)}) collective-permute-start(bf16[1024,256]{1,0:T(8,128)(2,1)} %get-tuple-element.26.own.p0), channel_id=1, source_target_pairs={{0,3},{1,0},{2,1},{3,2},{4,7},{5,4},{6,5},{7,6},{8,11},{9,8},{10,9... | collective-permute-start | bytes 1572872 | tf_op jit(solution)/shard_map/ppermute | solution.py:433
  99.1 20.8 %collective-permute-start.4 = (bf16[1024,256]{1,0:T(8,128)(2,1)}, bf16[1024,256]{1,0:T(8,128)(2,1)S(1)}, u32[]{:S(2)}, u32[]{:S(2)}) collective-permute-start(bf16[1024,256]{1,0:T(8,128)(2,1)} %get-tuple-element.26.own.p0), channel_id=1, source_target_pairs={{0,2},{1,3},{2,0},{3,1},{4,6},{5,7},{6,4},{7,5},{8,10},{9,11},{10,... | collective-permute-start | bytes 1572872 | tf_op jit(solution)/shard_map/ppermute | solution.py:433
  109.1 1.0 copy-start.1
  110.2 12.3 %copy-start.3 = (bf16[1024,256]{1,0:T(8,128)(2,1)}, bf16[1024,256]{1,0:T(8,128)(2,1)S(1)}, u32[]{:S(2)}) copy-start(bf16[1024,256]{1,0:T(8,128)(2,1)S(1)} %collective-permute-done.5.left.p1) | copy-start | bytes 1572868
  112.0 24.0 %copy-start.8 = (s32[1,1,128,8]{2,3,1,0:T(8,128)S(1)}, s32[1,1,128,8]{2,3,1,0:T(8,128)}, u32[]{:S(2)}) copy-start(s32[1,1,128,8]{2,3,1,0:T(8,128)} %param.14) | copy-start | bytes 12292
  112.0 24.2 %copy-start.2 = (bf16[1024,256]{1,0:T(8,128)(2,1)S(1)}, bf16[1024,256]{1,0:T(8,128)(2,1)}, u32[]{:S(2)}) copy-start(bf16[1024,256]{1,0:T(8,128)(2,1)} %get-tuple-element.26.own.p0) | copy-start | bytes 1572868
  122.5 47.0 %all-to-all-start.1 = ((bf16[128,8,256]{2,1,0:T(8,128)(2,1)}), bf16[128,8,256]{2,1,0:T(8,128)(2,1)S(1)}, u32[]{:S(2)}, u32[]{:S(2)}) async-start(bf16[128,8,256]{2,1,0:T(8,128)(2,1)} %bitcast.8), calls=%async_computation.1 | async-start | bytes 1048576 | tf_op jit(solution)/shard_map/all_to_all | solution.py:509
  136.2 1.0 copy-start.4
  137.2 1.0 copy-start.6

commit v8 on v6

--- a/solution.py
+++ b/solution.py
@@ -164,11 +164,14 @@
     tiles(lo, hi, tile)
 
 
-def prepare_kernel(keys_s, active_s, keys_v, table_hbm, adj_out, local_out, counts, adj, acc, table, sems):
+def prepare_kernel(active_s, keys_any, keys_v, table_hbm, adj_out, local_out, counts, adj, acc, table, keys_s, sems):
+    scalars = pltpu.make_async_copy(keys_any, keys_s, sems.at[3])
+    scalars.start()
     load = pltpu.make_async_copy(table_hbm, table, sems.at[2])
     load.start()
+    adj[...] = jnp.zeros_like(adj)
+    scalars.wait()
     boundary = local_edges(keys_s)
-    adj[...] = jnp.zeros_like(adj)
     build_adjacency(keys_s, keys_v, adj, boundary, active_s[0] * 128)
     save_adj = pltpu.make_async_copy(adj.at[pl.ds(0, PART), :], adj_out, sems.at[0])
     save_adj.start()
@@ -386,15 +389,16 @@
     adj, before, counts = pl.pallas_call(
         prepare_kernel,
         grid_spec=pltpu.PrefetchScalarGridSpec(
-            num_scalar_prefetch=2,
+            num_scalar_prefetch=1,
             grid=(),
-            in_specs=[VMEM, HBM],
+            in_specs=[ANY, VMEM, HBM],
             out_specs=(HBM, HBM, VMEM),
             scratch_shapes=[
                 pltpu.VMEM((PADDED, ROWS), BF16),
                 pltpu.VMEM((PADDED, WIDTH), F32),
                 pltpu.VMEM((ROWS, WIDTH), BF16),
-                pltpu.SemaphoreType.DMA((3,)),
+                pltpu.SMEM((EDGES,), jnp.int32),
+                pltpu.SemaphoreType.DMA((4,)),
             ],
         ),
         out_shape=(
@@ -404,7 +408,7 @@
         ),
         compiler_params=params(30),
         name="prepare",
-    )(keys_s, active, keys_v, in_hbm(features))
+    )(active, keys_s, keys_v, in_hbm(features))
     chunks = PART // CHUNK
     rank = lax.axis_index("src")
 

time: 169 us -> 170 us (level)
  the two profiles are of different devices: /device:TPU:33 before, /device:TPU:35 now
where the time goes in v8:
time: 170 us; the launch traced here: 169 us
  Pallas kernels  55.8 us (33%)
  waiting for transfers between devices  52.9 us (31%)
  starting transfers between devices  47.3 us (28%)
  other arithmetic  7.63 us (4%)
  local copies, waits for them, and re-layouts  3.36 us (2%)
    all_to_all x1, waiting for transfers between devices, local(): lax.all_to_all(outgoing.reshape(peers, capacity, WIDTH), 'dom', split_axi...  22.6 us
    ppermute x6, waiting for transfers between devices, shifted(): return lax.ppermute(x, 'src', [(j, (j + k) % 4) for j in range(4)])  21.4 us
    all_to_all x1, starting transfers between devices, local(): lax.all_to_all(picked, 'dom', split_axis=0, concat_axis=0, tiled=True)  19.5 us
    ppermute x6, starting transfers between devices, shifted(): return lax.ppermute(x, 'src', [(j, (j + k) % 4) for j in range(4)])  17.6 us
    pallas_call x1, Pallas kernels, local(): pl.pallas_call(prepare_kernel, grid_spec=pltpu.PrefetchScalarGridSpec(num...  16.4 us
    pallas_call x3, Pallas kernels, partials(): pl.pallas_call(functools.partial(forward_remote_kernel, shifts), grid_spe...  12 us
    all_to_all x1, starting transfers between devices, local(): lax.all_to_all(outgoing.reshape(peers, capacity, WIDTH), 'dom', split_axi...  10.2 us
    all_to_all x1, waiting for transfers between devices, local(): lax.all_to_all(picked, 'dom', split_axis=0, concat_axis=0, tiled=True)  8.87 us
  transfers between devices with their start and end apart: 8, of which 7 were waited for; matrix products, arithmetic and copies ran while one was open for 5% of the time, Pallas kernels for 25%

profile of v8, /device:TPU:35, one launch (start us, length us, event | category | flops | bytes accessed | tf_op | source)
XLA Modules:
  0.0 168.7 jit_solution(1546265637432908193)
XLA Ops:
  0.6 2.9 %pick_rows.1 = bf16[128,8,256]{2,1,0:T(8,128)(2,1)} custom-call(s32[8,128]{1,0:T(8,128)} %bitcast.23, bf16[1024,256]{1,0:T(8,128)(2,1)} %feats.1), custom_call_target="tpu_custom_call" | custom-call | tf_op jit(solution)/shard_map/pick_rows/pallas_call | solution.py:366
  3.6 19.5 %all-to-all-start = ((bf16[128,8,256]{2,1,0:T(8,128)(2,1)}), bf16[128,8,256]{2,1,0:T(8,128)(2,1)S(1)}, u32[]{:S(2)}, u32[]{:S(2)}) async-start(bf16[128,8,256]{2,1,0:T(8,128)(2,1)} %pick_rows.1), calls=%async_computation | async-start | bytes 1048576 | tf_op jit(solution)/shard_map/all_to_all | solution.py:379
  23.7 0.8 and_add_fusion
  24.6 6.8 %sort.10 = (s32[8192]{0:T(1024)S(1)}, s32[8192]{0:T(1024)}) sort(s32[8192]{0:T(1024)S(1)} %fusion, s32[8192]{0:T(1024)S(1)} %iota.11), dimensions={0}, to_apply=%region_0.1 | sort | flops 106496 | bytes 131072 | tf_op jit(solution)/shard_map/sort | solution.py:386
  31.4 16.4 %prepare.1 = (bf16[4096,1024]{1,0:T(8,128)(2,1)}, f32[4096,256]{1,0:T(8,128)}, bf16[4,16,256]{2,1,0:T(8,128)(2,1)S(1)}) custom-call(s32[1]{0:T(128)} %bitcast.13.active_s, s32[8192]{0:T(1024)S(1)} %get-tuple-element.16.keys_any.keys_s, s32[64,1,128]{2,1,0:T(1,128)S(1)} %bitcast.19, bf16[1024,256]{1,0:T(8,128)(2,1)} %feats.1), custom_call_target="tpu_custom_call" | custom-call | tf_op jit(solution)/shard_map/prepare/pallas_call | solution.py:389
  47.8 8.9 %all-to-all-done = bf16[128,8,256]{2,1,0:T(8,128)(2,1)S(1)} async-done(((bf16[128,8,256]{2,1,0:T(8,128)(2,1)}), bf16[128,8,256]{2,1,0:T(8,128)(2,1)S(1)}, u32[]{:S(2)}, u32[]{:S(2)}) %all-to-all-start) | async-done | bytes 524320 | tf_op jit(solution)/shard_map/all_to_all | solution.py:379
  56.6 3.4 %aggregate_remote_2.1 = bf16[1040,256]{1,0:T(8,128)(2,1)S(1)} custom-call(s32[4]{0:T(128)S(1)} %and_select_fusion.owner_s, bf16[1024,256]{1,0:T(8,128)(2,1)S(1)} %bitcast.15, bf16[4,16,256]{2,1,0:T(8,128)(2,1)S(1)} %get-tuple-element.17.counts, bf16[4096,1024]{1,0:T(8,128)(2,1)} %get-tuple-element.18.adj_hbm.adj, f32[4096,256]{1,0:T(8,128)} %get-tuple-element.19.local_hbm), custom_call_target="tpu_custom_call" | custom-call | tf_op jit(solution)/shard_map/aggregate_remote_2/pallas_call | solution.py:422
  60.0 3.8 %collective-permute-start.2 = (bf16[1040,256]{1,0:T(8,128)(2,1)S(1)}, bf16[1040,256]{1,0:T(8,128)(2,1)S(1)}, u32[]{:S(2)}, u32[]{:S(2)}) collective-permute-start(bf16[1040,256]{1,0:T(8,128)(2,1)S(1)} %aggregate_remote_2.1), channel_id=1, source_target_pairs={{0,2},{1,3},{2,0},{3,1},{4,6},{5,7},{6,4},{7,5},{8,10},{9,11},{10,... | collective-permute-start | bytes 1597448 | tf_op jit(solution)/shard_map/ppermute | solution.py:418
  63.8 5.2 %aggregate_remote_1_3.1 = (bf16[1040,256]{1,0:T(8,128)(2,1)S(1)}, bf16[1040,256]{1,0:T(8,128)(2,1)S(1)}) custom-call(s32[4]{0:T(128)S(1)} %and_select_fusion.owner_s, bf16[1024,256]{1,0:T(8,128)(2,1)S(1)} %bitcast.16, bf16[4,16,256]{2,1,0:T(8,128)(2,1)S(1)} %get-tuple-element.17.counts, bf16[4096,1024]{1,0:T(8,128)(2,1)} %get-tuple-element.18.adj_hbm.adj, ...), custom_call_target="tpu_custom_call" | custom-call | tf_op jit(solution)/shard_map/aggregate_remote_1_3/pallas_call | solution.py:422
  69.0 1.9 %collective-permute-start = (bf16[1040,256]{1,0:T(8,128)(2,1)S(1)}, bf16[1040,256]{1,0:T(8,128)(2,1)S(1)}, u32[]{:S(2)}, u32[]{:S(2)}) collective-permute-start(bf16[1040,256]{1,0:T(8,128)(2,1)S(1)} %get-tuple-element.21), channel_id=1, source_target_pairs={{0,1},{1,2},{2,3},{3,0},{4,5},{5,6},{6,7},{7,4},{8,9},{9,10},{10,1... | collective-permute-start | bytes 1597448 | tf_op jit(solution)/shard_map/ppermute | solution.py:418
  70.9 0.0 copy-start.9
  70.9 3.4 %collective-permute-start.1 = (bf16[1040,256]{1,0:T(8,128)(2,1)S(1)}, bf16[1040,256]{1,0:T(8,128)(2,1)S(1)}, u32[]{:S(2)}, u32[]{:S(2)}) collective-permute-start(bf16[1040,256]{1,0:T(8,128)(2,1)S(1)} %get-tuple-element.23), channel_id=1, source_target_pairs={{0,3},{1,0},{2,1},{3,2},{4,7},{5,4},{6,5},{7,6},{8,11},{9,8},{10,9... | collective-permute-start | bytes 1597448 | tf_op jit(solution)/shard_map/ppermute | solution.py:418
  74.3 6.8 %adjacency_transposed.1.adj = bf16[8,1024,512]{2,1,0:T(8,128)(2,1)S(1)} custom-call(bf16[4096,1024]{1,0:T(8,128)(2,1)} %get-tuple-element.18.adj_hbm.adj), custom_call_target="tpu_custom_call" | custom-call | tf_op jit(solution)/shard_map/adjacency_transposed/pallas_call | solution.py:449
  81.1 0.0 copy-done.9
  81.2 0.0 copy-start
  81.2 0.0 copy-start.5
  81.2 0.0 copy-start.7
  81.2 3.4 %aggregate_remote_0.1.refs_0_.refs_4_ = bf16[1040,256]{1,0:T(8,128)(2,1)S(1)} custom-call(s32[4]{0:T(128)S(1)} %and_select_fusion.owner_s, bf16[1024,256]{1,0:T(8,128)(2,1)S(1)} %bitcast.17, bf16[4,16,256]{2,1,0:T(8,128)(2,1)S(1)} %get-tuple-element.17.counts, bf16[4096,1024]{1,0:T(8,128)(2,1)} %get-tuple-element.18.adj_hbm.adj, ...), custom_call_target="tpu_custom_call" | custom-call | tf_op jit(solution)/shard_map/aggregate_remote_0/pallas_call | solution.py:422
  84.6 0.0 collective-permute-done.2.refs_3_.refs_7_
  84.6 4.1 %collective-permute-done.refs_1_.refs_5_ = bf16[1040,256]{1,0:T(8,128)(2,1)S(1)} collective-permute-done((bf16[1040,256]{1,0:T(8,128)(2,1)S(1)}, bf16[1040,256]{1,0:T(8,128)(2,1)S(1)}, u32[]{:S(2)}, u32[]{:S(2)}) %collective-permute-start) | collective-permute-done | bytes 532512 | tf_op jit(solution)/shard_map/ppermute | solution.py:418
  88.8 0.2 collective-permute-done.1.refs_2_.refs_6_
  88.9 0.0 copy-done
  88.9 0.0 copy-done.5
  88.9 0.0 copy-done.7
  88.9 3.1 %dense_layer.1 = (bf16[1024,256]{1,0:T(8,128)(2,1)}, bf16[1024,256]{1,0:T(8,128)(2,1)}, bf16[1024,256]{1,0:T(8,128)(2,1)}) custom-call(bf16[1024,256]{1,0:T(8,128)(2,1)S(1)} %copy-done, bf16[1024,256]{1,0:T(8,128)(2,1)} %cots.1, bf16[256,256]{1,0:T(8,128)(2,1)S(1)} %copy-done.5, bf16[256,256]{1,0:T(8,128)(2,1)S(1)} %copy-done.7, ...), custom_call_target="tpu_custom_call" | custom-call | tf_op jit(solution)/shard_map/dense_layer/pallas_call | solution.py:465
  92.0 3.1 %collective-permute-start.5 = (bf16[1024,256]{1,0:T(8,128)(2,1)}, bf16[1024,256]{1,0:T(8,128)(2,1)S(1)}, u32[]{:S(2)}, u32[]{:S(2)}) collective-permute-start(bf16[1024,256]{1,0:T(8,128)(2,1)} %get-tuple-element.26.own.p0), channel_id=1, source_target_pairs={{0,1},{1,2},{2,3},{3,0},{4,5},{5,6},{6,7},{7,4},{8,9},{9,10},{10,1... | collective-permute-start | bytes 1572872 | tf_op jit(solution)/shard_map/ppermute | solution.py:418
  95.1 2.1 %collective-permute-start.3 = (bf16[1024,256]{1,0:T(8,128)(2,1)}, bf16[1024,256]{1,0:T(8,128)(2,1)S(1)}, u32[]{:S(2)}, u32[]{:S(2)}) collective-permute-start(bf16[1024,256]{1,0:T(8,128)(2,1)} %get-tuple-element.26.own.p0), channel_id=1, source_target_pairs={{0,3},{1,0},{2,1},{3,2},{4,7},{5,4},{6,5},{7,6},{8,11},{9,8},{10,9... | collective-permute-start | bytes 1572872 | tf_op jit(solution)/shard_map/ppermute | solution.py:418
  97.3 3.3 %collective-permute-start.4 = (bf16[1024,256]{1,0:T(8,128)(2,1)}, bf16[1024,256]{1,0:T(8,128)(2,1)S(1)}, u32[]{:S(2)}, u32[]{:S(2)}) collective-permute-start(bf16[1024,256]{1,0:T(8,128)(2,1)} %get-tuple-element.26.own.p0), channel_id=1, source_target_pairs={{0,2},{1,3},{2,0},{3,1},{4,6},{5,7},{6,4},{7,5},{8,10},{9,11},{10,... | collective-permute-start | bytes 1572872 | tf_op jit(solution)/shard_map/ppermute | solution.py:418
  100.6 6.5 %collective-permute-done.5.left.p1 = bf16[1024,256]{1,0:T(8,128)(2,1)S(1)} collective-permute-done((bf16[1024,256]{1,0:T(8,128)(2,1)}, bf16[1024,256]{1,0:T(8,128)(2,1)S(1)}, u32[]{:S(2)}, u32[]{:S(2)}) %collective-permute-start.5) | collective-permute-done | bytes 524320 | tf_op jit(solution)/shard_map/ppermute | solution.py:418
  107.1 1.0 copy-done.1
  108.1 1.8 %scatter_near.1.near = f32[1024,256]{1,0:T(8,128)S(1)} custom-call(s32[4]{0:T(128)S(1)} %and_select_fusion.owner_s, bf16[1024,256]{1,0:T(8,128)(2,1)S(1)} %copy-done.1, bf16[1024,256]{1,0:T(8,128)(2,1)S(1)} %collective-permute-done.5.left.p1, bf16[8,1024,512]{2,1,0:T(8,128)(2,1)S(1)} %adjacency_transposed.1.adj), custom_call_target="tpu_custom_call" | custom-call | tf_op jit(solution)/shard_map/scatter_near/pallas_call | solution.py:482
  109.9 0.0 copy-start.8
  109.9 0.0 copy-start.2
  109.9 0.8 collective-permute-done.3.right.p2
  110.7 9.9 %collective-permute-done.4.far.p3 = bf16[1024,256]{1,0:T(8,128)(2,1)S(1)} collective-permute-done((bf16[1024,256]{1,0:T(8,128)(2,1)}, bf16[1024,256]{1,0:T(8,128)(2,1)S(1)}, u32[]{:S(2)}, u32[]{:S(2)}) %collective-permute-start.4) | collective-permute-done | bytes 524320 | tf_op jit(solution)/shard_map/ppermute | solution.py:418
  120.6 2.6 %scatter_far.1 = bf16[1024,256]{1,0:T(8,128)(2,1)} custom-call(s32[4]{0:T(128)S(1)} %and_select_fusion.owner_s, bf16[1024,256]{1,0:T(8,128)(2,1)S(1)} %collective-permute-done.3.right.p2, bf16[1024,256]{1,0:T(8,128)(2,1)S(1)} %collective-permute-done.4.far.p3, f32[1024,256]{1,0:T(8,128)S(1)} %scatter_near.1.near, ...), custom_call_target="tpu_custom_call" | custom-call | tf_op jit(solution)/shard_map/scatter_far/pallas_call | solution.py:482
  123.2 0.0 copy-done.3
  123.2 10.2 %all-to-all-start.1 = ((bf16[128,8,256]{2,1,0:T(8,128)(2,1)}), bf16[128,8,256]{2,1,0:T(8,128)(2,1)S(1)}, u32[]{:S(2)}, u32[]{:S(2)}) async-start(bf16[128,8,256]{2,1,0:T(8,128)(2,1)} %bitcast.8), calls=%async_computation.1 | async-start | bytes 1048576 | tf_op jit(solution)/shard_map/all_to_all | solution.py:494
  133.4 0.0 copy-done.8
  133.4 0.1 copy.12
  133.5 0.1 reshape.47
  133.6 0.0 copy-done.2
  133.6 0.0 copy-start.4
  133.6 1.0 copy-done.4
  134.6 1.0 copy-done.6
  135.7 8.7 %scatter_local.1.kept = f32[1024,256]{1,0:T(8,128)S(1)} custom-call(s32[8192]{0:T(1024)S(1)} %get-tuple-element.16.keys_any.keys_s, s32[1]{0:T(128)} %bitcast.14.active_s, s32[4]{0:T(128)S(1)} %and_select_fusion.owner_s, s32[64,1,128]{2,1,0:T(1,128)S(1)} %bitcast.20, bf16[1024,256]{1,0:T(8,128)(2,1)S(1)} %copy-done.6, bf16[256,256]{1,0:T(8,128)(2,1)S(1)} %copy-done.5, ...), custom_call_target="tpu_custom_call" | custom-call | tf_op jit(solution)/shard_map/scatter_local/pallas_call | solution.py:497
  144.4 22.6 %all-to-all-done.1 = bf16[128,8,256]{2,1,0:T(8,128)(2,1)S(1)} async-done(((bf16[128,8,256]{2,1,0:T(8,128)(2,1)}), bf16[128,8,256]{2,1,0:T(8,128)(2,1)S(1)}, u32[]{:S(2)}, u32[]{:S(2)}) %all-to-all-start.1) | async-done | bytes 524320 | tf_op jit(solution)/shard_map/all_to_all | solution.py:494
  167.0 1.6 combine.1
  (7 shorter events, 0.0 us)
Async XLA Ops:
  3.6 53.1 %all-to-all-start = ((bf16[128,8,256]{2,1,0:T(8,128)(2,1)}), bf16[128,8,256]{2,1,0:T(8,128)(2,1)S(1)}, u32[]{:S(2)}, u32[]{:S(2)}) async-start(bf16[128,8,256]{2,1,0:T(8,128)(2,1)} %pick_rows.1), calls=%async_computation | async-start | bytes 1048576 | tf_op jit(solution)/shard_map/all_to_all | solution.py:379
  60.0 24.6 %collective-permute-start.2 = (bf16[1040,256]{1,0:T(8,128)(2,1)S(1)}, bf16[1040,256]{1,0:T(8,128)(2,1)S(1)}, u32[]{:S(2)}, u32[]{:S(2)}) collective-permute-start(bf16[1040,256]{1,0:T(8,128)(2,1)S(1)} %aggregate_remote_2.1), channel_id=1, source_target_pairs={{0,2},{1,3},{2,0},{3,1},{4,6},{5,7},{6,4},{7,5},{8,10},{9,11},{10,... | collective-permute-start | bytes 1597448 | tf_op jit(solution)/shard_map/ppermute | solution.py:418
  69.0 19.8 %collective-permute-start = (bf16[1040,256]{1,0:T(8,128)(2,1)S(1)}, bf16[1040,256]{1,0:T(8,128)(2,1)S(1)}, u32[]{:S(2)}, u32[]{:S(2)}) collective-permute-start(bf16[1040,256]{1,0:T(8,128)(2,1)S(1)} %get-tuple-element.21), channel_id=1, source_target_pairs={{0,1},{1,2},{2,3},{3,0},{4,5},{5,6},{6,7},{7,4},{8,9},{9,10},{10,1... | collective-permute-start | bytes 1597448 | tf_op jit(solution)/shard_map/ppermute | solution.py:418
  70.9 10.2 %copy-start.9 = (bf16[256]{0:T(256)(128)(2,1)S(1)}, bf16[256]{0:T(256)(128)(2,1)}, u32[]{:S(2)}) copy-start(bf16[256]{0:T(256)(128)(2,1)} %param.13) | copy-start | bytes 1540
  70.9 18.0 %collective-permute-start.1 = (bf16[1040,256]{1,0:T(8,128)(2,1)S(1)}, bf16[1040,256]{1,0:T(8,128)(2,1)S(1)}, u32[]{:S(2)}, u32[]{:S(2)}) collective-permute-start(bf16[1040,256]{1,0:T(8,128)(2,1)S(1)} %get-tuple-element.23), channel_id=1, source_target_pairs={{0,3},{1,0},{2,1},{3,2},{4,7},{5,4},{6,5},{7,6},{8,11},{9,8},{10,9... | collective-permute-start | bytes 1597448 | tf_op jit(solution)/shard_map/ppermute | solution.py:418
  81.2 7.8 %copy-start = (bf16[1024,256]{1,0:T(8,128)(2,1)S(1)}, bf16[1024,256]{1,0:T(8,128)(2,1)}, u32[]{:S(2)}) copy-start(bf16[1024,256]{1,0:T(8,128)(2,1)} %feats.1) | copy-start | bytes 1572868
  81.2 7.8 %copy-start.5 = (bf16[256,256]{1,0:T(8,128)(2,1)S(1)}, bf16[256,256]{1,0:T(8,128)(2,1)}, u32[]{:S(2)}) copy-start(bf16[256,256]{1,0:T(8,128)(2,1)} %w_self.3) | copy-start | bytes 393220
  81.2 7.8 %copy-start.7 = (bf16[256,256]{1,0:T(8,128)(2,1)S(1)}, bf16[256,256]{1,0:T(8,128)(2,1)}, u32[]{:S(2)}) copy-start(bf16[256,256]{1,0:T(8,128)(2,1)} %w_neigh.1) | copy-start | bytes 393220
  92.0 15.1 %collective-permute-start.5 = (bf16[1024,256]{1,0:T(8,128)(2,1)}, bf16[1024,256]{1,0:T(8,128)(2,1)S(1)}, u32[]{:S(2)}, u32[]{:S(2)}) collective-permute-start(bf16[1024,256]{1,0:T(8,128)(2,1)} %get-tuple-element.26.own.p0), channel_id=1, source_target_pairs={{0,1},{1,2},{2,3},{3,0},{4,5},{5,6},{6,7},{7,4},{8,9},{9,10},{10,1... | collective-permute-start | bytes 1572872 | tf_op jit(solution)/shard_map/ppermute | solution.py:418
  95.1 15.5 %collective-permute-start.3 = (bf16[1024,256]{1,0:T(8,128)(2,1)}, bf16[1024,256]{1,0:T(8,128)(2,1)S(1)}, u32[]{:S(2)}, u32[]{:S(2)}) collective-permute-start(bf16[1024,256]{1,0:T(8,128)(2,1)} %get-tuple-element.26.own.p0), channel_id=1, source_target_pairs={{0,3},{1,0},{2,1},{3,2},{4,7},{5,4},{6,5},{7,6},{8,11},{9,8},{10,9... | collective-permute-start | bytes 1572872 | tf_op jit(solution)/shard_map/ppermute | solution.py:418
  97.3 23.3 %collective-permute-start.4 = (bf16[1024,256]{1,0:T(8,128)(2,1)}, bf16[1024,256]{1,0:T(8,128)(2,1)S(1)}, u32[]{:S(2)}, u32[]{:S(2)}) collective-permute-start(bf16[1024,256]{1,0:T(8,128)(2,1)} %get-tuple-element.26.own.p0), channel_id=1, source_target_pairs={{0,2},{1,3},{2,0},{3,1},{4,6},{5,7},{6,4},{7,5},{8,10},{9,11},{10,... | collective-permute-start | bytes 1572872 | tf_op jit(solution)/shard_map/ppermute | solution.py:418
  107.1 1.0 copy-start.1
  108.1 15.1 %copy-start.3 = (bf16[1024,256]{1,0:T(8,128)(2,1)}, bf16[1024,256]{1,0:T(8,128)(2,1)S(1)}, u32[]{:S(2)}) copy-start(bf16[1024,256]{1,0:T(8,128)(2,1)S(1)} %collective-permute-done.5.left.p1) | copy-start | bytes 1572868
  109.9 23.5 %copy-start.8 = (s32[1,1,128,8]{2,3,1,0:T(8,128)S(1)}, s32[1,1,128,8]{2,3,1,0:T(8,128)}, u32[]{:S(2)}) copy-start(s32[1,1,128,8]{2,3,1,0:T(8,128)} %param.14) | copy-start | bytes 12292
  109.9 23.7 %copy-start.2 = (bf16[1024,256]{1,0:T(8,128)(2,1)S(1)}, bf16[1024,256]{1,0:T(8,128)(2,1)}, u32[]{:S(2)}) copy-start(bf16[1024,256]{1,0:T(8,128)(2,1)} %get-tuple-element.26.own.p0) | copy-start | bytes 1572868
  123.2 43.8 %all-to-all-start.1 = ((bf16[128,8,256]{2,1,0:T(8,128)(2,1)}), bf16[128,8,256]{2,1,0:T(8,128)(2,1)S(1)}, u32[]{:S(2)}, u32[]{:S(2)}) async-start(bf16[128,8,256]{2,1,0:T(8,128)(2,1)} %bitcast.8), calls=%async_computation.1 | async-start | bytes 1048576 | tf_op jit(solution)/shard_map/all_to_all | solution.py:494
  133.6 1.0 copy-start.4
  134.6 1.0 copy-start.6

commit v9 on v8

--- a/solution.py
+++ b/solution.py
@@ -332,12 +332,12 @@
     return total
 
 
-def backward_near_kernel(owner_s, own, left, adj, out):
-    out[...] = piece_sum(owner_s, ((0, own), (3, left)), adj, None)
-
-
-def backward_far_kernel(owner_s, right, far, near, adj, out):
-    out[...] = piece_sum(owner_s, ((1, right), (2, far)), adj, near[...]).astype(BF16)
+def backward_first_kernel(owner_s, own, far, adj, out):
+    out[...] = piece_sum(owner_s, ((0, own), (2, far)), adj, None)
+
+
+def backward_last_kernel(owner_s, left, right, start, adj, out):
+    out[...] = piece_sum(owner_s, ((3, left), (1, right)), adj, start[...]).astype(BF16)
 
 
 def backward_local_kernel(keys_s, active_s, owner_s, keys_v, up, w_self, p0, p1, p2, p3, out, spread, rows_ref, sems):
@@ -489,8 +489,8 @@
             name=name,
         )(order, *pieces, adj_t)
 
-    near = backward(backward_near_kernel, (scaled, prev), F32, "scatter_near")
-    outgoing = backward(backward_far_kernel, (follow, far, near), BF16, "scatter_far")
+    begun = backward(backward_first_kernel, (scaled, far), F32, "scatter_first")
+    outgoing = backward(backward_last_kernel, (prev, follow, begun), BF16, "scatter_last")
     returned = lax.all_to_all(
         outgoing.reshape(peers, capacity, WIDTH), "dom", split_axis=0, concat_axis=0, tiled=True
     ).reshape(peers * capacity, WIDTH)

time: 170 us -> 168 us (0.988)
  transfers between devices with their start and end apart: 8 -> 8, of which waited for: 7 -> 7; matrix products, arithmetic and copies ran while one was open for 5% -> 5% of each run, Pallas kernels for 25% -> 26%
where the time goes in v9:
time: 168 us
  Pallas kernels  56.5 us (34%)
  waiting for transfers between devices  52.2 us (31%)
  starting transfers between devices  46.4 us (28%)
  other arithmetic  7.63 us (5%)
  local copies, waits for them, and re-layouts  3.36 us (2%)
  between operations  1.69 us (1%)
    all_to_all x1, waiting for transfers between devices, local(): lax.all_to_all(outgoing.reshape(peers, capacity, WIDTH), 'dom', split_axi...  23.1 us
    ppermute x6, waiting for transfers between devices, shifted(): return lax.ppermute(x, 'src', [(j, (j + k) % 4) for j in range(4)])  21.3 us
    all_to_all x1, starting transfers between devices, local(): lax.all_to_all(picked, 'dom', split_axis=0, concat_axis=0, tiled=True)  19.5 us
    ppermute x6, starting transfers between devices, shifted(): return lax.ppermute(x, 'src', [(j, (j + k) % 4) for j in range(4)])  17.8 us
    pallas_call x1, Pallas kernels, local(): pl.pallas_call(prepare_kernel, grid_spec=pltpu.PrefetchScalarGridSpec(num...  17.6 us
    pallas_call x3, Pallas kernels, partials(): pl.pallas_call(functools.partial(forward_remote_kernel, shifts), grid_spe...  12 us
    all_to_all x1, starting transfers between devices, local(): lax.all_to_all(outgoing.reshape(peers, capacity, WIDTH), 'dom', split_axi...  9.15 us
    pallas_call x1, Pallas kernels, local(): pl.pallas_call(backward_local_kernel, grid_spec=pltpu.PrefetchScalarGridS...  8.14 us
  transfers between devices with their start and end apart: 8, of which 7 were waited for; matrix products, arithmetic and copies ran while one was open for 5% of the time, Pallas kernels for 26%

profile of v9, /device:TPU:35, one launch (start us, length us, event | category | flops | bytes accessed | tf_op | source)
XLA Modules:
  0.0 167.8 jit_solution(6458348415132256286)
XLA Ops:
  0.6 2.9 %pick_rows.1 = bf16[128,8,256]{2,1,0:T(8,128)(2,1)} custom-call(s32[8,128]{1,0:T(8,128)} %bitcast.23, bf16[1024,256]{1,0:T(8,128)(2,1)} %feats.1), custom_call_target="tpu_custom_call" | custom-call | tf_op jit(solution)/shard_map/pick_rows/pallas_call | solution.py:366
  3.6 19.5 %all-to-all-start = ((bf16[128,8,256]{2,1,0:T(8,128)(2,1)}), bf16[128,8,256]{2,1,0:T(8,128)(2,1)S(1)}, u32[]{:S(2)}, u32[]{:S(2)}) async-start(bf16[128,8,256]{2,1,0:T(8,128)(2,1)} %pick_rows.1), calls=%async_computation | async-start | bytes 1048576 | tf_op jit(solution)/shard_map/all_to_all | solution.py:379
  23.7 0.8 and_add_fusion
  24.6 6.8 %sort.10 = (s32[8192]{0:T(1024)S(1)}, s32[8192]{0:T(1024)}) sort(s32[8192]{0:T(1024)S(1)} %fusion, s32[8192]{0:T(1024)S(1)} %iota.11), dimensions={0}, to_apply=%region_0.1 | sort | flops 106496 | bytes 131072 | tf_op jit(solution)/shard_map/sort | solution.py:386
  31.4 17.6 %prepare.1 = (bf16[4096,1024]{1,0:T(8,128)(2,1)}, f32[4096,256]{1,0:T(8,128)}, bf16[4,16,256]{2,1,0:T(8,128)(2,1)S(1)}) custom-call(s32[1]{0:T(128)} %bitcast.13.active_s, s32[8192]{0:T(1024)S(1)} %get-tuple-element.16.keys_any.keys_s, s32[64,1,128]{2,1,0:T(1,128)S(1)} %bitcast.19, bf16[1024,256]{1,0:T(8,128)(2,1)} %feats.1), custom_call_target="tpu_custom_call" | custom-call | tf_op jit(solution)/shard_map/prepare/pallas_call | solution.py:389
  49.0 7.7 %all-to-all-done = bf16[128,8,256]{2,1,0:T(8,128)(2,1)S(1)} async-done(((bf16[128,8,256]{2,1,0:T(8,128)(2,1)}), bf16[128,8,256]{2,1,0:T(8,128)(2,1)S(1)}, u32[]{:S(2)}, u32[]{:S(2)}) %all-to-all-start) | async-done | bytes 524320 | tf_op jit(solution)/shard_map/all_to_all | solution.py:379
  56.6 3.4 %aggregate_remote_2.1 = bf16[1040,256]{1,0:T(8,128)(2,1)S(1)} custom-call(s32[4]{0:T(128)S(1)} %and_select_fusion.owner_s, bf16[1024,256]{1,0:T(8,128)(2,1)S(1)} %bitcast.15, bf16[4,16,256]{2,1,0:T(8,128)(2,1)S(1)} %get-tuple-element.17.counts, bf16[4096,1024]{1,0:T(8,128)(2,1)} %get-tuple-element.18.adj_hbm.adj, f32[4096,256]{1,0:T(8,128)} %get-tuple-element.19.local_hbm), custom_call_target="tpu_custom_call" | custom-call | tf_op jit(solution)/shard_map/aggregate_remote_2/pallas_call | solution.py:422
  60.0 3.8 %collective-permute-start.2 = (bf16[1040,256]{1,0:T(8,128)(2,1)S(1)}, bf16[1040,256]{1,0:T(8,128)(2,1)S(1)}, u32[]{:S(2)}, u32[]{:S(2)}) collective-permute-start(bf16[1040,256]{1,0:T(8,128)(2,1)S(1)} %aggregate_remote_2.1), channel_id=1, source_target_pairs={{0,2},{1,3},{2,0},{3,1},{4,6},{5,7},{6,4},{7,5},{8,10},{9,11},{10,... | collective-permute-start | bytes 1597448 | tf_op jit(solution)/shard_map/ppermute | solution.py:418
  63.8 5.2 %aggregate_remote_1_3.1 = (bf16[1040,256]{1,0:T(8,128)(2,1)S(1)}, bf16[1040,256]{1,0:T(8,128)(2,1)S(1)}) custom-call(s32[4]{0:T(128)S(1)} %and_select_fusion.owner_s, bf16[1024,256]{1,0:T(8,128)(2,1)S(1)} %bitcast.16, bf16[4,16,256]{2,1,0:T(8,128)(2,1)S(1)} %get-tuple-element.17.counts, bf16[4096,1024]{1,0:T(8,128)(2,1)} %get-tuple-element.18.adj_hbm.adj, ...), custom_call_target="tpu_custom_call" | custom-call | tf_op jit(solution)/shard_map/aggregate_remote_1_3/pallas_call | solution.py:422
  69.0 1.9 %collective-permute-start = (bf16[1040,256]{1,0:T(8,128)(2,1)S(1)}, bf16[1040,256]{1,0:T(8,128)(2,1)S(1)}, u32[]{:S(2)}, u32[]{:S(2)}) collective-permute-start(bf16[1040,256]{1,0:T(8,128)(2,1)S(1)} %get-tuple-element.21), channel_id=1, source_target_pairs={{0,1},{1,2},{2,3},{3,0},{4,5},{5,6},{6,7},{7,4},{8,9},{9,10},{10,1... | collective-permute-start | bytes 1597448 | tf_op jit(solution)/shard_map/ppermute | solution.py:418
  70.9 0.0 copy-start.9
  70.9 3.4 %collective-permute-start.1 = (bf16[1040,256]{1,0:T(8,128)(2,1)S(1)}, bf16[1040,256]{1,0:T(8,128)(2,1)S(1)}, u32[]{:S(2)}, u32[]{:S(2)}) collective-permute-start(bf16[1040,256]{1,0:T(8,128)(2,1)S(1)} %get-tuple-element.23), channel_id=1, source_target_pairs={{0,3},{1,0},{2,1},{3,2},{4,7},{5,4},{6,5},{7,6},{8,11},{9,8},{10,9... | collective-permute-start | bytes 1597448 | tf_op jit(solution)/shard_map/ppermute | solution.py:418
  74.3 6.8 %adjacency_transposed.1.adj = bf16[8,1024,512]{2,1,0:T(8,128)(2,1)S(1)} custom-call(bf16[4096,1024]{1,0:T(8,128)(2,1)} %get-tuple-element.18.adj_hbm.adj), custom_call_target="tpu_custom_call" | custom-call | tf_op jit(solution)/shard_map/adjacency_transposed/pallas_call | solution.py:449
  81.1 0.0 copy-done.9
  81.2 0.0 copy-start
  81.2 0.0 copy-start.5
  81.2 0.0 copy-start.7
  81.2 3.4 %aggregate_remote_0.1.refs_0_.refs_4_ = bf16[1040,256]{1,0:T(8,128)(2,1)S(1)} custom-call(s32[4]{0:T(128)S(1)} %and_select_fusion.owner_s, bf16[1024,256]{1,0:T(8,128)(2,1)S(1)} %bitcast.17, bf16[4,16,256]{2,1,0:T(8,128)(2,1)S(1)} %get-tuple-element.17.counts, bf16[4096,1024]{1,0:T(8,128)(2,1)} %get-tuple-element.18.adj_hbm.adj, ...), custom_call_target="tpu_custom_call" | custom-call | tf_op jit(solution)/shard_map/aggregate_remote_0/pallas_call | solution.py:422
  84.6 0.0 collective-permute-done.2.refs_3_.refs_7_
  84.6 4.1 %collective-permute-done.refs_1_.refs_5_ = bf16[1040,256]{1,0:T(8,128)(2,1)S(1)} collective-permute-done((bf16[1040,256]{1,0:T(8,128)(2,1)S(1)}, bf16[1040,256]{1,0:T(8,128)(2,1)S(1)}, u32[]{:S(2)}, u32[]{:S(2)}) %collective-permute-start) | collective-permute-done | bytes 532512 | tf_op jit(solution)/shard_map/ppermute | solution.py:418
  88.8 0.2 collective-permute-done.1.refs_2_.refs_6_
  88.9 0.0 copy-done
  88.9 0.0 copy-done.5
  88.9 0.0 copy-done.7
  88.9 3.1 %dense_layer.1 = (bf16[1024,256]{1,0:T(8,128)(2,1)}, bf16[1024,256]{1,0:T(8,128)(2,1)}, bf16[1024,256]{1,0:T(8,128)(2,1)}) custom-call(bf16[1024,256]{1,0:T(8,128)(2,1)S(1)} %copy-done, bf16[1024,256]{1,0:T(8,128)(2,1)} %cots.1, bf16[256,256]{1,0:T(8,128)(2,1)S(1)} %copy-done.5, bf16[256,256]{1,0:T(8,128)(2,1)S(1)} %copy-done.7, ...), custom_call_target="tpu_custom_call" | custom-call | tf_op jit(solution)/shard_map/dense_layer/pallas_call | solution.py:465
  92.0 3.3 %collective-permute-start.5 = (bf16[1024,256]{1,0:T(8,128)(2,1)}, bf16[1024,256]{1,0:T(8,128)(2,1)S(1)}, u32[]{:S(2)}, u32[]{:S(2)}) collective-permute-start(bf16[1024,256]{1,0:T(8,128)(2,1)} %get-tuple-element.26.own.p0), channel_id=1, source_target_pairs={{0,2},{1,3},{2,0},{3,1},{4,6},{5,7},{6,4},{7,5},{8,10},{9,11},{10,... | collective-permute-start | bytes 1572872 | tf_op jit(solution)/shard_map/ppermute | solution.py:418
  95.3 2.0 %collective-permute-start.3 = (bf16[1024,256]{1,0:T(8,128)(2,1)}, bf16[1024,256]{1,0:T(8,128)(2,1)S(1)}, u32[]{:S(2)}, u32[]{:S(2)}) collective-permute-start(bf16[1024,256]{1,0:T(8,128)(2,1)} %get-tuple-element.26.own.p0), channel_id=1, source_target_pairs={{0,1},{1,2},{2,3},{3,0},{4,5},{5,6},{6,7},{7,4},{8,9},{9,10},{10,1... | collective-permute-start | bytes 1572872 | tf_op jit(solution)/shard_map/ppermute | solution.py:418
  97.3 3.5 %collective-permute-start.4 = (bf16[1024,256]{1,0:T(8,128)(2,1)}, bf16[1024,256]{1,0:T(8,128)(2,1)S(1)}, u32[]{:S(2)}, u32[]{:S(2)}) collective-permute-start(bf16[1024,256]{1,0:T(8,128)(2,1)} %get-tuple-element.26.own.p0), channel_id=1, source_target_pairs={{0,3},{1,0},{2,1},{3,2},{4,7},{5,4},{6,5},{7,6},{8,11},{9,8},{10,9... | collective-permute-start | bytes 1572872 | tf_op jit(solution)/shard_map/ppermute | solution.py:418
  100.8 7.8 %collective-permute-done.5.far.p3 = bf16[1024,256]{1,0:T(8,128)(2,1)S(1)} collective-permute-done((bf16[1024,256]{1,0:T(8,128)(2,1)}, bf16[1024,256]{1,0:T(8,128)(2,1)S(1)}, u32[]{:S(2)}, u32[]{:S(2)}) %collective-permute-start.5) | collective-permute-done | bytes 524320 | tf_op jit(solution)/shard_map/ppermute | solution.py:418
  108.6 1.0 copy-done.1
  109.6 1.8 %scatter_first.1.start = f32[1024,256]{1,0:T(8,128)S(1)} custom-call(s32[4]{0:T(128)S(1)} %and_select_fusion.owner_s, bf16[1024,256]{1,0:T(8,128)(2,1)S(1)} %copy-done.1, bf16[1024,256]{1,0:T(8,128)(2,1)S(1)} %collective-permute-done.5.far.p3, bf16[8,1024,512]{2,1,0:T(8,128)(2,1)S(1)} %adjacency_transposed.1.adj), custom_call_target="tpu_custom_call" | custom-call | tf_op jit(solution)/shard_map/scatter_first/pallas_call | solution.py:482
  111.4 0.0 copy-start.8
  111.4 0.0 copy-start.2
  111.5 8.5 %collective-permute-done.3.left.p1 = bf16[1024,256]{1,0:T(8,128)(2,1)S(1)} collective-permute-done((bf16[1024,256]{1,0:T(8,128)(2,1)}, bf16[1024,256]{1,0:T(8,128)(2,1)S(1)}, u32[]{:S(2)}, u32[]{:S(2)}) %collective-permute-start.3) | collective-permute-done | bytes 524320 | tf_op jit(solution)/shard_map/ppermute | solution.py:418
  120.0 0.7 collective-permute-done.4.right.p2
  120.7 2.6 %scatter_last.1 = bf16[1024,256]{1,0:T(8,128)(2,1)} custom-call(s32[4]{0:T(128)S(1)} %and_select_fusion.owner_s, bf16[1024,256]{1,0:T(8,128)(2,1)S(1)} %collective-permute-done.3.left.p1, bf16[1024,256]{1,0:T(8,128)(2,1)S(1)} %collective-permute-done.4.right.p2, f32[1024,256]{1,0:T(8,128)S(1)} %scatter_first.1.start, ...), custom_call_target="tpu_custom_call" | custom-call | tf_op jit(solution)/shard_map/scatter_last/pallas_call | solution.py:482
  123.3 0.0 copy-done.3
  123.3 9.1 %all-to-all-start.1 = ((bf16[128,8,256]{2,1,0:T(8,128)(2,1)}), bf16[128,8,256]{2,1,0:T(8,128)(2,1)S(1)}, u32[]{:S(2)}, u32[]{:S(2)}) async-start(bf16[128,8,256]{2,1,0:T(8,128)(2,1)} %bitcast.8), calls=%async_computation.1 | async-start | bytes 1048576 | tf_op jit(solution)/shard_map/all_to_all | solution.py:494
  132.4 0.0 copy-done.8
  132.4 0.1 copy.12
  132.5 0.1 reshape.47
  132.6 0.0 copy-done.2
  132.6 0.0 copy-start.4
  132.6 1.0 copy-done.4
  133.7 1.0 copy-done.6
  134.7 8.1 %scatter_local.1.kept = f32[1024,256]{1,0:T(8,128)S(1)} custom-call(s32[8192]{0:T(1024)S(1)} %get-tuple-element.16.keys_any.keys_s, s32[1]{0:T(128)} %bitcast.14.active_s, s32[4]{0:T(128)S(1)} %and_select_fusion.owner_s, s32[64,1,128]{2,1,0:T(1,128)S(1)} %bitcast.20, bf16[1024,256]{1,0:T(8,128)(2,1)S(1)} %copy-done.6, bf16[256,256]{1,0:T(8,128)(2,1)S(1)} %copy-done.5, ...), custom_call_target="tpu_custom_call" | custom-call | tf_op jit(solution)/shard_map/scatter_local/pallas_call | solution.py:497
  142.9 23.1 %all-to-all-done.1 = bf16[128,8,256]{2,1,0:T(8,128)(2,1)S(1)} async-done(((bf16[128,8,256]{2,1,0:T(8,128)(2,1)}), bf16[128,8,256]{2,1,0:T(8,128)(2,1)S(1)}, u32[]{:S(2)}, u32[]{:S(2)}) %all-to-all-start.1) | async-done | bytes 524320 | tf_op jit(solution)/shard_map/all_to_all | solution.py:494
  166.0 1.6 combine.1
  (7 shorter events, 0.0 us)
Async XLA Ops:
  3.6 53.1 %all-to-all-start = ((bf16[128,8,256]{2,1,0:T(8,128)(2,1)}), bf16[128,8,256]{2,1,0:T(8,128)(2,1)S(1)}, u32[]{:S(2)}, u32[]{:S(2)}) async-start(bf16[128,8,256]{2,1,0:T(8,128)(2,1)} %pick_rows.1), calls=%async_computation | async-start | bytes 1048576 | tf_op jit(solution)/shard_map/all_to_all | solution.py:379
  60.0 24.6 %collective-permute-start.2 = (bf16[1040,256]{1,0:T(8,128)(2,1)S(1)}, bf16[1040,256]{1,0:T(8,128)(2,1)S(1)}, u32[]{:S(2)}, u32[]{:S(2)}) collective-permute-start(bf16[1040,256]{1,0:T(8,128)(2,1)S(1)} %aggregate_remote_2.1), channel_id=1, source_target_pairs={{0,2},{1,3},{2,0},{3,1},{4,6},{5,7},{6,4},{7,5},{8,10},{9,11},{10,... | collective-permute-start | bytes 1597448 | tf_op jit(solution)/shard_map/ppermute | solution.py:418
  69.0 19.8 %collective-permute-start = (bf16[1040,256]{1,0:T(8,128)(2,1)S(1)}, bf16[1040,256]{1,0:T(8,128)(2,1)S(1)}, u32[]{:S(2)}, u32[]{:S(2)}) collective-permute-start(bf16[1040,256]{1,0:T(8,128)(2,1)S(1)} %get-tuple-element.21), channel_id=1, source_target_pairs={{0,1},{1,2},{2,3},{3,0},{4,5},{5,6},{6,7},{7,4},{8,9},{9,10},{10,1... | collective-permute-start | bytes 1597448 | tf_op jit(solution)/shard_map/ppermute | solution.py:418
  70.9 10.2 %copy-start.9 = (bf16[256]{0:T(256)(128)(2,1)S(1)}, bf16[256]{0:T(256)(128)(2,1)}, u32[]{:S(2)}) copy-start(bf16[256]{0:T(256)(128)(2,1)} %param.13) | copy-start | bytes 1540
  70.9 18.0 %collective-permute-start.1 = (bf16[1040,256]{1,0:T(8,128)(2,1)S(1)}, bf16[1040,256]{1,0:T(8,128)(2,1)S(1)}, u32[]{:S(2)}, u32[]{:S(2)}) collective-permute-start(bf16[1040,256]{1,0:T(8,128)(2,1)S(1)} %get-tuple-element.23), channel_id=1, source_target_pairs={{0,3},{1,0},{2,1},{3,2},{4,7},{5,4},{6,5},{7,6},{8,11},{9,8},{10,9... | collective-permute-start | bytes 1597448 | tf_op jit(solution)/shard_map/ppermute | solution.py:418
  81.2 7.8 %copy-start = (bf16[1024,256]{1,0:T(8,128)(2,1)S(1)}, bf16[1024,256]{1,0:T(8,128)(2,1)}, u32[]{:S(2)}) copy-start(bf16[1024,256]{1,0:T(8,128)(2,1)} %feats.1) | copy-start | bytes 1572868
  81.2 7.8 %copy-start.5 = (bf16[256,256]{1,0:T(8,128)(2,1)S(1)}, bf16[256,256]{1,0:T(8,128)(2,1)}, u32[]{:S(2)}) copy-start(bf16[256,256]{1,0:T(8,128)(2,1)} %w_self.3) | copy-start | bytes 393220
  81.2 7.8 %copy-start.7 = (bf16[256,256]{1,0:T(8,128)(2,1)S(1)}, bf16[256,256]{1,0:T(8,128)(2,1)}, u32[]{:S(2)}) copy-start(bf16[256,256]{1,0:T(8,128)(2,1)} %w_neigh.1) | copy-start | bytes 393220
  92.0 16.6 %collective-permute-start.5 = (bf16[1024,256]{1,0:T(8,128)(2,1)}, bf16[1024,256]{1,0:T(8,128)(2,1)S(1)}, u32[]{:S(2)}, u32[]{:S(2)}) collective-permute-start(bf16[1024,256]{1,0:T(8,128)(2,1)} %get-tuple-element.26.own.p0), channel_id=1, source_target_pairs={{0,2},{1,3},{2,0},{3,1},{4,6},{5,7},{6,4},{7,5},{8,10},{9,11},{10,... | collective-permute-start | bytes 1572872 | tf_op jit(solution)/shard_map/ppermute | solution.py:418
  95.3 24.7 %collective-permute-start.3 = (bf16[1024,256]{1,0:T(8,128)(2,1)}, bf16[1024,256]{1,0:T(8,128)(2,1)S(1)}, u32[]{:S(2)}, u32[]{:S(2)}) collective-permute-start(bf16[1024,256]{1,0:T(8,128)(2,1)} %get-tuple-element.26.own.p0), channel_id=1, source_target_pairs={{0,1},{1,2},{2,3},{3,0},{4,5},{5,6},{6,7},{7,4},{8,9},{9,10},{10,1... | collective-permute-start | bytes 1572872 | tf_op jit(solution)/shard_map/ppermute | solution.py:418
  97.3 23.4 %collective-permute-start.4 = (bf16[1024,256]{1,0:T(8,128)(2,1)}, bf16[1024,256]{1,0:T(8,128)(2,1)S(1)}, u32[]{:S(2)}, u32[]{:S(2)}) collective-permute-start(bf16[1024,256]{1,0:T(8,128)(2,1)} %get-tuple-element.26.own.p0), channel_id=1, source_target_pairs={{0,3},{1,0},{2,1},{3,2},{4,7},{5,4},{6,5},{7,6},{8,11},{9,8},{10,9... | collective-permute-start | bytes 1572872 | tf_op jit(solution)/shard_map/ppermute | solution.py:418
  108.6 1.0 copy-start.1
  109.6 13.6 %copy-start.3 = (bf16[1024,256]{1,0:T(8,128)(2,1)}, bf16[1024,256]{1,0:T(8,128)(2,1)S(1)}, u32[]{:S(2)}) copy-start(bf16[1024,256]{1,0:T(8,128)(2,1)S(1)} %collective-permute-done.5.far.p3) | copy-start | bytes 1572868
  111.4 21.0 %copy-start.8 = (s32[1,1,128,8]{2,3,1,0:T(8,128)S(1)}, s32[1,1,128,8]{2,3,1,0:T(8,128)}, u32[]{:S(2)}) copy-start(s32[1,1,128,8]{2,3,1,0:T(8,128)} %param.14) | copy-start | bytes 12292
  111.4 21.2 %copy-start.2 = (bf16[1024,256]{1,0:T(8,128)(2,1)S(1)}, bf16[1024,256]{1,0:T(8,128)(2,1)}, u32[]{:S(2)}) copy-start(bf16[1024,256]{1,0:T(8,128)(2,1)} %get-tuple-element.26.own.p0) | copy-start | bytes 1572868
  123.3 42.7 %all-to-all-start.1 = ((bf16[128,8,256]{2,1,0:T(8,128)(2,1)}), bf16[128,8,256]{2,1,0:T(8,128)(2,1)S(1)}, u32[]{:S(2)}, u32[]{:S(2)}) async-start(bf16[128,8,256]{2,1,0:T(8,128)(2,1)} %bitcast.8), calls=%async_computation.1 | async-start | bytes 1048576 | tf_op jit(solution)/shard_map/all_to_all | solution.py:494
  132.6 1.0 copy-start.4
  133.7 1.0 copy-start.6
